TPU v7x, 32 devices: a whole 2x2x4 slice. The times are simulated.
32 devices in a mesh: groups: 2 (over y), ctx: 16 (over z, x, core), head: 1.
Axes of the slice: x: 2, y: 2, z: 4, core: 2. Of those that a mesh axis runs over, the one named last changes fastest.
Arguments:
- queries: bfloat16 [4096, 4096], P(('groups', 'ctx'), 'head'), parts along dimension 0, may hold values from -8 to 8
- keys: bfloat16 [4096, 1024], P(('groups', 'ctx'), 'head'), parts along dimension 0, may hold values from -8 to 8
- values: bfloat16 [4096, 1024], P(('groups', 'ctx'), 'head'), parts along dimension 0, may hold values from -6 to 6
- grad_out: bfloat16 [4096, 4096], P(('groups', 'ctx'), 'head'), parts along dimension 0, may hold values from -6 to 6
Outputs:
- grad_queries: bfloat16 [4096, 4096], P(('groups', 'ctx'), 'head'), parts along dimension 0
- grad_keys: bfloat16 [4096, 1024], P(('groups', 'ctx'), 'head'), parts along dimension 0
- grad_values: bfloat16 [4096, 1024], P(('groups', 'ctx'), 'head'), parts along dimension 0
- log_norm: float32 [4096, 32], P(('groups', 'ctx'), 'head'), parts along dimension 0
There are 2 independent parts, one for each index of `groups`. A program takes and returns all parts, laid end to end along the dimension named above; each array names one. Nothing has to cross between parts.
All inputs are finite; a program needn't handle non-finite values.
Results may differ from a plain program's by a relative error of at most 0.0099.
Values may be sent and summed in bfloat16 or wider, within the bound.
No kernel may reach another device: no remote copies, remote signals or barrier semaphores. Data moves between devices by JAX's collectives and lax.ppermute only.
A program may use at most 64 MiB of HBM per device.

v0:
```python
import math

import jax
import jax.numpy as jnp
from jax import lax
from jax.sharding import PartitionSpec as P

HEAD_SIZE = 128
W = 512
STRIDE = 128


NEG_FILL = -1e30


def shifted(shard, axis, by):
    peers = lax.axis_size(axis)
    pairs = [(i, i + by) for i in range(peers) if 0 <= i + by < peers]
    return lax.ppermute(shard, axis, pairs)


def head_terms(query_one, grad_one, key_one, value_one, allowed):
    token_rows = query_one.shape[0]
    heads_per_group = query_one.shape[1] // HEAD_SIZE
    scale_factor = 1.0 / math.sqrt(HEAD_SIZE)
    query_heads = query_one.reshape(token_rows, heads_per_group, HEAD_SIZE)
    grad_heads = grad_one.reshape(token_rows, heads_per_group, HEAD_SIZE)
    scores = (
        jnp.einsum("qrd,kd->rqk", query_heads, key_one, preferred_element_type=jnp.float32)
        * scale_factor
    )
    scores = jnp.where(allowed[None], scores, NEG_FILL)
    top_score = jnp.max(scores, axis=-1)
    log_norm = top_score + jnp.log(jnp.sum(jnp.exp(scores - top_score[..., None]), axis=-1))
    probs = jnp.exp(scores - log_norm[..., None])
    probability_lowp = probs.astype(jnp.bfloat16)
    attended = jnp.einsum(
        "rqk,kd->qrd", probability_lowp, value_one, preferred_element_type=jnp.float32
    )
    delta_rows = jnp.sum(grad_heads.astype(jnp.float32) * attended, axis=-1)
    dprobs = jnp.einsum("qrd,kd->rqk", grad_heads, value_one, preferred_element_type=jnp.float32)
    score_gradient = (
        probs * (dprobs - jnp.transpose(delta_rows)[:, :, None]) * scale_factor
    ).astype(jnp.bfloat16)
    grad_query = jnp.einsum(
        "rqk,kd->qrd", score_gradient, key_one, preferred_element_type=jnp.float32
    )
    grad_query = grad_query.astype(jnp.bfloat16).reshape(token_rows, heads_per_group * HEAD_SIZE)
    key_gradient = jnp.einsum(
        "rqk,qrd->kd", score_gradient, query_heads, preferred_element_type=jnp.float32
    )
    value_gradient = jnp.einsum(
        "rqk,qrd->kd", probability_lowp, grad_heads, preferred_element_type=jnp.float32
    )
    return (grad_query, jnp.transpose(log_norm), key_gradient, value_gradient)


def local(queries, keys, values, grad_out):
    token_rows = queries.shape[0]
    key_value_width = keys.shape[1]
    kv_heads = key_value_width // HEAD_SIZE
    heads_per_group = queries.shape[1] // key_value_width
    hops = (W + token_rows - 1) // token_rows
    win_len = (hops + 1) * token_rows
    first = lax.axis_index("ctx") * token_rows
    key_value = jnp.concatenate([keys, values], axis=1)
    earlier = [shifted(key_value, "ctx", distance) for distance in range(hops, 0, -1)]
    window = jnp.concatenate(earlier + [key_value], axis=0)
    local_strided = key_value.reshape(token_rows // STRIDE, STRIDE, 2 * key_value_width)[:, 0]
    strided = lax.all_gather(local_strided, "ctx", axis=0, tiled=True)
    strided_count = strided.shape[0]
    every_key = jnp.concatenate([window, strided], axis=0)
    key_count = every_key.shape[0]
    later = (first + jnp.arange(token_rows, dtype=jnp.int32))[:, None]
    key_pos = (first - hops * token_rows + jnp.arange(win_len, dtype=jnp.int32))[None, :]
    strided_pos = (jnp.arange(strided_count, dtype=jnp.int32) * STRIDE)[None, :]
    in_window = (
        (key_pos >= 0) & (key_pos <= later) & (later - key_pos < W) & (key_pos % STRIDE != 0)
    )
    in_stride = strided_pos <= later
    allowed = jnp.concatenate([in_window, in_stride], axis=1)
    query_split = jnp.transpose(
        queries.reshape(token_rows, kv_heads, heads_per_group * HEAD_SIZE), (1, 0, 2)
    )
    grad_split = jnp.transpose(
        grad_out.reshape(token_rows, kv_heads, heads_per_group * HEAD_SIZE), (1, 0, 2)
    )
    key_split = jnp.transpose(
        every_key[:, :key_value_width].reshape(key_count, kv_heads, HEAD_SIZE), (1, 0, 2)
    )
    value_split = jnp.transpose(
        every_key[:, key_value_width:].reshape(key_count, kv_heads, HEAD_SIZE), (1, 0, 2)
    )

    def per_head(operands):
        return head_terms(operands[0], operands[1], operands[2], operands[3], allowed)

    grad_query, log_norm, key_gradient, value_gradient = lax.map(
        per_head, (query_split, grad_split, key_split, value_split)
    )
    grad_queries = jnp.transpose(grad_query, (1, 0, 2)).reshape(
        token_rows, kv_heads * heads_per_group * HEAD_SIZE
    )
    log_norms = jnp.transpose(log_norm, (1, 0, 2)).reshape(token_rows, kv_heads * heads_per_group)
    key_terms = jnp.transpose(key_gradient, (1, 0, 2)).reshape(key_count, key_value_width)
    value_terms = jnp.transpose(value_gradient, (1, 0, 2)).reshape(key_count, key_value_width)
    terms = jnp.concatenate([key_terms, value_terms], axis=1)

    def window_part(distance):
        return terms[(hops - distance) * token_rows : (hops - distance + 1) * token_rows]

    total = window_part(0)
    for distance in range(1, hops + 1):
        total = total + shifted(
            window_part(distance).astype(jnp.bfloat16), "ctx", -distance
        ).astype(jnp.float32)
    strided_terms = terms[win_len:]
    own_count = token_rows // STRIDE
    own_strided = lax.psum_scatter(strided_terms, "ctx", scatter_dimension=0, tiled=True)
    shaped = total.reshape(own_count, STRIDE, 2 * key_value_width)
    total = jnp.concatenate([shaped[:, :1] + own_strided[:, None], shaped[:, 1:]], axis=1)
    total = total.reshape(token_rows, 2 * key_value_width)
    grad_keys = total[:, :key_value_width].astype(jnp.bfloat16)
    grad_values = total[:, key_value_width:].astype(jnp.bfloat16)
    return (grad_queries, grad_keys, grad_values, log_norms)


def solution(mesh):
    placed = (
        P(("groups", "ctx"), "head"),
        P(("groups", "ctx"), "head"),
        P(("groups", "ctx"), "head"),
        P(("groups", "ctx"), "head"),
    )
    return jax.shard_map(
        local,
        mesh=mesh,
        in_specs=placed,
        out_specs=(
            P(("groups", "ctx"), "head"),
            P(("groups", "ctx"), "head"),
            P(("groups", "ctx"), "head"),
            P(("groups", "ctx"), "head"),
        ),
        check_vma=False,
    )
```

profile of v0, /device:TPU:0, one launch (start us, length us, event | category | flops | bytes accessed | tf_op | source)
XLA Modules:
  0.0 234.0 jit_solution(9395199586200635128)
XLA Ops:
  7.2 1.8 constant_dynamic-update-slice_fusion.3
  9.0 1.7 constant_dynamic-update-slice_fusion.2
  10.7 4.9 %collective-permute-start = (bf16[128,2048]{1,0:T(8,128)(2,1)}, bf16[128,2048]{1,0:T(8,128)(2,1)S(1)}, u32[]{:S(2)}, u32[]{:S(2)}) collective-permute-start(bf16[128,2048]{1,0:T(8,128)(2,1)} %constant_dynamic-update-slice_fusion.2), channel_id=1, source_target_pairs={{0,4},{1,5},{2,6},{3,7},{4,8},{5,9},{6,10},{7,11},{8,12},{9,13},{1... | collective-permute-start | bytes 1572872 | tf_op jit(solution)/shard_map/ppermute | solution.py:19
  15.7 2.6 %collective-permute-start.1 = (bf16[128,2048]{1,0:T(8,128)(2,1)}, bf16[128,2048]{1,0:T(8,128)(2,1)S(1)}, u32[]{:S(2)}, u32[]{:S(2)}) collective-permute-start(bf16[128,2048]{1,0:T(8,128)(2,1)} %constant_dynamic-update-slice_fusion.2), channel_id=1, source_target_pairs={{0,3},{1,4},{2,5},{3,6},{4,7},{5,8},{6,9},{7,10},{8,11},{9,12},{10... | collective-permute-start | bytes 1572872 | tf_op jit(solution)/shard_map/ppermute | solution.py:19
  18.3 3.5 %collective-permute-start.2 = (bf16[128,2048]{1,0:T(8,128)(2,1)}, bf16[128,2048]{1,0:T(8,128)(2,1)S(1)}, u32[]{:S(2)}, u32[]{:S(2)}) collective-permute-start(bf16[128,2048]{1,0:T(8,128)(2,1)} %constant_dynamic-update-slice_fusion.2), channel_id=1, source_target_pairs={{0,2},{1,3},{2,4},{3,5},{4,6},{5,7},{6,8},{7,9},{8,10},{9,11},{10,... | collective-permute-start | bytes 1572872 | tf_op jit(solution)/shard_map/ppermute | solution.py:19
  21.7 2.6 %collective-permute-start.3 = (bf16[128,2048]{1,0:T(8,128)(2,1)}, bf16[128,2048]{1,0:T(8,128)(2,1)S(1)}, u32[]{:S(2)}, u32[]{:S(2)}) collective-permute-start(bf16[128,2048]{1,0:T(8,128)(2,1)} %constant_dynamic-update-slice_fusion.2), channel_id=1, source_target_pairs={{0,1},{1,2},{2,3},{3,4},{4,5},{5,6},{6,7},{7,8},{8,9},{9,10},{10,1... | collective-permute-start | bytes 1572872 | tf_op jit(solution)/shard_map/ppermute | solution.py:19
  25.6 2.3 copy.38
  27.9 1.3 copy.39
  29.2 37.9 %all-gather = bf16[16,1,2048]{2,1,0:T(2,128)(2,1)S(1)} all-gather(bf16[1,1,2048]{2,1,0:T(2,128)(2,1)S(1)} %slice.58), channel_id=2, replica_groups=mesh['groups'=2,'ctx'=16,'head'=1] {'ctx'}, dimensions={0}, use_global_device_ids=true | all-gather | bytes 69632 | tf_op jit(solution)/shard_map/all_gather | solution.py:70
  69.2 48.5 %while.16 = (s32[]{:T(128)}, bf16[8,128,512]{1,2,0:T(8,128)(2,1)}, f32[8,128,4]{1,2,0:T(4,128)}, f32[8,656,128]{2,1,0:T(8,128)}, f32[8,656,128]{2,1,0:T(8,128)},...) while((s32[]{:T(128)}, bf16[8,128,512]{1,2,0:T(8,128)(2,1)}, ...), condition=%wide.region_4.5_spmd, body=%wide.region_0.4_spmd.sunk | while | flops 520862720 | bytes 11759745 | solution.py:98
  117.8 2.3 bitcast_dynamic-update-slice_fusion.1
  121.1 1.9 copy-done
  124.2 1.3 collective-permute-start.4
  125.5 1.3 collective-permute-start.5
  126.8 1.3 collective-permute-start.6
  128.1 1.3 collective-permute-start.7
  130.0 1.6 slice.67
  131.6 1.3 copy.49
  132.9 18.1 %collective-permute-done.5 = bf16[128,2048]{1,0:T(8,128)(2,1)S(1)} collective-permute-done((bf16[128,2048]{1,0:T(8,128)(2,1)}, bf16[128,2048]{1,0:T(8,128)(2,1)S(1)}, u32[]{:S(2)}, u32[]{:S(2)}) %collective-permute-start.5) | collective-permute-done | bytes 524320 | tf_op jit(solution)/shard_map/ppermute | solution.py:19
  151.1 1.7 collective-permute-done.6
  152.8 17.2 %collective-permute-done.7 = bf16[128,2048]{1,0:T(8,128)(2,1)} collective-permute-done((bf16[128,2048]{1,0:T(8,128)(2,1)S(1)}, bf16[128,2048]{1,0:T(8,128)(2,1)}, u32[]{:S(2)}, u32[]{:S(2)}) %collective-permute-start.7) | collective-permute-done | bytes 524320 | tf_op jit(solution)/shard_map/ppermute | solution.py:19
  169.9 1.9 fusion.28
  171.9 52.8 %all-reduce.3.cloned.1.call-done = f32[16,2048]{1,0:T(8,128)} async-done(((f32[16,2048]{1,0:T(8,128)}), f32[16,2048]{1,0:T(8,128)}) %all-reduce.3.cloned.1.call-update) | async-done | bytes 131088
  224.7 1.5 slice_add_fusion.1
  (131 shorter events, 55.4 us)
Async XLA Ops:
  7.2 20.7 %copy-start.2 = (bf16[128,4096]{1,0:T(8,128)(2,1)S(1)}, bf16[128,4096]{1,0:T(8,128)(2,1)}, u32[]{:S(2)}) copy-start(bf16[128,4096]{1,0:T(8,128)(2,1)} %param.9) | copy-start | bytes 3145732
  7.2 217.5 %all-reduce.3.cloned.1.call-start = ((), (), s32[]{:S(2)}) async-start(), calls=%async_computation | async-start | bytes 262144
  10.7 56.4 %collective-permute-start = (bf16[128,2048]{1,0:T(8,128)(2,1)}, bf16[128,2048]{1,0:T(8,128)(2,1)S(1)}, u32[]{:S(2)}, u32[]{:S(2)}) collective-permute-start(bf16[128,2048]{1,0:T(8,128)(2,1)} %constant_dynamic-update-slice_fusion.2), channel_id=1, source_target_pairs={{0,4},{1,5},{2,6},{3,7},{4,8},{5,9},{6,10},{7,11},{8,12},{9,13},{1... | collective-permute-start | bytes 1572872 | tf_op jit(solution)/shard_map/ppermute | solution.py:19
  15.7 51.5 %collective-permute-start.1 = (bf16[128,2048]{1,0:T(8,128)(2,1)}, bf16[128,2048]{1,0:T(8,128)(2,1)S(1)}, u32[]{:S(2)}, u32[]{:S(2)}) collective-permute-start(bf16[128,2048]{1,0:T(8,128)(2,1)} %constant_dynamic-update-slice_fusion.2), channel_id=1, source_target_pairs={{0,3},{1,4},{2,5},{3,6},{4,7},{5,8},{6,9},{7,10},{8,11},{9,12},{10... | collective-permute-start | bytes 1572872 | tf_op jit(solution)/shard_map/ppermute | solution.py:19
  18.3 48.9 %collective-permute-start.2 = (bf16[128,2048]{1,0:T(8,128)(2,1)}, bf16[128,2048]{1,0:T(8,128)(2,1)S(1)}, u32[]{:S(2)}, u32[]{:S(2)}) collective-permute-start(bf16[128,2048]{1,0:T(8,128)(2,1)} %constant_dynamic-update-slice_fusion.2), channel_id=1, source_target_pairs={{0,2},{1,3},{2,4},{3,5},{4,6},{5,7},{6,8},{7,9},{8,10},{9,11},{10,... | collective-permute-start | bytes 1572872 | tf_op jit(solution)/shard_map/ppermute | solution.py:19
  21.7 45.5 %collective-permute-start.3 = (bf16[128,2048]{1,0:T(8,128)(2,1)}, bf16[128,2048]{1,0:T(8,128)(2,1)S(1)}, u32[]{:S(2)}, u32[]{:S(2)}) collective-permute-start(bf16[128,2048]{1,0:T(8,128)(2,1)} %constant_dynamic-update-slice_fusion.2), channel_id=1, source_target_pairs={{0,1},{1,2},{2,3},{3,4},{4,5},{5,6},{6,7},{7,8},{8,9},{9,10},{10,1... | collective-permute-start | bytes 1572872 | tf_op jit(solution)/shard_map/ppermute | solution.py:19
  29.2 38.1 %copy-start.4 = (bf16[128,1024]{1,0:T(8,128)(2,1)S(1)}, bf16[128,1024]{1,0:T(8,128)(2,1)}, u32[]{:S(2)}) copy-start(bf16[128,1024]{1,0:T(8,128)(2,1)} %param.7) | copy-start | bytes 786436
  29.2 38.1 %copy-start.5 = (bf16[128,1024]{1,0:T(8,128)(2,1)S(1)}, bf16[128,1024]{1,0:T(8,128)(2,1)}, u32[]{:S(2)}) copy-start(bf16[128,1024]{1,0:T(8,128)(2,1)} %param.8) | copy-start | bytes 786436
  117.8 2.6 %copy-start.1 = (f32[8,656,128]{2,1,0:T(8,128)S(1)}, f32[8,656,128]{2,1,0:T(8,128)}, u32[]{:S(2)}) copy-start(f32[8,656,128]{2,1,0:T(8,128)} %get-tuple-element.61) | copy-start | bytes 8060932
  120.7 2.4 %copy-start = (f32[656,2048]{1,0:T(8,128)}, f32[656,2048]{1,0:T(8,128)S(1)}, u32[]{:S(2)}) copy-start(f32[656,2048]{1,0:T(8,128)S(1)} %bitcast_dynamic-update-slice_fusion) | copy-start | bytes 16121860
  123.1 6.4 %copy-start.6 = (u32[32]{0:T(128)S(1)}, u32[32]{0:T(128)}, u32[]{:S(2)}) copy-start(u32[32]{0:T(128)} %constant.60) | copy-start | bytes 388
  123.1 8.6 %copy-start.3 = (bf16[8,128,512]{1,2,0:T(8,128)(2,1)S(1)}, bf16[8,128,512]{1,2,0:T(8,128)(2,1)}, u32[]{:S(2)}) copy-start(bf16[8,128,512]{1,2,0:T(8,128)(2,1)} %get-tuple-element.59) | copy-start | bytes 3145732
  124.2 8.7 %collective-permute-start.4 = (bf16[128,2048]{1,0:T(8,128)(2,1)}, bf16[128,2048]{1,0:T(8,128)(2,1)S(1)}, u32[]{:S(2)}, u32[]{:S(2)}) collective-permute-start(bf16[128,2048]{1,0:T(8,128)(2,1)} %get-tuple-element.119), channel_id=1, source_target_pairs={{1,0},{2,1},{3,2},{4,3},{5,4},{6,5},{7,6},{8,7},{9,8},{10,9},{11,1... | collective-permute-start | bytes 1572872 | tf_op jit(solution)/shard_map/ppermute | solution.py:19
  125.5 25.6 %collective-permute-start.5 = (bf16[128,2048]{1,0:T(8,128)(2,1)}, bf16[128,2048]{1,0:T(8,128)(2,1)S(1)}, u32[]{:S(2)}, u32[]{:S(2)}) collective-permute-start(bf16[128,2048]{1,0:T(8,128)(2,1)} %get-tuple-element.122), channel_id=1, source_target_pairs={{2,0},{3,1},{4,2},{5,3},{6,4},{7,5},{8,6},{9,7},{10,8},{11,9},{12,... | collective-permute-start | bytes 1572872 | tf_op jit(solution)/shard_map/ppermute | solution.py:19
  126.8 25.9 %collective-permute-start.6 = (bf16[128,2048]{1,0:T(8,128)(2,1)S(1)}, bf16[128,2048]{1,0:T(8,128)(2,1)}, u32[]{:S(2)}, u32[]{:S(2)}) collective-permute-start(bf16[128,2048]{1,0:T(8,128)(2,1)S(1)} %get-tuple-element.121), channel_id=1, source_target_pairs={{3,0},{4,1},{5,2},{6,3},{7,4},{8,5},{9,6},{10,7},{11,8},{12,9},{13... | collective-permute-start | bytes 1572872 | tf_op jit(solution)/shard_map/ppermute | solution.py:19
  128.1 41.8 %collective-permute-start.7 = (bf16[128,2048]{1,0:T(8,128)(2,1)S(1)}, bf16[128,2048]{1,0:T(8,128)(2,1)}, u32[]{:S(2)}, u32[]{:S(2)}) collective-permute-start(bf16[128,2048]{1,0:T(8,128)(2,1)S(1)} %get-tuple-element.120), channel_id=1, source_target_pairs={{4,0},{5,1},{6,2},{7,3},{8,4},{9,5},{10,6},{11,7},{12,8},{13,9},{1... | collective-permute-start | bytes 1572872 | tf_op jit(solution)/shard_map/ppermute | solution.py:19
Sparse Core Ops, SparseCore 0:
  131.7 92.9 all-reduce.2
where the time goes:
time: 236 us; the launch traced here: 234 us
  waiting for transfers between devices  89.8 us (38%)
  blocking collectives  37.9 us (16%)
  local copies, waits for them, and re-layouts  33.5 us (14%)
  matrix products  28.7 us (12%)
  starting transfers between devices  18.8 us (8%)
  between operations  14.4 us (6%)
  other arithmetic  10.7 us (5%)
    unnamed x2, waiting for transfers between devices  52.8 us
    all_gather x1, blocking collectives, local(): strided = lax.all_gather(local_strided, 'ctx', axis=0, tiled=True)  37.9 us
    ppermute x8, waiting for transfers between devices, shifted(): return lax.ppermute(shard, axis, pairs)  37 us
    ppermute x8, starting transfers between devices, shifted(): return lax.ppermute(shard, axis, pairs)  18.8 us
    unnamed x28, local copies, waits for them, and re-layouts  12.1 us
    dot_general x8, matrix products, head_terms(): jnp.einsum('rqk,qrd->kd', probability_lowp, grad_heads, preferred_element...  8.61 us
    dot_general x8, matrix products, head_terms(): jnp.einsum('rqk,qrd->kd', score_gradient, query_heads, preferred_element_...  8.61 us
    dynamic_slice x8, local copies, waits for them, and re-layouts, local(): lax.map(per_head, (query_split, grad_split, key_split, value_split))  7.89 us
  transfers between devices with their start and end apart: 9, of which 4 were waited for; matrix products, arithmetic and copies ran while one was open for 4% of the time, Pallas kernels for 0%

commit v1 on v0

v1 whole, which is shorter than its diff:
```python
import functools
import math

import jax
import jax.numpy as jnp
from jax import lax
from jax.experimental import pallas as pl
from jax.experimental.pallas import tpu as pltpu
from jax.sharding import PartitionSpec as P

HEAD_SIZE = 128
W = 512
STRIDE = 128
CHUNKS = 2

NEG_FILL = -1e30
SCALE = 1.0 / math.sqrt(HEAD_SIZE)


def dot_nt(left, right):
    return lax.dot_general(
        left, right, (((1,), (1,)), ((), ())), preferred_element_type=jnp.float32
    )


def dot_nn(left, right):
    return lax.dot_general(
        left, right, (((1,), (0,)), ((), ())), preferred_element_type=jnp.float32
    )


def dot_tn(left, right):
    return lax.dot_general(
        left, right, (((0,), (0,)), ((), ())), preferred_element_type=jnp.float32
    )


def attention_kernel(
    place,
    q_own,
    q_other,
    o_own,
    o_other,
    kv_here,
    kv_near,
    kv_past,
    kv_far,
    dq_own,
    dq_other,
    norm,
    g_here,
    g_near,
    g_past,
    g_far,
):
    half = q_own.shape[0]
    rows = 2 * half
    far_rows = kv_far.shape[0]
    heads = q_own.shape[1] // HEAD_SIZE
    core, pair = place[0], place[1]

    def token(shape, axis):
        at = lax.broadcasted_iota(jnp.int32, shape, axis)
        return at + jnp.where(at < half, core * half, -core * half)

    lower = token((rows, rows), 0) <= token((rows, rows), 1)
    far_at = lax.broadcasted_iota(jnp.int32, (far_rows, rows), 0)
    far_token = (far_at // 2) * rows + jnp.where(far_at % 2 == 0, core, 1 - core) * half
    far_open = far_token <= pair * rows + token((far_rows, rows), 1) - W
    near_bias = jnp.where(pair >= 1, 0.0, NEG_FILL)
    past_bias = jnp.where(pair >= 2, 0.0, NEG_FILL)

    def stacked(side):
        columns = slice(side * HEAD_SIZE, (side + 1) * HEAD_SIZE)
        return jnp.concatenate(
            [kv_here[:, columns], kv_near[:, columns], kv_past[:, columns], kv_far[:, columns]],
            axis=0,
        )

    key_all, value_all = stacked(0), stacked(1)
    key_terms = value_terms = None

    for head in range(heads):
        columns = slice(head * HEAD_SIZE, (head + 1) * HEAD_SIZE)
        query = jnp.concatenate([q_own[:, columns], q_other[:, columns]], axis=0)
        grad = jnp.concatenate([o_own[:, columns], o_other[:, columns]], axis=0)
        score = dot_nt(key_all, query)
        edge = jnp.where(lower, score[:rows], score[2 * rows : 3 * rows] + past_bias)
        near = score[rows : 2 * rows] + near_bias
        far = jnp.where(far_open, score[3 * rows :], NEG_FILL)
        top = jnp.maximum(
            jnp.maximum(
                jnp.max(edge, axis=0, keepdims=True), jnp.max(near, axis=0, keepdims=True)
            ),
            jnp.max(far, axis=0, keepdims=True),
        )
        edge, near, far = (
            jnp.exp2((part - top) * (SCALE * math.log2(math.e))) for part in (edge, near, far)
        )
        total = (
            jnp.sum(edge, axis=0, keepdims=True)
            + jnp.sum(near, axis=0, keepdims=True)
            + jnp.sum(far, axis=0, keepdims=True)
        )
        norm[head : head + 1, :] = top * SCALE + jnp.log(total)
        inverse = 1.0 / total
        edge, near, far = (part * inverse for part in (edge, near, far))
        dprob = dot_nt(value_all, grad)
        d_edge = jnp.where(lower, dprob[:rows], dprob[2 * rows : 3 * rows])
        d_near = dprob[rows : 2 * rows]
        d_far = dprob[3 * rows :]
        delta = (
            jnp.sum(edge * d_edge, axis=0, keepdims=True)
            + jnp.sum(near * d_near, axis=0, keepdims=True)
            + jnp.sum(far * d_far, axis=0, keepdims=True)
        )
        d_edge, d_near, d_far = (
            part * (d_part - delta)
            for part, d_part in ((edge, d_edge), (near, d_near), (far, d_far))
        )

        def split(on_edge, on_near, on_far):
            return jnp.concatenate(
                [
                    jnp.where(lower, on_edge, 0.0).astype(jnp.bfloat16),
                    on_near.astype(jnp.bfloat16),
                    jnp.where(lower, 0.0, on_edge).astype(jnp.bfloat16),
                    on_far.astype(jnp.bfloat16),
                ],
                axis=0,
            )

        prob = split(edge, near, far)
        dscore = split(d_edge, d_near, d_far)
        value_term = dot_nn(prob, grad)
        key_term = dot_nn(dscore, query)
        value_terms = value_term if head == 0 else value_terms + value_term
        key_terms = key_term if head == 0 else key_terms + key_term
        query_term = (dot_tn(dscore, key_all) * SCALE).astype(jnp.bfloat16)
        dq_own[:, columns] = query_term[:half]
        dq_other[:, columns] = query_term[half:]

    terms = jnp.concatenate([key_terms * SCALE, value_terms], axis=1)
    g_here[...] = terms[:rows]
    g_near[...] = terms[rows : 2 * rows].astype(jnp.bfloat16)
    g_past[...] = terms[2 * rows : 3 * rows].astype(jnp.bfloat16)
    g_far[...] = terms[3 * rows :]


def attention(place, queries, q_other, grad_out, o_other, kv_here, kv_near, kv_past, kv_far, chunk):
    half = queries.shape[0]
    rows = 2 * half
    far_rows = kv_far.shape[0]
    both = 2 * HEAD_SIZE
    count = kv_here.shape[1] // both
    group_width = q_other.shape[1] // (count * CHUNKS)
    heads = group_width // HEAD_SIZE
    first = chunk * count
    per_core = count * CHUNKS

    own = pl.BlockSpec((half, group_width), lambda h, place: (0, place[0] * per_core + first + h))
    other = pl.BlockSpec((half, group_width), lambda h, place: (0, first + h))
    block = pl.BlockSpec((rows, both), lambda h, place: (0, h))
    out = pl.BlockSpec((half, group_width), lambda h, place: (0, h))
    far_in = pl.BlockSpec((far_rows, both), lambda h, place: (0, first + h))
    far_out = pl.BlockSpec((far_rows, both), lambda h, place: (0, h))
    keys_seen = 3 * rows + far_rows
    return pl.pallas_call(
        attention_kernel,
        name=f"attention_{chunk}",
        grid_spec=pltpu.PrefetchScalarGridSpec(
            num_scalar_prefetch=1,
            grid=(count,),
            in_specs=[own, other, own, other, block, block, block, far_in],
            out_specs=[
                out,
                out,
                pl.BlockSpec((None, heads, rows), lambda h, place: (h, 0, 0)),
                block,
                block,
                block,
                far_out,
            ],
        ),
        out_shape=[
            jax.ShapeDtypeStruct((half, count * group_width), jnp.bfloat16),
            jax.ShapeDtypeStruct((half, count * group_width), jnp.bfloat16),
            jax.ShapeDtypeStruct((count, heads, rows), jnp.float32),
            jax.ShapeDtypeStruct((rows, count * both), jnp.float32),
            jax.ShapeDtypeStruct((rows, count * both), jnp.bfloat16),
            jax.ShapeDtypeStruct((rows, count * both), jnp.bfloat16),
            jax.ShapeDtypeStruct((far_rows, count * both), jnp.float32),
        ],
        compiler_params=pltpu.CompilerParams(vmem_limit_bytes=40 * 1024 * 1024),
        cost_estimate=pl.CostEstimate(
            flops=count * heads * rows * keys_seen * HEAD_SIZE * 10,
            transcendentals=count * heads * rows * keys_seen,
            bytes_accessed=count * (6 * half * group_width * 2 + 5 * rows * both * 4),
        ),
    )(place, queries, q_other, grad_out, o_other, kv_here, kv_near, kv_past, kv_far)


def local(queries, keys, values, grad_out):
    half, kv_width = keys.shape
    kv_heads = kv_width // HEAD_SIZE
    both = 2 * HEAD_SIZE
    group_width = queries.shape[1] // kv_heads
    rows = 2 * half
    peers = lax.axis_size("ctx")
    pairs = peers // 2
    assert half == STRIDE and W == 2 * rows and peers % 2 == 0 and kv_heads % (2 * CHUNKS) == 0
    per_core = kv_heads // 2
    count = per_core // CHUNKS
    index = lax.axis_index("ctx")
    core, pair = index % 2, index // 2
    place = jnp.stack([core, pair]).astype(jnp.int32)

    def swap(x):
        return lax.ppermute(x, "ctx", [(i, i ^ 1) for i in range(peers)])

    def shifted(x, by):
        return lax.ppermute(x, "ctx", [(i, i + by) for i in range(peers) if 0 <= i + by < peers])

    def exchanged(x):
        groups = [list(range(parity, peers, 2)) for parity in range(2)]
        return lax.all_to_all(x, "ctx", 0, 0, axis_index_groups=groups, tiled=True)

    def part(x, which, width):
        return lax.dynamic_slice_in_dim(x, which * width, width, 1)

    def joined(mine, theirs):
        return jnp.where(
            core == 0,
            jnp.concatenate([mine, theirs], axis=1),
            jnp.concatenate([theirs, mine], axis=1),
        )

    key_value = jnp.stack(
        [keys.reshape(half, kv_heads, HEAD_SIZE), values.reshape(half, kv_heads, HEAD_SIZE)], axis=2
    ).reshape(half, kv_heads * both)
    kv_mine = part(key_value, core, per_core * both)
    kv_other = swap(part(key_value, 1 - core, per_core * both))

    here, near, past = [], [], []
    for chunk in range(CHUNKS):
        columns = slice(chunk * count * both, (chunk + 1) * count * both)
        here.append(jnp.concatenate([kv_mine[:, columns], kv_other[:, columns]], axis=0))
        near.append(shifted(here[chunk], 2))
        past.append(shifted(here[chunk], 4))
    strided = jnp.concatenate([kv_mine[:1], kv_other[:1]], axis=1)
    far = exchanged(jnp.broadcast_to(strided, (pairs, 2 * per_core * both)))
    far = far.reshape(2 * pairs, per_core * both)
    q_other = swap(part(queries, 1 - core, per_core * group_width))
    o_other = swap(part(grad_out, 1 - core, per_core * group_width))

    dq_own, dq_other, norms, sums, far_terms = [], [], [], [], []
    for chunk in range(CHUNKS):
        out = attention(
            place,
            queries,
            q_other,
            grad_out,
            o_other,
            here[chunk],
            near[chunk],
            past[chunk],
            far,
            chunk,
        )
        dq_own.append(out[0])
        dq_other.append(swap(out[1]))
        norms.append(out[2])
        near_terms, past_terms = shifted(out[4], -2), shifted(out[5], -4)
        sums.append((out[3], near_terms, past_terms))
        far_terms.append(out[6])

    far_terms = jnp.concatenate(far_terms, axis=1).reshape(pairs, 2 * per_core * both)
    strided_sum = jnp.sum(exchanged(far_terms), axis=0).reshape(2, per_core * both)
    row = lax.broadcasted_iota(jnp.int32, (rows, 1), 0)
    total = jnp.concatenate(
        [a + b.astype(jnp.float32) + c.astype(jnp.float32) for a, b, c in sums], axis=1
    )
    total = (
        total
        + jnp.where(row == 0, strided_sum[:1], 0.0)
        + jnp.where(row == half, strided_sum[1:], 0.0)
    ).astype(jnp.bfloat16)
    grads = joined(total[:half], swap(total[half:])).reshape(half, kv_heads, 2, HEAD_SIZE)
    grad_keys = grads[:, :, 0].reshape(half, kv_width)
    grad_values = grads[:, :, 1].reshape(half, kv_width)
    grad_queries = joined(jnp.concatenate(dq_own, axis=1), jnp.concatenate(dq_other, axis=1))
    norm = jnp.concatenate(norms, axis=0).reshape(-1, rows)
    log_norm = joined(norm[:, :half].T, swap(norm[:, half:]).T)
    return (grad_queries, grad_keys, grad_values, log_norm)


def solution(mesh):
    placed = P(("groups", "ctx"), "head")
    return jax.shard_map(
        local,
        mesh=mesh,
        in_specs=(placed,) * 4,
        out_specs=(placed,) * 4,
        check_vma=False,
    )
```

time: 236 us -> 96.2 us (0.41)
  waiting for transfers between devices: 89.8 us -> 19.8 us
  blocking collectives: 37.9 us -> 0 us
  matrix products: 28.7 us -> 0 us
  Pallas kernels: 0 us -> 17.1 us
  between operations: 14.4 us -> 1.04 us
  local copies, waits for them, and re-layouts: 33.5 us -> 21.8 us
  starting transfers between devices: 18.8 us -> 30 us
  other arithmetic: 10.7 us -> 5.67 us
    unnamed x2 -> x0, waiting for transfers between devices: 52.8 us -> none
    all_gather x1 -> x0, blocking collectives: 37.9 us -> none  [local(): strided = lax.all_gather(local_strided, 'ctx', axis=0, tiled=True)]
    dot_general x48 -> x0, matrix products: 28.7 us -> none  [the longest x8 8.61 us: head_terms(): jnp.einsum('rqk,qrd->kd', probability_lowp, grad_heads, preferred_element...]
    ppermute x8 -> x15, waiting for transfers between devices: 37 us -> 19.2 us  [the longest x8 19.1 us: shifted(): lax.ppermute(x, 'ctx', [(i, i + by) for i in range(peers) if 0 <= i + by...]
    pallas_call x0 -> x2, Pallas kernels: none -> 17.1 us  [attention(): pl.pallas_call(attention_kernel, name=f'attention_{chunk}', grid_spec=plt...]
    all_to_all x0 -> x2, starting transfers between devices: none -> 7.2 us  [exchanged(): return lax.all_to_all(x, 'ctx', 0, 0, axis_index_groups=groups, tiled=True)]
    dynamic_slice x8 -> x3, local copies, waits for them, and re-layouts: 7.89 us -> 2.39 us  [part(): return lax.dynamic_slice_in_dim(x, which * width, width, 1)]
    dynamic_update_slice x8 -> x0, local copies, waits for them, and re-layouts: 5.36 us -> none  [local(): lax.map(per_head, (query_split, grad_split, key_split, value_split))]
  transfers between devices with their start and end apart: 9 -> 17, of which waited for: 4 -> 5; matrix products, arithmetic and copies ran while one was open for 4% -> 10% of each run, Pallas kernels for 0% -> 8%
where the time goes in v1:
time: 96.2 us; the launch traced here: 95.4 us
  starting transfers between devices  30 us (31%)
  local copies, waits for them, and re-layouts  21.8 us (23%)
  waiting for transfers between devices  19.8 us (21%)
  Pallas kernels  17.1 us (18%)
  other arithmetic  5.67 us (6%)
  between operations  1.04 us (1%)
    ppermute x8, starting transfers between devices, shifted(): lax.ppermute(x, 'ctx', [(i, i + by) for i in range(peers) if 0 <= i + by...  21.2 us
    ppermute x8, waiting for transfers between devices, shifted(): lax.ppermute(x, 'ctx', [(i, i + by) for i in range(peers) if 0 <= i + by...  19.1 us
    pallas_call x2, Pallas kernels, attention(): pl.pallas_call(attention_kernel, name=f'attention_{chunk}', grid_spec=plt...  17.1 us
    unnamed x38, local copies, waits for them, and re-layouts  12.9 us
    all_to_all x2, starting transfers between devices, exchanged(): return lax.all_to_all(x, 'ctx', 0, 0, axis_index_groups=groups, tiled=True)  7.2 us
    dynamic_slice x3, local copies, waits for them, and re-layouts, part(): return lax.dynamic_slice_in_dim(x, which * width, width, 1)  2.39 us
    another operation x2, local copies, waits for them, and re-layouts, local(): jnp.stack([keys.reshape(half, kv_heads, HEAD_SIZE), values.reshape(half,...  2.26 us
  transfers between devices with their start and end apart: 17, of which 5 were waited for; matrix products, arithmetic and copies ran while one was open for 10% of the time, Pallas kernels for 8%

profile of v1, /device:TPU:0, one launch (start us, length us, event | category | flops | bytes accessed | tf_op | source)
XLA Modules:
  0.0 95.4 jit_solution(28679125809366273)
XLA Ops:
  0.6 1.1 %stack_reshape.8 = bf16[128,8,1,128]{3,2,1,0:T(2,128)(2,1)S(1)} reshape(bf16[128,1024]{1,0:T(8,128)(2,1)} %param.5) | data formatting | bytes 524288 | tf_op jit(solution)/shard_map/stack;reshape | solution.py:238
  1.8 1.1 %stack_reshape.9 = bf16[128,8,1,128]{3,2,1,0:T(2,128)(2,1)S(1)} reshape(bf16[128,1024]{1,0:T(8,128)(2,1)} %param.6) | data formatting | bytes 524288 | tf_op jit(solution)/shard_map/stack;reshape | solution.py:238
  2.9 1.2 %pad_maximum_fusion = bf16[128,8,2,128]{3,2,1,0:T(2,128)(2,1)S(1)} fusion(bf16[128,8,1,128]{3,2,1,0:T(2,128)(2,1)S(1)} %stack_reshape.9, bf16[128,8,1,128]{3,2,1,0:T(2,128)(2,1)S(1)} %stack_reshape.8), kind=kLoop, calls=%fused_computation.4 | loop fusion | flops 1048576 | bytes 1048576 | tf_op jit(solution)/shard_map/stack | solution.py:238
  7.9 1.0 %constant_dynamic-slice_fusion.1 = (bf16[128,512]{1,0:T(8,128)(2,1)S(1)}, bf16[128,512]{1,0:T(8,128)(2,1)S(1)}) fusion(bf16[128,2048]{1,0:T(8,128)(2,1)} %copy-done.15, s32[]{:T(128)S(6)} %select_n.57, s32[]{:T(128)S(6)} %add.46), kind=kLoop, calls=%fused_computation.16 | loop fusion | bytes 524296 | tf_op jit(solution)/shard_map/slice | solution.py:247
  9.0 4.5 %collective-permute-start.3 = (bf16[256,512]{1,0:T(8,128)(2,1)S(1)}, bf16[256,512]{1,0:T(8,128)(2,1)S(1)}, u32[]{:S(2)}, u32[]{:S(2)}) collective-permute-start(bf16[256,512]{1,0:T(8,128)(2,1)S(1)} %pad_maximum_fusion.1.kv_here), channel_id=1, source_target_pairs={{0,2},{1,3},{2,4},{3,5},{4,6},{5,7},{6,8},{7,9},{8,10},{9,11},{10,... | collective-permute-start | bytes 786440 | tf_op jit(solution)/shard_map/ppermute | solution.py:222
  13.4 3.5 %collective-permute-start.4 = (bf16[256,512]{1,0:T(8,128)(2,1)S(1)}, bf16[256,512]{1,0:T(8,128)(2,1)S(1)}, u32[]{:S(2)}, u32[]{:S(2)}) collective-permute-start(bf16[256,512]{1,0:T(8,128)(2,1)S(1)} %pad_maximum_fusion.1.kv_here), channel_id=1, source_target_pairs={{0,4},{1,5},{2,6},{3,7},{4,8},{5,9},{6,10},{7,11},{8,12},{9,13},{1... | collective-permute-start | bytes 786440 | tf_op jit(solution)/shard_map/ppermute | solution.py:222
  19.7 3.9 %all-to-all-start = ((bf16[8,2,1024]{2,1,0:T(2,128)(2,1)}), bf16[8,2,1024]{2,1,0:T(2,128)(2,1)S(1)}, u32[]{:S(2)}, u32[]{:S(2)}) async-start(bf16[8,2,1024]{2,1,0:T(2,128)(2,1)} %reshape.53), calls=%async_computation | async-start | bytes 65536 | tf_op jit(solution)/shard_map/all_to_all | solution.py:226
  23.6 4.7 %collective-permute-start.5 = (bf16[256,512]{1,0:T(8,128)(2,1)S(1)}, bf16[256,512]{1,0:T(8,128)(2,1)}, u32[]{:S(2)}, u32[]{:S(2)}) collective-permute-start(bf16[256,512]{1,0:T(8,128)(2,1)S(1)} %pad_maximum_fusion.2.kv_here), channel_id=1, source_target_pairs={{0,2},{1,3},{2,4},{3,5},{4,6},{5,7},{6,8},{7,9},{8,10},{9,11},{10,... | collective-permute-start | bytes 786440 | tf_op jit(solution)/shard_map/ppermute | solution.py:222
  28.3 3.4 %collective-permute-start.6 = (bf16[256,512]{1,0:T(8,128)(2,1)S(1)}, bf16[256,512]{1,0:T(8,128)(2,1)}, u32[]{:S(2)}, u32[]{:S(2)}) collective-permute-start(bf16[256,512]{1,0:T(8,128)(2,1)S(1)} %pad_maximum_fusion.2.kv_here), channel_id=1, source_target_pairs={{0,4},{1,5},{2,6},{3,7},{4,8},{5,9},{6,10},{7,11},{8,12},{9,13},{1... | collective-permute-start | bytes 786440 | tf_op jit(solution)/shard_map/ppermute | solution.py:222
  33.5 1.2 %copy-done.2 = bf16[128,4096]{1,0:T(8,128)(2,1)S(1)} copy-done((bf16[128,4096]{1,0:T(8,128)(2,1)S(1)}, bf16[128,4096]{1,0:T(8,128)(2,1)}, u32[]{:S(2)}) %copy-start.2) | copy-done | bytes 1048600
  34.7 1.0 %copy-done.4 = bf16[128,2048]{1,0:T(8,128)(2,1)S(1)} copy-done((bf16[128,2048]{1,0:T(8,128)(2,1)S(1)}, bf16[128,2048]{1,0:T(8,128)(2,1)}, u32[]{:S(2)}) %copy-start.4) | copy-done | bytes 524312
  37.7 8.1 %attention_0.1 = (bf16[128,1024]{1,0:T(8,128)(2,1)S(1)}, bf16[128,1024]{1,0:T(8,128)(2,1)S(1)}, f32[2,4,256]{2,1,0:T(4,128)S(1)}, f32[256,512]{1,0:T(8,128)S(1)}...) custom-call(s32[2]{0:T(128)S(1)} %pad_add_fusion.place, ...), custom_call_target="tpu_custom_call" | custom-call | flops 2055208960 | bytes 4194304 | tf_op jit(solution)/shard_map/attention_0/pallas_call | solution.py:168
  47.9 9.0 %attention_1.1 = (bf16[128,1024]{1,0:T(8,128)(2,1)S(1)}, bf16[128,1024]{1,0:T(8,128)(2,1)S(1)}, f32[2,4,256]{2,1,0:T(4,128)S(1)}, f32[256,512]{1,0:T(8,128)S(1)}...) custom-call(s32[2]{0:T(128)S(1)} %pad_add_fusion.place, ...), custom_call_target="tpu_custom_call" | custom-call | flops 2055208960 | bytes 4194304 | tf_op jit(solution)/shard_map/attention_1/pallas_call | solution.py:168
  59.8 3.3 %all-to-all-start.1 = ((f32[8,1,2048]{2,1,0:T(1,128)}), f32[8,1,2048]{2,1,0:T(1,128)S(1)}, u32[]{:S(2)}, u32[]{:S(2)}) async-start(f32[8,1,2048]{2,1,0:T(1,128)} %all_to_all.13), calls=%async_computation.1 | async-start | bytes 131072 | tf_op jit(solution)/shard_map/all_to_all | solution.py:226
  63.2 1.3 %collective-permute-start.10 = (bf16[256,512]{1,0:T(8,128)(2,1)}, bf16[256,512]{1,0:T(8,128)(2,1)S(1)}, u32[]{:S(2)}, u32[]{:S(2)}) collective-permute-start(bf16[256,512]{1,0:T(8,128)(2,1)} %copy-done.9), channel_id=1, source_target_pairs={{4,0},{5,1},{6,2},{7,3},{8,4},{9,5},{10,6},{11,7},{12,8},{13,9},{1... | collective-permute-start | bytes 786440 | tf_op jit(solution)/shard_map/ppermute | solution.py:222
  64.5 1.3 %collective-permute-start.9 = (bf16[256,512]{1,0:T(8,128)(2,1)}, bf16[256,512]{1,0:T(8,128)(2,1)S(1)}, u32[]{:S(2)}, u32[]{:S(2)}) collective-permute-start(bf16[256,512]{1,0:T(8,128)(2,1)} %copy-done.7), channel_id=1, source_target_pairs={{2,0},{3,1},{4,2},{5,3},{6,4},{7,5},{8,6},{9,7},{10,8},{11,9},{12,... | collective-permute-start | bytes 786440 | tf_op jit(solution)/shard_map/ppermute | solution.py:222
  65.8 1.3 %collective-permute-start.11 = (bf16[256,512]{1,0:T(8,128)(2,1)}, bf16[256,512]{1,0:T(8,128)(2,1)S(1)}, u32[]{:S(2)}, u32[]{:S(2)}) collective-permute-start(bf16[256,512]{1,0:T(8,128)(2,1)} %copy-done.10), channel_id=1, source_target_pairs={{2,0},{3,1},{4,2},{5,3},{6,4},{7,5},{8,6},{9,7},{10,8},{11,9},{12,... | collective-permute-start | bytes 786440 | tf_op jit(solution)/shard_map/ppermute | solution.py:222
  67.1 1.3 %collective-permute-start.12 = (bf16[256,512]{1,0:T(8,128)(2,1)}, bf16[256,512]{1,0:T(8,128)(2,1)S(1)}, u32[]{:S(2)}, u32[]{:S(2)}) collective-permute-start(bf16[256,512]{1,0:T(8,128)(2,1)} %copy-done.8), channel_id=1, source_target_pairs={{4,0},{5,1},{6,2},{7,3},{8,4},{9,5},{10,6},{11,7},{12,8},{13,9},{1... | collective-permute-start | bytes 786440 | tf_op jit(solution)/shard_map/ppermute | solution.py:222
  70.3 4.4 %collective-permute-done.10 = bf16[256,512]{1,0:T(8,128)(2,1)S(1)} collective-permute-done((bf16[256,512]{1,0:T(8,128)(2,1)}, bf16[256,512]{1,0:T(8,128)(2,1)S(1)}, u32[]{:S(2)}, u32[]{:S(2)}) %collective-permute-start.10) | collective-permute-done | bytes 262176 | tf_op jit(solution)/shard_map/ppermute | solution.py:222
  74.6 1.1 %collective-permute-done.9 = bf16[256,512]{1,0:T(8,128)(2,1)S(1)} collective-permute-done((bf16[256,512]{1,0:T(8,128)(2,1)}, bf16[256,512]{1,0:T(8,128)(2,1)S(1)}, u32[]{:S(2)}, u32[]{:S(2)}) %collective-permute-start.9) | collective-permute-done | bytes 262176 | tf_op jit(solution)/shard_map/ppermute | solution.py:222
  76.4 1.0 %convert_add_fusion.1 = f32[256,512]{1,0:T(8,128)S(1)} fusion(bf16[256,512]{1,0:T(8,128)(2,1)S(1)} %collective-permute-done.10, f32[256,512]{1,0:T(8,128)S(1)} %get-tuple-element.22, bf16[256,512]{1,0:T(8,128)(2,1)} %copy-done.16), kind=kLoop, calls=%fused_computation.7 | loop fusion | flops 524288 | bytes 1572864 | tf_op jit(solution)/shard_map/add | solution.py:281
  77.4 3.6 %collective-permute-done.11 = bf16[256,512]{1,0:T(8,128)(2,1)S(1)} collective-permute-done((bf16[256,512]{1,0:T(8,128)(2,1)}, bf16[256,512]{1,0:T(8,128)(2,1)S(1)}, u32[]{:S(2)}, u32[]{:S(2)}) %collective-permute-start.11) | collective-permute-done | bytes 262176 | tf_op jit(solution)/shard_map/ppermute | solution.py:222
  81.0 10.1 %collective-permute-done.12 = bf16[256,512]{1,0:T(8,128)(2,1)S(1)} collective-permute-done((bf16[256,512]{1,0:T(8,128)(2,1)}, bf16[256,512]{1,0:T(8,128)(2,1)S(1)}, u32[]{:S(2)}, u32[]{:S(2)}) %collective-permute-start.12) | collective-permute-done | bytes 262176 | tf_op jit(solution)/shard_map/ppermute | solution.py:222
  92.0 1.2 %maximum_select_fusion = bf16[128,4096]{1,0:T(8,128)(2,1)} fusion(bf16[128,1024]{1,0:T(8,128)(2,1)S(1)} %collective-permute-done.8, bf16[128,1024]{1,0:T(8,128)(2,1)S(1)} %collective-permute-done.7, bf16[128,1024]{1,0:T(8,128)(2,1)S(1)} %get-tuple-element.19, bf16[128,1024]{1,0:T(8,128)(2,1)S(1)} %get-tuple-element.18, pred[]{:T(512)S(6)} %eq.29), kind=kLoop, calls=%fused_computation | loop fusion | flops 8912896 | bytes 2097153 | tf_op jit(solution)/shard_map/jit(_where)/select_n | solution.py:232
  (90 shorter events, 20.8 us)
Async XLA Ops:
  4.1 1.6 %copy-start = (bf16[128,4096]{1,0:T(8,128)(2,1)S(1)}, bf16[128,4096]{1,0:T(8,128)(2,1)}, u32[]{:S(2)}) copy-start(bf16[128,4096]{1,0:T(8,128)(2,1)} %q_own.3) | copy-start | bytes 3145732
  4.5 2.1 %copy-start.15 = (bf16[128,2048]{1,0:T(8,128)(2,1)}, bf16[128,2048]{1,0:T(8,128)(2,1)S(1)}, u32[]{:S(2)}) copy-start(bf16[128,2048]{1,0:T(8,128)(2,1)S(1)} %reshape.48) | copy-start | bytes 1572868
  4.5 2.1 %copy-start.1 = (bf16[128,4096]{1,0:T(8,128)(2,1)S(1)}, bf16[128,4096]{1,0:T(8,128)(2,1)}, u32[]{:S(2)}) copy-start(bf16[128,4096]{1,0:T(8,128)(2,1)} %o_own.3) | copy-start | bytes 3145732
  5.3 3.6 %collective-permute-start.2 = (bf16[128,1024]{1,0:T(8,128)(2,1)}, bf16[128,1024]{1,0:T(8,128)(2,1)S(1)}, u32[]{:S(2)}, u32[]{:S(2)}) collective-permute-start(bf16[128,1024]{1,0:T(8,128)(2,1)} %constant_dynamic-slice_fusion.2), channel_id=1, source_target_pairs={{0,1},{1,0},{2,3},{3,2},{4,5},{5,4},{6,7},{7,6},{8,9},{9,8},{10,11... | collective-permute-start | bytes 786440 | tf_op jit(solution)/shard_map/ppermute | solution.py:219
  6.6 26.1 %collective-permute-start = (bf16[128,2048]{1,0:T(8,128)(2,1)}, bf16[128,2048]{1,0:T(8,128)(2,1)S(1)}, u32[]{:S(2)}, u32[]{:S(2)}) collective-permute-start(bf16[128,2048]{1,0:T(8,128)(2,1)} %constant_dynamic-slice_fusion.5), channel_id=1, source_target_pairs={{0,1},{1,0},{2,3},{3,2},{4,5},{5,4},{6,7},{7,6},{8,9},{9,8},{10,11... | collective-permute-start | bytes 1572872 | tf_op jit(solution)/shard_map/ppermute | solution.py:219
  7.5 25.2 %collective-permute-start.1 = (bf16[128,2048]{1,0:T(8,128)(2,1)}, bf16[128,2048]{1,0:T(8,128)(2,1)S(1)}, u32[]{:S(2)}, u32[]{:S(2)}) collective-permute-start(bf16[128,2048]{1,0:T(8,128)(2,1)} %constant_dynamic-slice_fusion.4), channel_id=1, source_target_pairs={{0,1},{1,0},{2,3},{3,2},{4,5},{5,4},{6,7},{7,6},{8,9},{9,8},{10,11... | collective-permute-start | bytes 1572872 | tf_op jit(solution)/shard_map/ppermute | solution.py:219
  9.0 19.3 %collective-permute-start.3 = (bf16[256,512]{1,0:T(8,128)(2,1)S(1)}, bf16[256,512]{1,0:T(8,128)(2,1)S(1)}, u32[]{:S(2)}, u32[]{:S(2)}) collective-permute-start(bf16[256,512]{1,0:T(8,128)(2,1)S(1)} %pad_maximum_fusion.1.kv_here), channel_id=1, source_target_pairs={{0,2},{1,3},{2,4},{3,5},{4,6},{5,7},{6,8},{7,9},{8,10},{9,11},{10,... | collective-permute-start | bytes 786440 | tf_op jit(solution)/shard_map/ppermute | solution.py:222
  13.4 18.5 %collective-permute-start.4 = (bf16[256,512]{1,0:T(8,128)(2,1)S(1)}, bf16[256,512]{1,0:T(8,128)(2,1)S(1)}, u32[]{:S(2)}, u32[]{:S(2)}) collective-permute-start(bf16[256,512]{1,0:T(8,128)(2,1)S(1)} %pad_maximum_fusion.1.kv_here), channel_id=1, source_target_pairs={{0,4},{1,5},{2,6},{3,7},{4,8},{5,9},{6,10},{7,11},{8,12},{9,13},{1... | collective-permute-start | bytes 786440 | tf_op jit(solution)/shard_map/ppermute | solution.py:222
  19.7 12.0 %all-to-all-start = ((bf16[8,2,1024]{2,1,0:T(2,128)(2,1)}), bf16[8,2,1024]{2,1,0:T(2,128)(2,1)S(1)}, u32[]{:S(2)}, u32[]{:S(2)}) async-start(bf16[8,2,1024]{2,1,0:T(2,128)(2,1)} %reshape.53), calls=%async_computation | async-start | bytes 65536 | tf_op jit(solution)/shard_map/all_to_all | solution.py:226
  23.6 24.3 %collective-permute-start.5 = (bf16[256,512]{1,0:T(8,128)(2,1)S(1)}, bf16[256,512]{1,0:T(8,128)(2,1)}, u32[]{:S(2)}, u32[]{:S(2)}) collective-permute-start(bf16[256,512]{1,0:T(8,128)(2,1)S(1)} %pad_maximum_fusion.2.kv_here), channel_id=1, source_target_pairs={{0,2},{1,3},{2,4},{3,5},{4,6},{5,7},{6,8},{7,9},{8,10},{9,11},{10,... | collective-permute-start | bytes 786440 | tf_op jit(solution)/shard_map/ppermute | solution.py:222
  28.3 4.4 %copy-start.11 = (bf16[256,512]{1,0:T(8,128)(2,1)}, bf16[256,512]{1,0:T(8,128)(2,1)S(1)}, u32[]{:S(2)}) copy-start(bf16[256,512]{1,0:T(8,128)(2,1)S(1)} %collective-permute-done.3.kv_near) | copy-start | bytes 786436
  28.3 19.6 %collective-permute-start.6 = (bf16[256,512]{1,0:T(8,128)(2,1)S(1)}, bf16[256,512]{1,0:T(8,128)(2,1)}, u32[]{:S(2)}, u32[]{:S(2)}) collective-permute-start(bf16[256,512]{1,0:T(8,128)(2,1)S(1)} %pad_maximum_fusion.2.kv_here), channel_id=1, source_target_pairs={{0,4},{1,5},{2,6},{3,7},{4,8},{5,9},{6,10},{7,11},{8,12},{9,13},{1... | collective-permute-start | bytes 786440 | tf_op jit(solution)/shard_map/ppermute | solution.py:222
  33.5 1.2 %copy-start.2 = (bf16[128,4096]{1,0:T(8,128)(2,1)S(1)}, bf16[128,4096]{1,0:T(8,128)(2,1)}, u32[]{:S(2)}) copy-start(bf16[128,4096]{1,0:T(8,128)(2,1)} %o_own.3) | copy-start | bytes 3145732
  34.7 1.0 %copy-start.4 = (bf16[128,2048]{1,0:T(8,128)(2,1)S(1)}, bf16[128,2048]{1,0:T(8,128)(2,1)}, u32[]{:S(2)}) copy-start(bf16[128,2048]{1,0:T(8,128)(2,1)} %copy-done.3) | copy-start | bytes 1572868
  35.8 0.9 copy-start.12
  59.0 9.4 %collective-permute-start.14 = (f32[16,128]{1,0:T(8,128)S(1)}, f32[16,128]{1,0:T(8,128)S(1)}, u32[]{:S(2)}, u32[]{:S(2)}) collective-permute-start(f32[16,128]{1,0:T(8,128)S(1)} %get-tuple-element.53), channel_id=1, source_target_pairs={{0,1},{1,0},{2,3},{3,2},{4,5},{5,4},{6,7},{7,6},{8,9},{9,8},{10,11... | collective-permute-start | bytes 24584 | tf_op jit(solution)/shard_map/ppermute | solution.py:219
  59.8 10.4 %all-to-all-start.1 = ((f32[8,1,2048]{2,1,0:T(1,128)}), f32[8,1,2048]{2,1,0:T(1,128)S(1)}, u32[]{:S(2)}, u32[]{:S(2)}) async-start(f32[8,1,2048]{2,1,0:T(1,128)} %all_to_all.13), calls=%async_computation.1 | async-start | bytes 131072 | tf_op jit(solution)/shard_map/all_to_all | solution.py:226
  63.2 11.4 %collective-permute-start.10 = (bf16[256,512]{1,0:T(8,128)(2,1)}, bf16[256,512]{1,0:T(8,128)(2,1)S(1)}, u32[]{:S(2)}, u32[]{:S(2)}) collective-permute-start(bf16[256,512]{1,0:T(8,128)(2,1)} %copy-done.9), channel_id=1, source_target_pairs={{4,0},{5,1},{6,2},{7,3},{8,4},{9,5},{10,6},{11,7},{12,8},{13,9},{1... | collective-permute-start | bytes 786440 | tf_op jit(solution)/shard_map/ppermute | solution.py:222
  64.5 11.2 %collective-permute-start.9 = (bf16[256,512]{1,0:T(8,128)(2,1)}, bf16[256,512]{1,0:T(8,128)(2,1)S(1)}, u32[]{:S(2)}, u32[]{:S(2)}) collective-permute-start(bf16[256,512]{1,0:T(8,128)(2,1)} %copy-done.7), channel_id=1, source_target_pairs={{2,0},{3,1},{4,2},{5,3},{6,4},{7,5},{8,6},{9,7},{10,8},{11,9},{12,... | collective-permute-start | bytes 786440 | tf_op jit(solution)/shard_map/ppermute | solution.py:222
  65.8 15.2 %collective-permute-start.11 = (bf16[256,512]{1,0:T(8,128)(2,1)}, bf16[256,512]{1,0:T(8,128)(2,1)S(1)}, u32[]{:S(2)}, u32[]{:S(2)}) collective-permute-start(bf16[256,512]{1,0:T(8,128)(2,1)} %copy-done.10), channel_id=1, source_target_pairs={{2,0},{3,1},{4,2},{5,3},{6,4},{7,5},{8,6},{9,7},{10,8},{11,9},{12,... | collective-permute-start | bytes 786440 | tf_op jit(solution)/shard_map/ppermute | solution.py:222
  67.1 24.0 %collective-permute-start.12 = (bf16[256,512]{1,0:T(8,128)(2,1)}, bf16[256,512]{1,0:T(8,128)(2,1)S(1)}, u32[]{:S(2)}, u32[]{:S(2)}) collective-permute-start(bf16[256,512]{1,0:T(8,128)(2,1)} %copy-done.8), channel_id=1, source_target_pairs={{4,0},{5,1},{6,2},{7,3},{8,4},{9,5},{10,6},{11,7},{12,8},{13,9},{1... | collective-permute-start | bytes 786440 | tf_op jit(solution)/shard_map/ppermute | solution.py:222
  68.4 23.6 %collective-permute-start.7 = (bf16[128,1024]{1,0:T(8,128)(2,1)}, bf16[128,1024]{1,0:T(8,128)(2,1)S(1)}, u32[]{:S(2)}, u32[]{:S(2)}) collective-permute-start(bf16[128,1024]{1,0:T(8,128)(2,1)} %copy-done.5), channel_id=1, source_target_pairs={{0,1},{1,0},{2,3},{3,2},{4,5},{5,4},{6,7},{7,6},{8,9},{9,8},{10,11... | collective-permute-start | bytes 786440 | tf_op jit(solution)/shard_map/ppermute | solution.py:219
  74.6 17.4 %collective-permute-start.8 = (bf16[128,1024]{1,0:T(8,128)(2,1)}, bf16[128,1024]{1,0:T(8,128)(2,1)S(1)}, u32[]{:S(2)}, u32[]{:S(2)}) collective-permute-start(bf16[128,1024]{1,0:T(8,128)(2,1)} %copy-done.6), channel_id=1, source_target_pairs={{0,1},{1,0},{2,3},{3,2},{4,5},{5,4},{6,7},{7,6},{8,9},{9,8},{10,11... | collective-permute-start | bytes 786440 | tf_op jit(solution)/shard_map/ppermute | solution.py:219
  91.5 1.7 %collective-permute-start.13 = (bf16[128,1024]{1,0:T(8,128)(2,1)S(1)}, bf16[128,1024]{1,0:T(8,128)(2,1)S(1)}, u32[]{:S(2)}, u32[]{:S(2)}) collective-permute-start(bf16[128,1024]{1,0:T(8,128)(2,1)S(1)} %get-tuple-element.47), channel_id=1, source_target_pairs={{0,1},{1,0},{2,3},{3,2},{4,5},{5,4},{6,7},{7,6},{8,9},{9,8},{10,11... | collective-permute-start | bytes 786440 | tf_op jit(solution)/shard_map/ppermute | solution.py:219
  (10 other events, 7.4 us)

commit v2 on v1

v2 whole, which is shorter than its diff:
```python
import functools
import math

import jax
import jax.numpy as jnp
from jax import lax
from jax.experimental import pallas as pl
from jax.experimental.pallas import tpu as pltpu
from jax.sharding import PartitionSpec as P

HEAD_SIZE = 128
W = 512
STRIDE = 128
CHUNKS = 2

NEG_FILL = -1e30
SCALE = 1.0 / math.sqrt(HEAD_SIZE)


def vmem_shape(shape, dtype):
    return pltpu.VMEM(shape, dtype)


def in_vmem(*arrays):
    return [pltpu.with_memory_space_constraint(x, pltpu.VMEM) for x in arrays]


def head_columns(which, width=HEAD_SIZE):
    return pl.ds(pl.multiple_of(which * width, width), width)


def dot_nt(left, right):
    return lax.dot_general(
        left, right, (((1,), (1,)), ((), ())), preferred_element_type=jnp.float32
    )


def dot_nn(left, right):
    return lax.dot_general(
        left, right, (((1,), (0,)), ((), ())), preferred_element_type=jnp.float32
    )


def dot_tn(left, right):
    return lax.dot_general(
        left, right, (((0,), (0,)), ((), ())), preferred_element_type=jnp.float32
    )


def attention_kernel(
    chunk,
    place,
    q_own,
    q_other,
    o_own,
    o_other,
    kv_here,
    kv_near,
    kv_past,
    kv_far,
    dq_own,
    dq_other,
    norm,
    g_here,
    g_near,
    g_past,
    g_far,
):
    half = q_own.shape[0]
    rows = 2 * half
    far_rows = kv_far.shape[0]
    count = kv_here.shape[1] // (2 * HEAD_SIZE)
    heads = dq_own.shape[1] // (count * HEAD_SIZE)
    core, pair = place[0], place[1]

    def token(shape, axis):
        at = lax.broadcasted_iota(jnp.int32, shape, axis)
        return at + jnp.where(at < half, core * half, -core * half)

    lower = token((rows, rows), 0) <= token((rows, rows), 1)
    far_at = lax.broadcasted_iota(jnp.int32, (far_rows, rows), 0)
    far_token = (far_at // 2) * rows + jnp.where(far_at % 2 == 0, core, 1 - core) * half
    far_open = far_token <= pair * rows + token((far_rows, rows), 1) - W
    near_bias = jnp.where(pair >= 1, 0.0, NEG_FILL)
    past_bias = jnp.where(pair >= 2, 0.0, NEG_FILL)

    def stacked(at, side):
        columns = slice((2 * at + side) * HEAD_SIZE, (2 * at + side + 1) * HEAD_SIZE)
        start = (2 * (chunk * count + at) + side) * HEAD_SIZE
        return jnp.concatenate(
            [
                kv_here[:, columns],
                kv_near[:, columns],
                kv_past[:, columns],
                kv_far[:, start : start + HEAD_SIZE],
            ],
            axis=0,
        )

    for at in range(count):
        key_all, value_all = stacked(at, 0), stacked(at, 1)
        key_terms = value_terms = None

        for head in range(heads):
            columns = slice((at * heads + head) * HEAD_SIZE, (at * heads + head + 1) * HEAD_SIZE)
            source = head_columns((core * (count * CHUNKS) + chunk * count + at) * heads + head)
            query = jnp.concatenate([q_own[:, source], q_other[:, source]], axis=0)
            grad = jnp.concatenate([o_own[:, source], o_other[:, source]], axis=0)
            score = dot_nt(key_all, query)
            edge = jnp.where(lower, score[:rows], score[2 * rows : 3 * rows] + past_bias)
            near = score[rows : 2 * rows] + near_bias
            far = jnp.where(far_open, score[3 * rows :], NEG_FILL)
            top = jnp.maximum(
                jnp.maximum(
                    jnp.max(edge, axis=0, keepdims=True), jnp.max(near, axis=0, keepdims=True)
                ),
                jnp.max(far, axis=0, keepdims=True),
            )
            edge, near, far = (
                jnp.exp2((part - top) * (SCALE * math.log2(math.e))) for part in (edge, near, far)
            )
            total = (
                jnp.sum(edge, axis=0, keepdims=True)
                + jnp.sum(near, axis=0, keepdims=True)
                + jnp.sum(far, axis=0, keepdims=True)
            )
            norm[at * heads + head : at * heads + head + 1, :] = top * SCALE + jnp.log(total)
            inverse = 1.0 / total
            edge, near, far = (part * inverse for part in (edge, near, far))
            dprob = dot_nt(value_all, grad)
            d_edge = jnp.where(lower, dprob[:rows], dprob[2 * rows : 3 * rows])
            d_near = dprob[rows : 2 * rows]
            d_far = dprob[3 * rows :]
            delta = (
                jnp.sum(edge * d_edge, axis=0, keepdims=True)
                + jnp.sum(near * d_near, axis=0, keepdims=True)
                + jnp.sum(far * d_far, axis=0, keepdims=True)
            )
            d_edge, d_near, d_far = (
                part * (d_part - delta)
                for part, d_part in ((edge, d_edge), (near, d_near), (far, d_far))
            )

            def split(on_edge, on_near, on_far):
                return jnp.concatenate(
                    [
                        jnp.where(lower, on_edge, 0.0).astype(jnp.bfloat16),
                        on_near.astype(jnp.bfloat16),
                        jnp.where(lower, 0.0, on_edge).astype(jnp.bfloat16),
                        on_far.astype(jnp.bfloat16),
                    ],
                    axis=0,
                )

            prob = split(edge, near, far)
            dscore = split(d_edge, d_near, d_far)
            value_term = dot_nn(prob, grad)
            key_term = dot_nn(dscore, query)
            value_terms = value_term if head == 0 else value_terms + value_term
            key_terms = key_term if head == 0 else key_terms + key_term
            query_term = (dot_tn(dscore, key_all) * SCALE).astype(jnp.bfloat16)
            dq_own[:, columns] = query_term[:half]
            dq_other[:, columns] = query_term[half:]

        terms = jnp.concatenate([key_terms * SCALE, value_terms], axis=1)
        columns = slice(2 * at * HEAD_SIZE, 2 * (at + 1) * HEAD_SIZE)
        g_here[:, columns] = terms[:rows]
        g_near[:, columns] = terms[rows : 2 * rows].astype(jnp.bfloat16)
        g_past[:, columns] = terms[2 * rows : 3 * rows].astype(jnp.bfloat16)
        g_far[:, columns] = terms[3 * rows :]


def attention(place, queries, q_other, grad_out, o_other, kv_here, kv_near, kv_past, kv_far, chunk):
    half = queries.shape[0]
    rows = 2 * half
    far_rows = kv_far.shape[0]
    both = 2 * HEAD_SIZE
    count = kv_here.shape[1] // both
    per_core = count * CHUNKS
    group_width = queries.shape[1] // (2 * per_core)
    heads = group_width // HEAD_SIZE

    whole = pl.BlockSpec(memory_space=pltpu.VMEM)
    keys_seen = 3 * rows + far_rows
    return pl.pallas_call(
        functools.partial(attention_kernel, chunk),
        name=f"attention_{chunk}",
        in_specs=[pl.BlockSpec(memory_space=pltpu.SMEM)] + [whole] * 8,
        out_specs=[whole] * 7,
        out_shape=[
            vmem_shape((half, count * group_width), jnp.bfloat16),
            vmem_shape((half, count * group_width), jnp.bfloat16),
            vmem_shape((count * heads, rows), jnp.float32),
            vmem_shape((rows, count * both), jnp.float32),
            vmem_shape((rows, count * both), jnp.bfloat16),
            vmem_shape((rows, count * both), jnp.bfloat16),
            vmem_shape((far_rows, count * both), jnp.float32),
        ],
        compiler_params=pltpu.CompilerParams(vmem_limit_bytes=20 * 1024 * 1024),
        cost_estimate=pl.CostEstimate(
            flops=count * heads * rows * keys_seen * HEAD_SIZE * 20,
            transcendentals=count * heads * rows * keys_seen,
            bytes_accessed=count * (6 * half * group_width * 2 + 5 * rows * both * 4),
        ),
    )(place, *in_vmem(queries, q_other, grad_out, o_other, kv_here, kv_near, kv_past, kv_far))


def arrange_kernel(place, keys, values, k_other, v_other, *outs):
    half = keys.shape[0]
    *payloads, strided = outs
    count = payloads[0].shape[1] // (2 * HEAD_SIZE)
    for chunk, payload in enumerate(payloads):
        for h in range(count):
            source = head_columns(place[0] * (count * CHUNKS) + chunk * count + h)
            for side, (mine, theirs) in enumerate(((keys, k_other), (values, v_other))):
                to = slice((2 * h + side) * HEAD_SIZE, (2 * h + side + 1) * HEAD_SIZE)
                payload[:half, to] = mine[:, source]
                payload[half:, to] = theirs[:, source]
        width = payload.shape[1]
        strided[0:1, chunk * width : (chunk + 1) * width] = payload[0:1, :]
        strided[1:2, chunk * width : (chunk + 1) * width] = payload[half : half + 1, :]


def arrange(place, keys, values, k_other, v_other):
    half, kv_width = keys.shape
    whole = pl.BlockSpec(memory_space=pltpu.VMEM)
    payload = vmem_shape((2 * half, kv_width // CHUNKS), keys.dtype)
    return pl.pallas_call(
        arrange_kernel,
        name="arrange",
        in_specs=[pl.BlockSpec(memory_space=pltpu.SMEM)] + [whole] * 4,
        out_specs=[whole] * (CHUNKS + 1),
        out_shape=[payload] * CHUNKS + [vmem_shape((2, kv_width), keys.dtype)],
    )(place, *in_vmem(keys, values, k_other, v_other))


def collect_kernel(chunk, here, near, past, strided, mine, theirs):
    half, width = mine.shape
    extra = jnp.sum(strided[:, :, chunk * width : (chunk + 1) * width], axis=0)
    total = here[...] + near[...].astype(jnp.float32) + past[...].astype(jnp.float32)
    row = lax.broadcasted_iota(jnp.int32, (half, 1), 0)
    mine[...] = (total[:half] + jnp.where(row == 0, extra[0:1], 0.0)).astype(mine.dtype)
    theirs[...] = (total[half:] + jnp.where(row == 0, extra[1:2], 0.0)).astype(theirs.dtype)


def collect(here, near, past, strided, chunk):
    rows, width = here.shape
    half = vmem_shape((rows // 2, width), jnp.bfloat16)
    whole = pl.BlockSpec(memory_space=pltpu.VMEM)
    return pl.pallas_call(
        functools.partial(collect_kernel, chunk),
        name=f"collect_{chunk}",
        in_specs=[whole] * 4,
        out_specs=[whole, whole],
        out_shape=[half, half],
        cost_estimate=pl.CostEstimate(
            flops=rows * width * 4, transcendentals=0, bytes_accessed=rows * width * 10
        ),
    )(*in_vmem(here, near, past, strided))


def place_kernel(place, *refs):
    *parts, grad_keys, grad_values = refs
    count = parts[0].shape[1] // (2 * HEAD_SIZE)
    for chunk in range(CHUNKS):
        mine, theirs = parts[2 * chunk : 2 * chunk + 2]
        for h in range(count):
            at = chunk * count + h
            for core, block in ((place[0], mine), (1 - place[0], theirs)):
                to = head_columns(core * (count * CHUNKS) + at)
                grad_keys[:, to] = block[:, 2 * h * HEAD_SIZE : (2 * h + 1) * HEAD_SIZE]
                grad_values[:, to] = block[:, (2 * h + 1) * HEAD_SIZE : (2 * h + 2) * HEAD_SIZE]


def placed_grads(place, parts, half, kv_width):
    whole = pl.BlockSpec(memory_space=pltpu.VMEM)
    out = jax.ShapeDtypeStruct((half, kv_width), jnp.bfloat16)
    return pl.pallas_call(
        place_kernel,
        name="place",
        in_specs=[pl.BlockSpec(memory_space=pltpu.SMEM)] + [whole] * len(parts),
        out_specs=[whole, whole],
        out_shape=[out, out],
    )(place, *in_vmem(*parts))


def local(queries, keys, values, grad_out):
    half, kv_width = keys.shape
    kv_heads = kv_width // HEAD_SIZE
    rows = 2 * half
    peers = lax.axis_size("ctx")
    pairs = peers // 2
    assert half == STRIDE and W == 2 * rows and peers % 2 == 0 and kv_heads % (2 * CHUNKS) == 0
    index = lax.axis_index("ctx")
    core, pair = index & 1, index >> 1
    place = jnp.stack([core, pair]).astype(jnp.int32)

    def swap(x):
        return lax.ppermute(x, "ctx", [(i, i ^ 1) for i in range(peers)])

    def shifted(x, by):
        return lax.ppermute(x, "ctx", [(i, i + by) for i in range(peers) if 0 <= i + by < peers])

    def exchanged(x):
        groups = [list(range(parity, peers, 2)) for parity in range(2)]
        return lax.all_to_all(x, "ctx", 0, 0, axis_index_groups=groups)

    def joined(mine, theirs):
        return jnp.where(
            core == 0,
            jnp.concatenate([mine, theirs], axis=1),
            jnp.concatenate([theirs, mine], axis=1),
        )

    *here, strided = arrange(place, keys, values, swap(keys), swap(values))
    near = [shifted(payload, 2) for payload in here]
    past = [shifted(payload, 4) for payload in here]
    far = exchanged(jnp.broadcast_to(strided[None], (pairs, 2, kv_width)))
    far = far.reshape(2 * pairs, kv_width)
    q_other, o_other = swap(queries), swap(grad_out)

    dq_own, dq_other, norms, sums, far_terms = [], [], [], [], []
    for chunk in range(CHUNKS):
        out = attention(
            place,
            queries,
            q_other,
            grad_out,
            o_other,
            here[chunk],
            near[chunk],
            past[chunk],
            far,
            chunk,
        )
        sums.append((out[3], shifted(out[4], -2), shifted(out[5], -4)))
        dq_own.append(out[0])
        dq_other.append(swap(out[1]))
        norms.append(out[2])
        far_terms.append(out[6])

    strided_terms = exchanged(jnp.concatenate(far_terms, axis=1).reshape(pairs, 2, kv_width))
    parts = []
    for chunk, (own, near_terms, past_terms) in enumerate(sums):
        mine, theirs = collect(own, near_terms, past_terms, strided_terms, chunk)
        parts += [mine, swap(theirs)]
    grad_keys, grad_values = placed_grads(place, parts, half, kv_width)
    grad_queries = joined(jnp.concatenate(dq_own, axis=1), jnp.concatenate(dq_other, axis=1))
    norm = jnp.concatenate(norms, axis=0)
    log_norm = joined(norm[:, :half].T, swap(norm[:, half:]).T)
    return (grad_queries, grad_keys, grad_values, log_norm)


def solution(mesh):
    placed = P(("groups", "ctx"), "head")
    return jax.shard_map(
        local,
        mesh=mesh,
        in_specs=(placed,) * 4,
        out_specs=(placed,) * 4,
        check_vma=False,
    )
```

time: 96.2 us -> 87.4 us (0.909)
  local copies, waits for them, and re-layouts: 21.8 us -> 7.05 us
  Pallas kernels: 17.1 us -> 21.5 us
  starting transfers between devices: 30 us -> 34.4 us
  other arithmetic: 5.67 us -> 3.68 us
    ppermute x8, waiting for transfers between devices: 19.1 us -> 2.53 us  [shifted(): lax.ppermute(x, 'ctx', [(i, i + by) for i in range(peers) if 0 <= i + by...]
    all_to_all x2, waiting for transfers between devices: 0.61 us -> 13.8 us  [exchanged(): return lax.all_to_all(x, 'ctx', 0, 0, axis_index_groups=groups)]
    unnamed x38 -> x19, local copies, waits for them, and re-layouts: 12.9 us -> 5.73 us
    all_to_all x2, starting transfers between devices: 7.2 us -> 12.3 us  [exchanged(): return lax.all_to_all(x, 'ctx', 0, 0, axis_index_groups=groups)]
    pallas_call x2 -> x6, Pallas kernels: 17.1 us -> 21.5 us  [the longest x2 18.8 us: attention(): pl.pallas_call(functools.partial(attention_kernel, chunk), name=f'attenti...]
    ppermute x7 -> x9, waiting for transfers between devices: 0.02 us -> 2.81 us  [swap(): return lax.ppermute(x, 'ctx', [(i, i ^ 1) for i in range(peers)])]
    dynamic_slice x3 -> x0, local copies, waits for them, and re-layouts: 2.39 us -> none  [part(): return lax.dynamic_slice_in_dim(x, which * width, width, 1)]
    another operation x2 -> x0, local copies, waits for them, and re-layouts: 2.26 us -> none  [local(): jnp.stack([keys.reshape(half, kv_heads, HEAD_SIZE), values.reshape(half,...]
  transfers between devices with their start and end apart: 17 -> 19, of which waited for: 5 -> 5; matrix products, arithmetic and copies ran while one was open for 10% -> 6% of each run, Pallas kernels for 8% -> 12%
where the time goes in v2:
time: 87.4 us; the launch traced here: 86.7 us
  starting transfers between devices  34.4 us (39%)
  Pallas kernels  21.5 us (25%)
  waiting for transfers between devices  19.1 us (22%)
  local copies, waits for them, and re-layouts  7.05 us (8%)
  other arithmetic  3.68 us (4%)
  between operations  0.88 us (1%)
    ppermute x8, starting transfers between devices, shifted(): lax.ppermute(x, 'ctx', [(i, i + by) for i in range(peers) if 0 <= i + by...  19.8 us
    pallas_call x2, Pallas kernels, attention(): pl.pallas_call(functools.partial(attention_kernel, chunk), name=f'attenti...  18.8 us
    all_to_all x2, waiting for transfers between devices, exchanged(): return lax.all_to_all(x, 'ctx', 0, 0, axis_index_groups=groups)  13.8 us
    all_to_all x2, starting transfers between devices, exchanged(): return lax.all_to_all(x, 'ctx', 0, 0, axis_index_groups=groups)  12.3 us
    unnamed x19, local copies, waits for them, and re-layouts  5.73 us
    select_n x2, other arithmetic, joined(): jnp.where(core == 0, jnp.concatenate([mine, theirs], axis=1), jnp.concate...  3.07 us
    ppermute x9, waiting for transfers between devices, swap(): return lax.ppermute(x, 'ctx', [(i, i ^ 1) for i in range(peers)])  2.81 us
    ppermute x8, waiting for transfers between devices, shifted(): lax.ppermute(x, 'ctx', [(i, i + by) for i in range(peers) if 0 <= i + by...  2.53 us
  transfers between devices with their start and end apart: 19, of which 5 were waited for; matrix products, arithmetic and copies ran while one was open for 6% of the time, Pallas kernels for 12%

profile of v2, /device:TPU:0, one launch (start us, length us, event | category | flops | bytes accessed | tf_op | source)
XLA Modules:
  0.0 86.7 jit_solution(1648901970188028929)
XLA Ops:
  2.4 2.0 %collective-permute-done.2.k_other = bf16[128,1024]{1,0:T(8,128)(2,1)S(1)} collective-permute-done((bf16[128,1024]{1,0:T(8,128)(2,1)}, bf16[128,1024]{1,0:T(8,128)(2,1)S(1)}, u32[]{:S(2)}, u32[]{:S(2)}) %collective-permute-start.2) | collective-permute-done | bytes 262176 | tf_op jit(solution)/shard_map/ppermute | solution.py:299
  5.1 0.9 %copy-done = bf16[128,1024]{1,0:T(8,128)(2,1)S(1)} copy-done((bf16[128,1024]{1,0:T(8,128)(2,1)S(1)}, bf16[128,1024]{1,0:T(8,128)(2,1)}, u32[]{:S(2)}) %copy-start) | copy-done | bytes 262168
  6.1 0.9 %copy-done.1 = bf16[128,1024]{1,0:T(8,128)(2,1)S(1)} copy-done((bf16[128,1024]{1,0:T(8,128)(2,1)S(1)}, bf16[128,1024]{1,0:T(8,128)(2,1)}, u32[]{:S(2)}) %copy-start.1) | copy-done | bytes 262168
  7.0 0.9 %arrange.1 = (bf16[256,512]{1,0:T(8,128)(2,1)S(1)}, bf16[256,512]{1,0:T(8,128)(2,1)S(1)}, bf16[2,1024]{1,0:T(2,128)(2,1)S(1)}) custom-call(s32[2]{0:T(128)} %pad_add_fusion.place, bf16[128,1024]{1,0:T(8,128)(2,1)S(1)} %copy-done, bf16[128,1024]{1,0:T(8,128)(2,1)S(1)} %copy-done.1, bf16[128,1024]{1,0:T(8,128)(2,1)S(1)} %collective-permute-done.2.k_other, ...), custom_call_target="tpu_custom_call" | custom-call | tf_op jit(solution)/shard_map/arrange/pallas_call | solution.py:228
  8.0 4.9 %collective-permute-start.5 = (bf16[256,512]{1,0:T(8,128)(2,1)S(1)}, bf16[256,512]{1,0:T(8,128)(2,1)S(1)}, u32[]{:S(2)}, u32[]{:S(2)}) collective-permute-start(bf16[256,512]{1,0:T(8,128)(2,1)S(1)} %get-tuple-element.27.kv_here), channel_id=1, source_target_pairs={{0,4},{1,5},{2,6},{3,7},{4,8},{5,9},{6,10},{7,11},{8,12},{9,13},{1... | collective-permute-start | bytes 786440 | tf_op jit(solution)/shard_map/ppermute | solution.py:302
  12.9 3.4 %collective-permute-start.4 = (bf16[256,512]{1,0:T(8,128)(2,1)S(1)}, bf16[256,512]{1,0:T(8,128)(2,1)S(1)}, u32[]{:S(2)}, u32[]{:S(2)}) collective-permute-start(bf16[256,512]{1,0:T(8,128)(2,1)S(1)} %get-tuple-element.27.kv_here), channel_id=1, source_target_pairs={{0,2},{1,3},{2,4},{3,5},{4,6},{5,7},{6,8},{7,9},{8,10},{9,11},{10,... | collective-permute-start | bytes 786440 | tf_op jit(solution)/shard_map/ppermute | solution.py:302
  17.6 3.8 %all-to-all-start = ((bf16[8,2,1024]{2,1,0:T(2,128)(2,1)}), bf16[8,2,1024]{2,1,0:T(2,128)(2,1)S(1)}, u32[]{:S(2)}, u32[]{:S(2)}) async-start(bf16[8,2,1024]{2,1,0:T(2,128)(2,1)} %broadcast_in_dim.2), calls=%async_computation | async-start | bytes 65536 | tf_op jit(solution)/shard_map/all_to_all | solution.py:306
  21.5 3.9 %collective-permute-start.7 = (bf16[256,512]{1,0:T(8,128)(2,1)S(1)}, bf16[256,512]{1,0:T(8,128)(2,1)S(1)}, u32[]{:S(2)}, u32[]{:S(2)}) collective-permute-start(bf16[256,512]{1,0:T(8,128)(2,1)S(1)} %get-tuple-element.30.kv_here), channel_id=1, source_target_pairs={{0,4},{1,5},{2,6},{3,7},{4,8},{5,9},{6,10},{7,11},{8,12},{9,13},{1... | collective-permute-start | bytes 786440 | tf_op jit(solution)/shard_map/ppermute | solution.py:302
  25.4 2.7 %all-to-all-done = bf16[8,2,1024]{2,1,0:T(2,128)(2,1)S(1)} async-done(((bf16[8,2,1024]{2,1,0:T(2,128)(2,1)}), bf16[8,2,1024]{2,1,0:T(2,128)(2,1)S(1)}, u32[]{:S(2)}, u32[]{:S(2)}) %all-to-all-start) | async-done | bytes 32800 | tf_op jit(solution)/shard_map/all_to_all | solution.py:306
  28.2 2.4 %collective-permute-start.6 = (bf16[256,512]{1,0:T(8,128)(2,1)S(1)}, bf16[256,512]{1,0:T(8,128)(2,1)S(1)}, u32[]{:S(2)}, u32[]{:S(2)}) collective-permute-start(bf16[256,512]{1,0:T(8,128)(2,1)S(1)} %get-tuple-element.30.kv_here), channel_id=1, source_target_pairs={{0,2},{1,3},{2,4},{3,5},{4,6},{5,7},{6,8},{7,9},{8,10},{9,11},{10,... | collective-permute-start | bytes 786440 | tf_op jit(solution)/shard_map/ppermute | solution.py:302
  30.7 1.2 %copy-done.4 = bf16[128,4096]{1,0:T(8,128)(2,1)S(1)} copy-done((bf16[128,4096]{1,0:T(8,128)(2,1)S(1)}, bf16[128,4096]{1,0:T(8,128)(2,1)}, u32[]{:S(2)}) %copy-start.4) | copy-done | bytes 1048600
  31.9 0.9 %copy-done.8 = bf16[256,512]{1,0:T(8,128)(2,1)S(1)} copy-done((bf16[256,512]{1,0:T(8,128)(2,1)S(1)}, bf16[256,512]{1,0:T(8,128)(2,1)}, u32[]{:S(2)}) %copy-start.8) | copy-done | bytes 262168
  32.8 9.3 %attention_0.1 = (bf16[128,1024]{1,0:T(8,128)(2,1)S(1)}, bf16[128,1024]{1,0:T(8,128)(2,1)S(1)}, f32[8,256]{1,0:T(8,128)S(1)}, f32[256,512]{1,0:T(8,128)S(1)}, bf...) custom-call(s32[2]{0:T(128)S(1)} %copy-done.2, bf16[128,4096]{1,0:T(8,128)(2,1)S(1)} %copy-done.3, ...), custom_call_target="tpu_custom_call" | custom-call | flops 4110417920 | bytes 4194304 | tf_op jit(solution)/shard_map/attention_0/pallas_call | solution.py:185
  42.1 0.9 %copy-done.6 = bf16[256,512]{1,0:T(8,128)(2,1)S(1)} copy-done((bf16[256,512]{1,0:T(8,128)(2,1)S(1)}, bf16[256,512]{1,0:T(8,128)(2,1)}, u32[]{:S(2)}) %copy-start.6) | copy-done | bytes 262168
  43.1 9.5 %attention_1.1 = (bf16[128,1024]{1,0:T(8,128)(2,1)S(1)}, bf16[128,1024]{1,0:T(8,128)(2,1)}, f32[8,256]{1,0:T(8,128)S(1)}, f32[256,512]{1,0:T(8,128)S(1)}, bf16[2...) custom-call(s32[2]{0:T(128)S(1)} %copy-done.2, bf16[128,4096]{1,0:T(8,128)(2,1)S(1)} %copy-done.3, ...), custom_call_target="tpu_custom_call" | custom-call | flops 4110417920 | bytes 4194304 | tf_op jit(solution)/shard_map/attention_1/pallas_call | solution.py:185
  52.6 1.3 %collective-permute-start.13 = (bf16[256,512]{1,0:T(8,128)(2,1)S(1)}, bf16[256,512]{1,0:T(8,128)(2,1)S(1)}, u32[]{:S(2)}, u32[]{:S(2)}) collective-permute-start(bf16[256,512]{1,0:T(8,128)(2,1)S(1)} %get-tuple-element.42), channel_id=1, source_target_pairs={{2,0},{3,1},{4,2},{5,3},{6,4},{7,5},{8,6},{9,7},{10,8},{11,9},{12,... | collective-permute-start | bytes 786440 | tf_op jit(solution)/shard_map/ppermute | solution.py:302
  54.0 1.3 %collective-permute-start.14 = (bf16[256,512]{1,0:T(8,128)(2,1)}, bf16[256,512]{1,0:T(8,128)(2,1)S(1)}, u32[]{:S(2)}, u32[]{:S(2)}) collective-permute-start(bf16[256,512]{1,0:T(8,128)(2,1)} %get-tuple-element.43), channel_id=1, source_target_pairs={{4,0},{5,1},{6,2},{7,3},{8,4},{9,5},{10,6},{11,7},{12,8},{13,9},{1... | collective-permute-start | bytes 786440 | tf_op jit(solution)/shard_map/ppermute | solution.py:302
  55.3 1.3 %collective-permute-start.10 = (bf16[256,512]{1,0:T(8,128)(2,1)}, bf16[256,512]{1,0:T(8,128)(2,1)S(1)}, u32[]{:S(2)}, u32[]{:S(2)}) collective-permute-start(bf16[256,512]{1,0:T(8,128)(2,1)} %get-tuple-element.35), channel_id=1, source_target_pairs={{2,0},{3,1},{4,2},{5,3},{6,4},{7,5},{8,6},{9,7},{10,8},{11,9},{12,... | collective-permute-start | bytes 786440 | tf_op jit(solution)/shard_map/ppermute | solution.py:302
  56.6 1.3 %collective-permute-start.11 = (bf16[256,512]{1,0:T(8,128)(2,1)}, bf16[256,512]{1,0:T(8,128)(2,1)S(1)}, u32[]{:S(2)}, u32[]{:S(2)}) collective-permute-start(bf16[256,512]{1,0:T(8,128)(2,1)} %get-tuple-element.36), channel_id=1, source_target_pairs={{4,0},{5,1},{6,2},{7,3},{8,4},{9,5},{10,6},{11,7},{12,8},{13,9},{1... | collective-permute-start | bytes 786440 | tf_op jit(solution)/shard_map/ppermute | solution.py:302
  58.5 2.5 %collective-permute-done.13.near = bf16[256,512]{1,0:T(8,128)(2,1)S(1)} collective-permute-done((bf16[256,512]{1,0:T(8,128)(2,1)S(1)}, bf16[256,512]{1,0:T(8,128)(2,1)S(1)}, u32[]{:S(2)}, u32[]{:S(2)}) %collective-permute-start.13) | collective-permute-done | bytes 262176 | tf_op jit(solution)/shard_map/ppermute | solution.py:302
  61.7 8.5 %all-to-all-start.1 = ((f32[8,2,1024]{2,1,0:T(2,128)}), f32[8,2,1024]{2,1,0:T(2,128)S(1)}, u32[]{:S(2)}, u32[]{:S(2)}) async-start(f32[8,2,1024]{2,1,0:T(2,128)} %reshape.16), calls=%async_computation.1 | async-start | bytes 131072 | tf_op jit(solution)/shard_map/all_to_all | solution.py:306
  70.7 11.1 %all-to-all-done.1.strided = f32[8,2,1024]{2,1,0:T(2,128)S(1)} async-done(((f32[8,2,1024]{2,1,0:T(2,128)}), f32[8,2,1024]{2,1,0:T(2,128)S(1)}, u32[]{:S(2)}, u32[]{:S(2)}) %all-to-all-start.1) | async-done | bytes 65568 | tf_op jit(solution)/shard_map/all_to_all | solution.py:306
  82.6 2.5 %maximum_select_fusion = bf16[128,4096]{1,0:T(8,128)(2,1)} fusion(bf16[128,1024]{1,0:T(8,128)(2,1)} %collective-permute-done.9, bf16[128,1024]{1,0:T(8,128)(2,1)} %collective-permute-done.8, bf16[128,1024]{1,0:T(8,128)(2,1)S(1)} %get-tuple-element.31, bf16[128,1024]{1,0:T(8,128)(2,1)S(1)} %get-tuple-element.29, pred[]{:T(512)S(6)} %eq.4), kind=kLoop, calls=%fused_computation | loop fusion | flops 8912896 | bytes 2097153 | tf_op jit(solution)/shard_map/jit(_where)/select_n | solution.py:309
  85.1 1.6 %place.1 = (bf16[128,1024]{1,0:T(8,128)(2,1)}, bf16[128,1024]{1,0:T(8,128)(2,1)}) custom-call(s32[2]{0:T(128)} %pad_add_fusion.place, bf16[128,512]{1,0:T(8,128)(2,1)S(1)} %get-tuple-element.39.refs_0_, bf16[128,512]{1,0:T(8,128)(2,1)S(1)} %collective-permute-done.12.refs_1_, bf16[128,512]{1,0:T(8,128)(2,1)S(1)} %get-tuple-element.44.refs_2_, ...), custom_call_target="tpu_custom_call" | custom-call | tf_op jit(solution)/shard_map/place/pallas_call | solution.py:278
  (48 shorter events, 6.6 us)
Async XLA Ops:
  0.6 30.0 %collective-permute-start = (bf16[128,4096]{1,0:T(8,128)(2,1)}, bf16[128,4096]{1,0:T(8,128)(2,1)}, u32[]{:S(2)}, u32[]{:S(2)}) collective-permute-start(bf16[128,4096]{1,0:T(8,128)(2,1)} %q_own.3), channel_id=1, source_target_pairs={{0,1},{1,0},{2,3},{3,2},{4,5},{5,4},{6,7},{7,6},{8,9},{9,8},{10,11... | collective-permute-start | bytes 3145736 | tf_op jit(solution)/shard_map/ppermute | solution.py:299
  1.1 29.5 %collective-permute-start.1 = (bf16[128,4096]{1,0:T(8,128)(2,1)}, bf16[128,4096]{1,0:T(8,128)(2,1)}, u32[]{:S(2)}, u32[]{:S(2)}) collective-permute-start(bf16[128,4096]{1,0:T(8,128)(2,1)} %o_own.3), channel_id=1, source_target_pairs={{0,1},{1,0},{2,3},{3,2},{4,5},{5,4},{6,7},{7,6},{8,9},{9,8},{10,11... | collective-permute-start | bytes 3145736 | tf_op jit(solution)/shard_map/ppermute | solution.py:299
  1.2 3.2 %collective-permute-start.2 = (bf16[128,1024]{1,0:T(8,128)(2,1)}, bf16[128,1024]{1,0:T(8,128)(2,1)S(1)}, u32[]{:S(2)}, u32[]{:S(2)}) collective-permute-start(bf16[128,1024]{1,0:T(8,128)(2,1)} %keys.1), channel_id=1, source_target_pairs={{0,1},{1,0},{2,3},{3,2},{4,5},{5,4},{6,7},{7,6},{8,9},{9,8},{10,11... | collective-permute-start | bytes 786440 | tf_op jit(solution)/shard_map/ppermute | solution.py:299
  1.7 3.5 %collective-permute-start.3 = (bf16[128,1024]{1,0:T(8,128)(2,1)}, bf16[128,1024]{1,0:T(8,128)(2,1)S(1)}, u32[]{:S(2)}, u32[]{:S(2)}) collective-permute-start(bf16[128,1024]{1,0:T(8,128)(2,1)} %values.1), channel_id=1, source_target_pairs={{0,1},{1,0},{2,3},{3,2},{4,5},{5,4},{6,7},{7,6},{8,9},{9,8},{10,11... | collective-permute-start | bytes 786440 | tf_op jit(solution)/shard_map/ppermute | solution.py:299
  7.0 23.6 %copy-start.2 = (s32[2]{0:T(128)S(1)}, s32[2]{0:T(128)}, u32[]{:S(2)}) copy-start(s32[2]{0:T(128)} %pad_add_fusion.place) | copy-start | bytes 28
  7.0 23.6 %copy-start.3 = (bf16[128,4096]{1,0:T(8,128)(2,1)S(1)}, bf16[128,4096]{1,0:T(8,128)(2,1)}, u32[]{:S(2)}) copy-start(bf16[128,4096]{1,0:T(8,128)(2,1)} %q_own.3) | copy-start | bytes 3145732
  8.0 34.1 %copy-start.5 = (bf16[256,512]{1,0:T(8,128)(2,1)}, bf16[256,512]{1,0:T(8,128)(2,1)S(1)}, u32[]{:S(2)}) copy-start(bf16[256,512]{1,0:T(8,128)(2,1)S(1)} %get-tuple-element.30.kv_here) | copy-start | bytes 786436
  8.0 20.2 %collective-permute-start.5 = (bf16[256,512]{1,0:T(8,128)(2,1)S(1)}, bf16[256,512]{1,0:T(8,128)(2,1)S(1)}, u32[]{:S(2)}, u32[]{:S(2)}) collective-permute-start(bf16[256,512]{1,0:T(8,128)(2,1)S(1)} %get-tuple-element.27.kv_here), channel_id=1, source_target_pairs={{0,4},{1,5},{2,6},{3,7},{4,8},{5,9},{6,10},{7,11},{8,12},{9,13},{1... | collective-permute-start | bytes 786440 | tf_op jit(solution)/shard_map/ppermute | solution.py:302
  12.9 17.7 %collective-permute-start.4 = (bf16[256,512]{1,0:T(8,128)(2,1)S(1)}, bf16[256,512]{1,0:T(8,128)(2,1)S(1)}, u32[]{:S(2)}, u32[]{:S(2)}) collective-permute-start(bf16[256,512]{1,0:T(8,128)(2,1)S(1)} %get-tuple-element.27.kv_here), channel_id=1, source_target_pairs={{0,2},{1,3},{2,4},{3,5},{4,6},{5,7},{6,8},{7,9},{8,10},{9,11},{10,... | collective-permute-start | bytes 786440 | tf_op jit(solution)/shard_map/ppermute | solution.py:302
  17.6 10.5 %all-to-all-start = ((bf16[8,2,1024]{2,1,0:T(2,128)(2,1)}), bf16[8,2,1024]{2,1,0:T(2,128)(2,1)S(1)}, u32[]{:S(2)}, u32[]{:S(2)}) async-start(bf16[8,2,1024]{2,1,0:T(2,128)(2,1)} %broadcast_in_dim.2), calls=%async_computation | async-start | bytes 65536 | tf_op jit(solution)/shard_map/all_to_all | solution.py:306
  21.5 20.6 %collective-permute-start.7 = (bf16[256,512]{1,0:T(8,128)(2,1)S(1)}, bf16[256,512]{1,0:T(8,128)(2,1)S(1)}, u32[]{:S(2)}, u32[]{:S(2)}) collective-permute-start(bf16[256,512]{1,0:T(8,128)(2,1)S(1)} %get-tuple-element.30.kv_here), channel_id=1, source_target_pairs={{0,4},{1,5},{2,6},{3,7},{4,8},{5,9},{6,10},{7,11},{8,12},{9,13},{1... | collective-permute-start | bytes 786440 | tf_op jit(solution)/shard_map/ppermute | solution.py:302
  28.2 13.9 %collective-permute-start.6 = (bf16[256,512]{1,0:T(8,128)(2,1)S(1)}, bf16[256,512]{1,0:T(8,128)(2,1)S(1)}, u32[]{:S(2)}, u32[]{:S(2)}) collective-permute-start(bf16[256,512]{1,0:T(8,128)(2,1)S(1)} %get-tuple-element.30.kv_here), channel_id=1, source_target_pairs={{0,2},{1,3},{2,4},{3,5},{4,6},{5,7},{6,8},{7,9},{8,10},{9,11},{10,... | collective-permute-start | bytes 786440 | tf_op jit(solution)/shard_map/ppermute | solution.py:302
  30.7 1.2 %copy-start.4 = (bf16[128,4096]{1,0:T(8,128)(2,1)S(1)}, bf16[128,4096]{1,0:T(8,128)(2,1)}, u32[]{:S(2)}) copy-start(bf16[128,4096]{1,0:T(8,128)(2,1)} %o_own.3) | copy-start | bytes 3145732
  42.1 1.0 %copy-start.6 = (bf16[256,512]{1,0:T(8,128)(2,1)S(1)}, bf16[256,512]{1,0:T(8,128)(2,1)}, u32[]{:S(2)}) copy-start(bf16[256,512]{1,0:T(8,128)(2,1)} %copy-done.5) | copy-start | bytes 786436
  52.6 8.4 %collective-permute-start.13 = (bf16[256,512]{1,0:T(8,128)(2,1)S(1)}, bf16[256,512]{1,0:T(8,128)(2,1)S(1)}, u32[]{:S(2)}, u32[]{:S(2)}) collective-permute-start(bf16[256,512]{1,0:T(8,128)(2,1)S(1)} %get-tuple-element.42), channel_id=1, source_target_pairs={{2,0},{3,1},{4,2},{5,3},{6,4},{7,5},{8,6},{9,7},{10,8},{11,9},{12,... | collective-permute-start | bytes 786440 | tf_op jit(solution)/shard_map/ppermute | solution.py:302
  53.9 4.0 %collective-permute-start.16 = (f32[16,128]{1,0:T(8,128)S(1)}, f32[16,128]{1,0:T(8,128)S(1)}, u32[]{:S(2)}, u32[]{:S(2)}) collective-permute-start(f32[16,128]{1,0:T(8,128)S(1)} %get-tuple-element.51), channel_id=1, source_target_pairs={{0,1},{1,0},{2,3},{3,2},{4,5},{5,4},{6,7},{7,6},{8,9},{9,8},{10,11... | collective-permute-start | bytes 24584 | tf_op jit(solution)/shard_map/ppermute | solution.py:299
  54.0 27.8 %collective-permute-start.14 = (bf16[256,512]{1,0:T(8,128)(2,1)}, bf16[256,512]{1,0:T(8,128)(2,1)S(1)}, u32[]{:S(2)}, u32[]{:S(2)}) collective-permute-start(bf16[256,512]{1,0:T(8,128)(2,1)} %get-tuple-element.43), channel_id=1, source_target_pairs={{4,0},{5,1},{6,2},{7,3},{8,4},{9,5},{10,6},{11,7},{12,8},{13,9},{1... | collective-permute-start | bytes 786440 | tf_op jit(solution)/shard_map/ppermute | solution.py:302
  55.3 26.7 %collective-permute-start.10 = (bf16[256,512]{1,0:T(8,128)(2,1)}, bf16[256,512]{1,0:T(8,128)(2,1)S(1)}, u32[]{:S(2)}, u32[]{:S(2)}) collective-permute-start(bf16[256,512]{1,0:T(8,128)(2,1)} %get-tuple-element.35), channel_id=1, source_target_pairs={{2,0},{3,1},{4,2},{5,3},{6,4},{7,5},{8,6},{9,7},{10,8},{11,9},{12,... | collective-permute-start | bytes 786440 | tf_op jit(solution)/shard_map/ppermute | solution.py:302
  56.6 25.4 %collective-permute-start.11 = (bf16[256,512]{1,0:T(8,128)(2,1)}, bf16[256,512]{1,0:T(8,128)(2,1)S(1)}, u32[]{:S(2)}, u32[]{:S(2)}) collective-permute-start(bf16[256,512]{1,0:T(8,128)(2,1)} %get-tuple-element.36), channel_id=1, source_target_pairs={{4,0},{5,1},{6,2},{7,3},{8,4},{9,5},{10,6},{11,7},{12,8},{13,9},{1... | collective-permute-start | bytes 786440 | tf_op jit(solution)/shard_map/ppermute | solution.py:302
  57.9 24.7 %collective-permute-start.9 = (bf16[128,1024]{1,0:T(8,128)(2,1)}, bf16[128,1024]{1,0:T(8,128)(2,1)}, u32[]{:S(2)}, u32[]{:S(2)}) collective-permute-start(bf16[128,1024]{1,0:T(8,128)(2,1)} %get-tuple-element.33), channel_id=1, source_target_pairs={{0,1},{1,0},{2,3},{3,2},{4,5},{5,4},{6,7},{7,6},{8,9},{9,8},{10,11... | collective-permute-start | bytes 786440 | tf_op jit(solution)/shard_map/ppermute | solution.py:299
  61.0 21.7 %collective-permute-start.8 = (bf16[128,1024]{1,0:T(8,128)(2,1)S(1)}, bf16[128,1024]{1,0:T(8,128)(2,1)}, u32[]{:S(2)}, u32[]{:S(2)}) collective-permute-start(bf16[128,1024]{1,0:T(8,128)(2,1)S(1)} %get-tuple-element.32), channel_id=1, source_target_pairs={{0,1},{1,0},{2,3},{3,2},{4,5},{5,4},{6,7},{7,6},{8,9},{9,8},{10,11... | collective-permute-start | bytes 786440 | tf_op jit(solution)/shard_map/ppermute | solution.py:299
  61.7 20.1 %all-to-all-start.1 = ((f32[8,2,1024]{2,1,0:T(2,128)}), f32[8,2,1024]{2,1,0:T(2,128)S(1)}, u32[]{:S(2)}, u32[]{:S(2)}) async-start(f32[8,2,1024]{2,1,0:T(2,128)} %reshape.16), calls=%async_computation.1 | async-start | bytes 131072 | tf_op jit(solution)/shard_map/all_to_all | solution.py:306
  81.9 3.2 %collective-permute-start.15 = (bf16[128,512]{1,0:T(8,128)(2,1)S(1)}, bf16[128,512]{1,0:T(8,128)(2,1)S(1)}, u32[]{:S(2)}, u32[]{:S(2)}) collective-permute-start(bf16[128,512]{1,0:T(8,128)(2,1)S(1)} %get-tuple-element.45), channel_id=1, source_target_pairs={{0,1},{1,0},{2,3},{3,2},{4,5},{5,4},{6,7},{7,6},{8,9},{9,8},{10,11... | collective-permute-start | bytes 393224 | tf_op jit(solution)/shard_map/ppermute | solution.py:299
  82.1 3.0 %collective-permute-start.12 = (bf16[128,512]{1,0:T(8,128)(2,1)S(1)}, bf16[128,512]{1,0:T(8,128)(2,1)S(1)}, u32[]{:S(2)}, u32[]{:S(2)}) collective-permute-start(bf16[128,512]{1,0:T(8,128)(2,1)S(1)} %get-tuple-element.40), channel_id=1, source_target_pairs={{0,1},{1,0},{2,3},{3,2},{4,5},{5,4},{6,7},{7,6},{8,9},{9,8},{10,11... | collective-permute-start | bytes 393224 | tf_op jit(solution)/shard_map/ppermute | solution.py:299
  (4 other events, 3.6 us)

commit v3 on v2

v3 whole, which is shorter than its diff:
```python
import functools
import math

import jax
import jax.numpy as jnp
from jax import lax
from jax.experimental import pallas as pl
from jax.experimental.pallas import tpu as pltpu
from jax.sharding import PartitionSpec as P

HEAD_SIZE = 128
W = 512
STRIDE = 128
CHUNKS = 2

NEG_FILL = -1e30
SCALE = 1.0 / math.sqrt(HEAD_SIZE)


def vmem_shape(shape, dtype):
    return pltpu.VMEM(shape, dtype)


def in_hbm(*arrays):
    return [pltpu.with_memory_space_constraint(x, pltpu.HBM) for x in arrays]


def in_vmem(*arrays):
    return [pltpu.with_memory_space_constraint(x, pltpu.VMEM) for x in arrays]


def head_columns(which, width=HEAD_SIZE):
    return pl.ds(pl.multiple_of(which * width, width), width)


def pair_position():
    index = lax.axis_index("ctx")
    return index & 1, index >> 1


def dot_nt(left, right):
    return lax.dot_general(
        left, right, (((1,), (1,)), ((), ())), preferred_element_type=jnp.float32
    )


def dot_nn(left, right):
    return lax.dot_general(
        left, right, (((1,), (0,)), ((), ())), preferred_element_type=jnp.float32
    )


def dot_tn(left, right):
    return lax.dot_general(
        left, right, (((0,), (0,)), ((), ())), preferred_element_type=jnp.float32
    )


def attention_kernel(
    chunk,
    q_own,
    q_other,
    o_own,
    o_other,
    kv_here_in,
    kv_near,
    kv_past,
    kv_far,
    dq_own,
    dq_other,
    norm,
    g_here,
    g_near,
    g_past,
    g_far,
    q_held,
    o_held,
    here_held,
    here_done,
    held_done,
):
    half = q_own.shape[0]
    rows = 2 * half
    far_rows = kv_far.shape[0]
    both = 2 * HEAD_SIZE
    count = kv_near.shape[1] // both
    width = dq_own.shape[1]
    heads = width // (count * HEAD_SIZE)
    core, pair = pair_position()
    here = here_held
    loads = []
    for at in range(count):
        columns = slice(at * both, (at + 1) * both)
        first = core * (count * CHUNKS) + chunk * count + at
        for side in range(2):
            batch = []
            if side == 0:
                batch.append(
                    pltpu.make_async_copy(
                        kv_here_in.at[:, columns], here_held.at[:, columns], here_done.at[at]
                    )
                )
            for which in range(2):
                source = (q_own, q_other, o_own, o_other)[2 * which + side]
                batch.append(
                    pltpu.make_async_copy(
                        source.at[:, head_columns(first, heads * HEAD_SIZE)],
                        (q_held, o_held)[which].at[at, side],
                        held_done.at[at, side, which],
                    )
                )
            loads.append(batch)
    for copy in sum(loads, []):
        copy.start()
    wide = (half, rows)
    lane = lax.broadcasted_iota(jnp.int32, wide, 1) % half
    lower = lax.broadcasted_iota(jnp.int32, wide, 0) <= lane
    far_at = lax.broadcasted_iota(jnp.int32, (far_rows, rows), 0)
    far_lane = lax.broadcasted_iota(jnp.int32, (far_rows, rows), 1) % half
    far_token = far_at * half
    near_bias = jnp.where(pair >= 1, 0.0, NEG_FILL)
    past_bias = jnp.where(pair >= 2, 0.0, NEG_FILL)
    sides = []
    for side in range(2):
        later = core if side == 0 else 1 - core
        sides.append(
            (
                later,
                far_token <= pair * rows + later * half + far_lane - W,
                jnp.where(later == 0, past_bias, 0.0),
            )
        )

    def keys_of(at, side, which):
        columns = slice((2 * at + which) * HEAD_SIZE, (2 * at + which + 1) * HEAD_SIZE)
        far_row = 2 * (chunk * count + at) + which
        same = slice(side * half, (side + 1) * half)
        cross = slice((1 - side) * half, (2 - side) * half)
        full = jnp.where(sides[side][0] == 1, here[cross, columns], kv_past[cross, columns])
        return jnp.concatenate(
            [
                here[same, columns],
                kv_past[same, columns],
                full,
                kv_near[:, columns],
                kv_far[:, far_row, :],
            ],
            axis=0,
        )

    def operands(at, side, first):
        query, grad = (
            jnp.concatenate(
                [
                    held[at, side, :, (first + k) * HEAD_SIZE : (first + k + 1) * HEAD_SIZE]
                    for k in range(2)
                ],
                axis=0,
            )
            for held in (q_held, o_held)
        )
        key_all, value_all = keys_of(at, side, 0), keys_of(at, side, 1)
        return query, grad, key_all, dot_nt(key_all, query), dot_nt(value_all, grad)

    def merged(whole, bias):
        edge = jnp.where(lower, whole[:half], whole[half:rows] + bias)
        return edge, whole[rows : rows + half], whole[rows + half : 2 * rows + half]

    def reduced(op, parts):
        out = [op(part, axis=0, keepdims=True) for part in parts]
        return out

    def weights(at, side, first, score, dprob):
        _, far_open, full_bias = sides[side]
        edge, full, near = merged(score, past_bias)
        parts = [
            edge,
            full + full_bias,
            near + near_bias,
            jnp.where(far_open, score[2 * rows + half :], NEG_FILL),
        ]
        top = functools.reduce(jnp.maximum, reduced(jnp.max, parts))
        parts = [jnp.exp2((part - top) * (SCALE * math.log2(math.e))) for part in parts]
        total = sum(reduced(jnp.sum, parts))
        log_total = top * SCALE + jnp.log(total)
        for k in range(2):
            row = at * heads + first + k
            norm[row : row + 1, side * half : (side + 1) * half] = log_total[
                :, k * half : (k + 1) * half
            ]
        inverse = 1.0 / total
        parts = [part * inverse for part in parts]
        d_parts = [*merged(dprob, 0.0), dprob[2 * rows + half :]]
        delta = sum(reduced(jnp.sum, [part * d_part for part, d_part in zip(parts, d_parts)]))
        d_parts = [part * (d_part - delta) for part, d_part in zip(parts, d_parts)]

        def split(edge, *others):
            return jnp.concatenate(
                [
                    jnp.where(lower, edge, 0.0).astype(jnp.bfloat16),
                    jnp.where(lower, 0.0, edge).astype(jnp.bfloat16),
                    *(part.astype(jnp.bfloat16) for part in others),
                ],
                axis=0,
            )

        return split(*parts), split(*d_parts)

    steps = [
        (at, side, first)
        for at in range(count)
        for side in range(2)
        for first in range(0, heads, 2)
    ]
    for copy in sum(loads, []):
        copy.wait()
    following = operands(*steps[0])
    terms = {}
    for number, (at, side, first) in enumerate(steps):
        query, grad, key_all, score, dprob = following
        if number + 1 < len(steps):
            following = operands(*steps[number + 1])
        prob, dscore = weights(at, side, first, score, dprob)
        new = (dot_nn(dscore, query), dot_nn(prob, grad))
        terms[side] = new if first == 0 else tuple(a + b for a, b in zip(terms[side], new))
        query_term = (dot_tn(key_all, dscore) * SCALE).T.astype(jnp.bfloat16)
        dq_side = dq_own if side == 0 else dq_other
        for k in range(2):
            columns = slice(
                (at * heads + first + k) * HEAD_SIZE, (at * heads + first + k + 1) * HEAD_SIZE
            )
            dq_side[:, columns] = query_term[k * half : (k + 1) * half]
        if side == 1 and first + 2 == heads:
            for which in range(2):
                scale = SCALE if which == 0 else 1.0
                columns = slice((2 * at + which) * HEAD_SIZE, (2 * at + which + 1) * HEAD_SIZE)
                own, other = (terms[k][which] * scale for k in range(2))
                for k, (mine, theirs) in enumerate(((own, other), (other, own))):
                    cross = theirs[rows : rows + half]
                    here_too = sides[1 - k][0] == 1
                    place = slice(k * half, (k + 1) * half)
                    g_here[place, columns] = mine[:half] + jnp.where(here_too, cross, 0.0)
                    g_past[place, columns] = (
                        mine[half:rows] + jnp.where(here_too, 0.0, cross)
                    ).astype(jnp.bfloat16)
                joint = own[rows + half :] + other[rows + half :]
                g_near[:, columns] = joint[:rows].astype(jnp.bfloat16)
                g_far[:, columns] = joint[rows:]


def attention(queries, q_other, grad_out, o_other, kv_here, kv_near, kv_past, kv_far, chunk):
    half = queries.shape[0]
    rows = 2 * half
    far_rows = kv_far.shape[0]
    both = 2 * HEAD_SIZE
    count = kv_here.shape[1] // both
    per_core = count * CHUNKS
    group_width = queries.shape[1] // (2 * per_core)
    heads = group_width // HEAD_SIZE

    whole = pl.BlockSpec(memory_space=pltpu.VMEM)
    keys_seen = 3 * rows + far_rows
    return pl.pallas_call(
        functools.partial(attention_kernel, chunk),
        name=f"attention_{chunk}",
        in_specs=[pl.BlockSpec(memory_space=pl.ANY)] * 5 + [whole] * 3,
        out_specs=[whole] * 7,
        out_shape=[
            vmem_shape((half, count * group_width), jnp.bfloat16),
            vmem_shape((half, count * group_width), jnp.bfloat16),
            vmem_shape((count * heads, rows), jnp.float32),
            vmem_shape((rows, count * both), jnp.float32),
            vmem_shape((rows, count * both), jnp.bfloat16),
            vmem_shape((rows, count * both), jnp.bfloat16),
            vmem_shape((far_rows, count * both), jnp.float32),
        ],
        scratch_shapes=[
            pltpu.VMEM((count, 2, half, group_width), jnp.bfloat16),
            pltpu.VMEM((count, 2, half, group_width), jnp.bfloat16),
            pltpu.VMEM((rows, count * both), jnp.bfloat16),
            pltpu.SemaphoreType.DMA((count,)),
            pltpu.SemaphoreType.DMA((count, 2, 2)),
        ],
        compiler_params=pltpu.CompilerParams(vmem_limit_bytes=20 * 1024 * 1024),
        cost_estimate=pl.CostEstimate(
            flops=count * heads * rows * keys_seen * HEAD_SIZE * 20,
            transcendentals=count * heads * rows * keys_seen,
            bytes_accessed=count * (6 * half * group_width * 2 + 5 * rows * both * 4),
        ),
    )(
        *in_hbm(queries, q_other, grad_out, o_other, kv_here), *in_vmem(kv_near, kv_past, kv_far)
    )


def arrange_kernel(keys, values, k_other, v_other, *outs):
    half = keys.shape[0]
    payloads = outs
    core, _ = pair_position()
    count = payloads[0].shape[1] // (2 * HEAD_SIZE)
    for chunk, payload in enumerate(payloads):
        for h in range(count):
            source = head_columns(core * (count * CHUNKS) + chunk * count + h)
            for side, (mine, theirs) in enumerate(((keys, k_other), (values, v_other))):
                to = slice((2 * h + side) * HEAD_SIZE, (2 * h + side + 1) * HEAD_SIZE)
                payload[:half, to] = mine[:, source]
                payload[half:, to] = theirs[:, source]


def own_rows_kernel(keys, values, out):
    per_core = out.shape[1] // 2
    for core in range(2):
        rows = []
        for h in range(core * per_core, (core + 1) * per_core):
            columns = slice(h * HEAD_SIZE, (h + 1) * HEAD_SIZE)
            rows += [keys[0:1, columns], values[0:1, columns]]
        block = jnp.concatenate([row.astype(jnp.float32) for row in rows], axis=0)
        for peer in range(core, out.shape[0], 2):
            out[peer] = block.astype(out.dtype)


def own_rows(keys, values, peers):
    kv_width = keys.shape[1]
    head = pl.BlockSpec((16, kv_width), lambda i: (0, 0))
    shape = (peers, kv_width // HEAD_SIZE, HEAD_SIZE)
    return pl.pallas_call(
        own_rows_kernel,
        name="own_rows",
        grid=(1,),
        in_specs=[head, head],
        out_specs=pl.BlockSpec(shape, lambda i: (0, 0, 0)),
        out_shape=jax.ShapeDtypeStruct(shape, keys.dtype),
    )(keys, values)


def arrange(keys, values, k_other, v_other):
    half, kv_width = keys.shape
    whole = pl.BlockSpec(memory_space=pltpu.VMEM)
    payload = pltpu.HBM((2 * half, kv_width // CHUNKS), keys.dtype)
    return pl.pallas_call(
        arrange_kernel,
        name="arrange",
        grid=(1,),
        in_specs=[pl.BlockSpec(keys.shape, lambda i: (0, 0))] * 2 + [whole] * 2,
        out_specs=[whole] * CHUNKS,
        out_shape=[payload] * CHUNKS,
    )(keys, values, *in_vmem(k_other, v_other))


def collect_kernel(chunk, here, near, past, strided, mine, theirs):
    half, width = mine.shape
    core, _ = pair_position()
    extra = jnp.sum(strided[:, :, chunk * width : (chunk + 1) * width], axis=0)
    extra = jnp.where(core == 0, extra, jnp.concatenate([extra[1:2], extra[0:1]], axis=0))
    total = here[...] + near[...].astype(jnp.float32) + past[...].astype(jnp.float32)
    row = lax.broadcasted_iota(jnp.int32, (half, 1), 0)
    mine[...] = (total[:half] + jnp.where(row == 0, extra[0:1], 0.0)).astype(mine.dtype)
    theirs[...] = (total[half:] + jnp.where(row == 0, extra[1:2], 0.0)).astype(theirs.dtype)


def collect(here, near, past, strided, chunk):
    rows, width = here.shape
    half = vmem_shape((rows // 2, width), jnp.bfloat16)
    whole = pl.BlockSpec(memory_space=pltpu.VMEM)
    return pl.pallas_call(
        functools.partial(collect_kernel, chunk),
        name=f"collect_{chunk}",
        in_specs=[whole] * 4,
        out_specs=[whole, whole],
        out_shape=[half, half],
        cost_estimate=pl.CostEstimate(
            flops=rows * width * 4, transcendentals=0, bytes_accessed=rows * width * 10
        ),
    )(*in_vmem(here, near, past, strided))


def place_kernel(*refs):
    here, _ = pair_position()
    *parts, grad_keys, grad_values = refs
    count = parts[0].shape[1] // (2 * HEAD_SIZE)
    for chunk in range(CHUNKS):
        mine, theirs = parts[2 * chunk : 2 * chunk + 2]
        for h in range(count):
            at = chunk * count + h
            for core, block in ((here, mine), (1 - here, theirs)):
                to = head_columns(core * (count * CHUNKS) + at)
                grad_keys[:, to] = block[:, 2 * h * HEAD_SIZE : (2 * h + 1) * HEAD_SIZE]
                grad_values[:, to] = block[:, (2 * h + 1) * HEAD_SIZE : (2 * h + 2) * HEAD_SIZE]


def placed_grads(parts, half, kv_width):
    whole = pl.BlockSpec(memory_space=pltpu.VMEM)
    out = jax.ShapeDtypeStruct((half, kv_width), jnp.bfloat16)
    return pl.pallas_call(
        place_kernel,
        name="place",
        in_specs=[whole] * len(parts),
        out_specs=[whole, whole],
        out_shape=[out, out],
    )(*in_vmem(*parts))


def local(queries, keys, values, grad_out):
    half, kv_width = keys.shape
    kv_heads = kv_width // HEAD_SIZE
    rows = 2 * half
    peers = lax.axis_size("ctx")
    pairs = peers // 2
    assert half == STRIDE and W == 2 * rows and peers % 2 == 0 and kv_heads % (2 * CHUNKS) == 0
    core, _ = pair_position()

    def swap(x):
        return lax.ppermute(x, "ctx", [(i, i ^ 1) for i in range(peers)])

    def shifted(x, by):
        return lax.ppermute(x, "ctx", [(i, (i + by) % peers) for i in range(peers)])

    def exchanged(x):
        groups = [list(range(parity, peers, 2)) for parity in range(2)]
        return lax.all_to_all(x, "ctx", 0, 0, axis_index_groups=groups)

    def joined(mine, theirs):
        return jnp.where(
            core == 0,
            jnp.concatenate([mine, theirs], axis=1),
            jnp.concatenate([theirs, mine], axis=1),
        )

    far = lax.all_to_all(own_rows(keys, values, peers), "ctx", 0, 0, tiled=True)
    here = arrange(keys, values, swap(keys), swap(values))
    near, past = [], []
    for chunk in range(CHUNKS):
        payload = here[chunk]
        if chunk > 0:
            payload, _ = lax.optimization_barrier((payload, far))
        near.append(shifted(payload, 2))
        past.append(shifted(payload, 4))
    q_sent, o_sent, _ = lax.optimization_barrier((queries, grad_out, here[0]))
    q_other, o_other = swap(q_sent), swap(o_sent)

    dq_own, dq_other, norms, sums, far_terms = [], [], [], [], []
    for chunk in range(CHUNKS):
        out = attention(
            queries,
            q_other,
            grad_out,
            o_other,
            here[chunk],
            near[chunk],
            past[chunk],
            far,
            chunk,
        )
        sums.append((out[3], shifted(out[4], -2), shifted(out[5], -4)))
        dq_own.append(out[0])
        dq_other.append(swap(out[1]))
        norms.append(out[2])
        far, _ = lax.optimization_barrier((far, out[2]))
        far_terms.append(out[6])

    strided_terms = exchanged(jnp.concatenate(far_terms, axis=1).reshape(pairs, 2, kv_width))
    grad_queries = joined(jnp.concatenate(dq_own, axis=1), jnp.concatenate(dq_other, axis=1))
    norm = jnp.concatenate(norms, axis=0)
    log_norm = joined(norm[:, :half].T, swap(norm[:, half:]).T)
    parts = []
    for chunk, (own, near_terms, past_terms) in enumerate(sums):
        if chunk > 0:
            own, grad_queries, log_norm, _ = lax.optimization_barrier(
                (own, grad_queries, log_norm, parts[-2])
            )
        mine, theirs = collect(own, near_terms, past_terms, strided_terms, chunk)
        parts += [mine, swap(theirs)]
    grad_keys, grad_values = placed_grads(parts, half, kv_width)
    return (grad_queries, grad_keys, grad_values, log_norm)


def solution(mesh):
    placed = P(("groups", "ctx"), "head")
    return jax.shard_map(
        local,
        mesh=mesh,
        in_specs=(placed,) * 4,
        out_specs=(placed,) * 4,
        check_vma=False,
    )
```

time: 87.4 us -> 71.8 us (0.82)
  blocking collectives: 0 us -> 13.1 us
  starting transfers between devices: 34.4 us -> 25.3 us
  waiting for transfers between devices: 19.1 us -> 10.8 us
  local copies, waits for them, and re-layouts: 7.05 us -> 0.68 us
  Pallas kernels: 21.5 us -> 17.8 us
    all_to_all x0 -> x1, blocking collectives: none -> 13.1 us  [local(): far = lax.all_to_all(own_rows(keys, values, peers), 'ctx', 0, 0, tiled=True)]
    all_to_all x2 -> x1, waiting for transfers between devices: 13.8 us -> 1.29 us  [exchanged(): return lax.all_to_all(x, 'ctx', 0, 0, axis_index_groups=groups)]
    all_to_all x2 -> x1, starting transfers between devices: 12.3 us -> 6.44 us  [exchanged(): return lax.all_to_all(x, 'ctx', 0, 0, axis_index_groups=groups)]
    unnamed x19 -> x3, local copies, waits for them, and re-layouts: 5.73 us -> 0.01 us
    pallas_call x2, Pallas kernels: 18.8 us -> 13.3 us  [attention(): pl.pallas_call(functools.partial(attention_kernel, chunk), name=f'attenti...]
    ppermute x8, waiting for transfers between devices: 2.53 us -> 6.84 us  [shifted(): return lax.ppermute(x, 'ctx', [(i, (i + by) % peers) for i in range(peers)])]
    ppermute x8, starting transfers between devices: 19.8 us -> 16.5 us  [shifted(): return lax.ppermute(x, 'ctx', [(i, (i + by) % peers) for i in range(peers)])]
    pallas_call x2 -> x3, Pallas kernels: 2.55 us -> 4.29 us  [the longest x1 1.95 us: arrange(): pl.pallas_call(arrange_kernel, name='arrange', grid=(1,), in_specs=[pl.Bl...]
  transfers between devices with their start and end apart: 19 -> 18, of which waited for: 5 -> 7; matrix products, arithmetic and copies ran while one was open for 6% -> 5% of each run, Pallas kernels for 12% -> 21%
where the time goes in v3:
time: 71.8 us; the launch traced here: 71.4 us
  starting transfers between devices  25.3 us (35%)
  Pallas kernels  17.8 us (25%)
  blocking collectives  13.1 us (18%)
  waiting for transfers between devices  10.8 us (15%)
  other arithmetic  3.02 us (4%)
  between operations  0.72 us (1%)
    ppermute x8, starting transfers between devices, shifted(): return lax.ppermute(x, 'ctx', [(i, (i + by) % peers) for i in range(peers)])  16.5 us
    pallas_call x2, Pallas kernels, attention(): pl.pallas_call(functools.partial(attention_kernel, chunk), name=f'attenti...  13.3 us
    all_to_all x1, blocking collectives, local(): far = lax.all_to_all(own_rows(keys, values, peers), 'ctx', 0, 0, tiled=True)  13.1 us
    ppermute x8, waiting for transfers between devices, shifted(): return lax.ppermute(x, 'ctx', [(i, (i + by) % peers) for i in range(peers)])  6.84 us
    all_to_all x1, starting transfers between devices, exchanged(): return lax.all_to_all(x, 'ctx', 0, 0, axis_index_groups=groups)  6.44 us
    select_n x2, other arithmetic, joined(): jnp.where(core == 0, jnp.concatenate([mine, theirs], axis=1), jnp.concate...  3.01 us
    ppermute x9, waiting for transfers between devices, swap(): return lax.ppermute(x, 'ctx', [(i, i ^ 1) for i in range(peers)])  2.7 us
    ppermute x9, starting transfers between devices, swap(): return lax.ppermute(x, 'ctx', [(i, i ^ 1) for i in range(peers)])  2.32 us
  transfers between devices with their start and end apart: 18, of which 7 were waited for; matrix products, arithmetic and copies ran while one was open for 5% of the time, Pallas kernels for 21%

profile of v3, /device:TPU:0, one launch (start us, length us, event | category | flops | bytes accessed | tf_op | source)
XLA Modules:
  0.0 71.4 jit_solution(7905087538587023928)
XLA Ops:
  0.6 0.5 collective-permute-start
  1.2 1.3 %collective-permute-done.k_other = bf16[128,1024]{1,0:T(8,128)(2,1)S(1)} collective-permute-done((bf16[128,1024]{1,0:T(8,128)(2,1)}, bf16[128,1024]{1,0:T(8,128)(2,1)S(1)}, u32[]{:S(2)}, u32[]{:S(2)}) %collective-permute-start) | collective-permute-done | bytes 262176 | tf_op jit(solution)/shard_map/ppermute | solution.py:412
  2.9 2.0 %arrange.1 = (bf16[256,512]{1,0:T(8,128)(2,1)}, bf16[256,512]{1,0:T(8,128)(2,1)}) custom-call(bf16[128,1024]{1,0:T(8,128)(2,1)} %keys.3, bf16[128,1024]{1,0:T(8,128)(2,1)} %values.3, bf16[128,1024]{1,0:T(8,128)(2,1)S(1)} %collective-permute-done.k_other, bf16[128,1024]{1,0:T(8,128)(2,1)S(1)} %collective-permute-done.1.v_other), custom_call_target="tpu_custom_call" | custom-call | tf_op jit(solution)/shard_map/arrange/pallas_call | solution.py:339
  5.4 2.9 %collective-permute-start.6 = (bf16[256,512]{1,0:T(8,128)(2,1)}, bf16[256,512]{1,0:T(8,128)(2,1)S(1)}, u32[]{:S(2)}, u32[]{:S(2)}) collective-permute-start(bf16[256,512]{1,0:T(8,128)(2,1)} %get-tuple-element.33.kv_here_in), channel_id=1, source_target_pairs={{0,2},{1,3},{2,4},{3,5},{4,6},{5,7},{6,8},{7,9},{8,10},{9,11},{10,... | collective-permute-start | bytes 786440 | tf_op jit(solution)/shard_map/ppermute | solution.py:415
  8.2 1.6 %collective-permute-start.7 = (bf16[256,512]{1,0:T(8,128)(2,1)}, bf16[256,512]{1,0:T(8,128)(2,1)S(1)}, u32[]{:S(2)}, u32[]{:S(2)}) collective-permute-start(bf16[256,512]{1,0:T(8,128)(2,1)} %get-tuple-element.33.kv_here_in), channel_id=1, source_target_pairs={{0,4},{1,5},{2,6},{3,7},{4,8},{5,9},{6,10},{7,11},{8,12},{9,13},{1... | collective-permute-start | bytes 786440 | tf_op jit(solution)/shard_map/ppermute | solution.py:415
  9.8 1.4 %own_rows.1 = bf16[16,8,128]{2,1,0:T(8,128)(2,1)} custom-call(bf16[128,1024]{1,0:T(8,128)(2,1)} %keys.3, bf16[128,1024]{1,0:T(8,128)(2,1)} %values.3), custom_call_target="tpu_custom_call" | custom-call | tf_op jit(solution)/shard_map/own_rows/pallas_call | solution.py:325
  11.2 13.1 %all_to_all.10.kv_far = bf16[16,8,128]{2,1,0:T(8,128)(2,1)S(1)} all-to-all(bf16[16,8,128]{2,1,0:T(8,128)(2,1)} %own_rows.1), channel_id=1, replica_groups=mesh['groups'=2,'ctx'=16,'head'=1] {'ctx'}, dimensions={0} | all-to-all | bytes 65536 | tf_op jit(solution)/shard_map/all_to_all | solution.py:428
  24.3 0.5 collective-permute-start.4
  24.8 0.7 collective-permute-start.5
  25.5 6.3 %attention_0.1 = (bf16[128,1024]{1,0:T(8,128)(2,1)S(1)}, bf16[128,1024]{1,0:T(8,128)(2,1)S(1)}, f32[8,256]{1,0:T(8,128)S(1)}, f32[256,512]{1,0:T(8,128)S(1)}, bf...) custom-call(bf16[128,4096]{1,0:T(8,128)(2,1)} %q_own.3, ...), custom_call_target="tpu_custom_call" | custom-call | flops 4110417920 | bytes 4194304 | tf_op jit(solution)/shard_map/attention_0/pallas_call | solution.py:263
  31.8 4.2 %collective-permute-start.11 = (bf16[256,512]{1,0:T(8,128)(2,1)S(1)}, bf16[256,512]{1,0:T(8,128)(2,1)S(1)}, u32[]{:S(2)}, u32[]{:S(2)}) collective-permute-start(bf16[256,512]{1,0:T(8,128)(2,1)S(1)} %get-tuple-element.47), channel_id=1, source_target_pairs={{0,14},{1,15},{2,0},{3,1},{4,2},{5,3},{6,4},{7,5},{8,6},{9,7},{10,... | collective-permute-start | bytes 786440 | tf_op jit(solution)/shard_map/ppermute | solution.py:415
  36.0 1.4 %collective-permute-start.12 = (bf16[256,512]{1,0:T(8,128)(2,1)S(1)}, bf16[256,512]{1,0:T(8,128)(2,1)S(1)}, u32[]{:S(2)}, u32[]{:S(2)}) collective-permute-start(bf16[256,512]{1,0:T(8,128)(2,1)S(1)} %get-tuple-element.48), channel_id=1, source_target_pairs={{0,12},{1,13},{2,14},{3,15},{4,0},{5,1},{6,2},{7,3},{8,4},{9,5},{1... | collective-permute-start | bytes 786440 | tf_op jit(solution)/shard_map/ppermute | solution.py:415
  37.4 7.0 %attention_1.1 = (bf16[128,1024]{1,0:T(8,128)(2,1)S(1)}, bf16[128,1024]{1,0:T(8,128)(2,1)}, f32[8,256]{1,0:T(8,128)S(1)}, f32[256,512]{1,0:T(8,128)S(1)}, bf16[2...) custom-call(bf16[128,4096]{1,0:T(8,128)(2,1)} %q_own.3, ...), custom_call_target="tpu_custom_call" | custom-call | flops 4110417920 | bytes 4194304 | tf_op jit(solution)/shard_map/attention_1/pallas_call | solution.py:263
  45.1 0.7 reshape.11
  45.7 6.4 %all-to-all-start.1 = ((f32[8,2,1024]{2,1,0:T(2,128)}), f32[8,2,1024]{2,1,0:T(2,128)S(1)}, u32[]{:S(2)}, u32[]{:S(2)}) async-start(f32[8,2,1024]{2,1,0:T(2,128)} %reshape.11), calls=%async_computation.1 | async-start | bytes 131072 | tf_op jit(solution)/shard_map/all_to_all | solution.py:419
  52.2 4.7 %collective-permute-start.14 = (bf16[256,512]{1,0:T(8,128)(2,1)}, bf16[256,512]{1,0:T(8,128)(2,1)S(1)}, u32[]{:S(2)}, u32[]{:S(2)}) collective-permute-start(bf16[256,512]{1,0:T(8,128)(2,1)} %get-tuple-element.55), channel_id=1, source_target_pairs={{0,14},{1,15},{2,0},{3,1},{4,2},{5,3},{6,4},{7,5},{8,6},{9,7},{10,... | collective-permute-start | bytes 786440 | tf_op jit(solution)/shard_map/ppermute | solution.py:415
  56.9 0.6 maximum_select_fusion.1
  57.5 0.6 collective-permute-start.15
  58.1 1.3 %all-to-all-done.1.strided = f32[8,2,1024]{2,1,0:T(2,128)S(1)} async-done(((f32[8,2,1024]{2,1,0:T(2,128)}), f32[8,2,1024]{2,1,0:T(2,128)S(1)}, u32[]{:S(2)}, u32[]{:S(2)}) %all-to-all-start.1) | async-done | bytes 65568 | tf_op jit(solution)/shard_map/all_to_all | solution.py:419
  59.5 2.4 %maximum_select_fusion = bf16[128,4096]{1,0:T(8,128)(2,1)} fusion(bf16[128,1024]{1,0:T(8,128)(2,1)} %collective-permute-done.9, bf16[128,1024]{1,0:T(8,128)(2,1)} %collective-permute-done.8, bf16[128,1024]{1,0:T(8,128)(2,1)S(1)} %get-tuple-element.42, bf16[128,1024]{1,0:T(8,128)(2,1)S(1)} %get-tuple-element.41, pred[]{:T(512)S(6)} %eq.4), kind=kLoop, calls=%fused_computation | loop fusion | flops 8912896 | bytes 2097153 | tf_op jit(solution)/shard_map/jit(_where)/select_n | solution.py:422
  61.9 2.0 %collective-permute-done.14.near = bf16[256,512]{1,0:T(8,128)(2,1)S(1)} collective-permute-done((bf16[256,512]{1,0:T(8,128)(2,1)}, bf16[256,512]{1,0:T(8,128)(2,1)S(1)}, u32[]{:S(2)}, u32[]{:S(2)}) %collective-permute-start.14) | collective-permute-done | bytes 262176 | tf_op jit(solution)/shard_map/ppermute | solution.py:415
  63.9 4.8 %collective-permute-done.15.past = bf16[256,512]{1,0:T(8,128)(2,1)S(1)} collective-permute-done((bf16[256,512]{1,0:T(8,128)(2,1)S(1)}, bf16[256,512]{1,0:T(8,128)(2,1)S(1)}, u32[]{:S(2)}, u32[]{:S(2)}) %collective-permute-start.15) | collective-permute-done | bytes 262176 | tf_op jit(solution)/shard_map/ppermute | solution.py:415
  69.4 0.8 %collective-permute-done.16.refs_3_ = bf16[128,512]{1,0:T(8,128)(2,1)S(1)} collective-permute-done((bf16[128,512]{1,0:T(8,128)(2,1)S(1)}, bf16[128,512]{1,0:T(8,128)(2,1)S(1)}, u32[]{:S(2)}, u32[]{:S(2)}) %collective-permute-start.16) | collective-permute-done | bytes 131104 | tf_op jit(solution)/shard_map/ppermute | solution.py:412
  70.4 0.9 %place.1 = (bf16[128,1024]{1,0:T(8,128)(2,1)}, bf16[128,1024]{1,0:T(8,128)(2,1)}) custom-call(bf16[128,512]{1,0:T(8,128)(2,1)S(1)} %get-tuple-element.51.refs_0_, bf16[128,512]{1,0:T(8,128)(2,1)S(1)} %collective-permute-done.13.refs_1_, bf16[128,512]{1,0:T(8,128)(2,1)S(1)} %get-tuple-element.57.refs_2_, bf16[128,512]{1,0:T(8,128)(2,1)S(1)} %collective-permute-done.16.refs_3_), custom_call_target="tpu_custom_call" | custom-call | tf_op jit(solution)/shard_map/place/pallas_call | solution.py:393
  (29 shorter events, 2.6 us)
Async XLA Ops:
  0.6 4.2 %copy-start = (bf16[128,4096]{1,0:T(8,128)(2,1)S(1)}, bf16[128,4096]{1,0:T(8,128)(2,1)}, u32[]{:S(2)}) copy-start(bf16[128,4096]{1,0:T(8,128)(2,1)} %q_own.3) | copy-start | bytes 3145732
  0.6 1.9 %collective-permute-start = (bf16[128,1024]{1,0:T(8,128)(2,1)}, bf16[128,1024]{1,0:T(8,128)(2,1)S(1)}, u32[]{:S(2)}, u32[]{:S(2)}) collective-permute-start(bf16[128,1024]{1,0:T(8,128)(2,1)} %keys.3), channel_id=1, source_target_pairs={{0,1},{1,0},{2,3},{3,2},{4,5},{5,4},{6,7},{7,6},{8,9},{9,8},{10,11... | collective-permute-start | bytes 786440 | tf_op jit(solution)/shard_map/ppermute | solution.py:412
  1.2 1.7 %collective-permute-start.1 = (bf16[128,1024]{1,0:T(8,128)(2,1)}, bf16[128,1024]{1,0:T(8,128)(2,1)S(1)}, u32[]{:S(2)}, u32[]{:S(2)}) collective-permute-start(bf16[128,1024]{1,0:T(8,128)(2,1)} %values.3), channel_id=1, source_target_pairs={{0,1},{1,0},{2,3},{3,2},{4,5},{5,4},{6,7},{7,6},{8,9},{9,8},{10,11... | collective-permute-start | bytes 786440 | tf_op jit(solution)/shard_map/ppermute | solution.py:412
  4.9 20.6 %collective-permute-start.2 = (bf16[128,4096]{1,0:T(8,128)(2,1)S(1)}, bf16[128,4096]{1,0:T(8,128)(2,1)}, u32[]{:S(2)}, u32[]{:S(2)}) collective-permute-start(bf16[128,4096]{1,0:T(8,128)(2,1)S(1)} %copy-done), channel_id=1, source_target_pairs={{0,1},{1,0},{2,3},{3,2},{4,5},{5,4},{6,7},{7,6},{8,9},{9,8},{10,11... | collective-permute-start | bytes 3145736 | tf_op jit(solution)/shard_map/ppermute | solution.py:412
  5.2 20.3 %collective-permute-start.3 = (bf16[128,4096]{1,0:T(8,128)(2,1)}, bf16[128,4096]{1,0:T(8,128)(2,1)}, u32[]{:S(2)}, u32[]{:S(2)}) collective-permute-start(bf16[128,4096]{1,0:T(8,128)(2,1)} %o_own.3), channel_id=1, source_target_pairs={{0,1},{1,0},{2,3},{3,2},{4,5},{5,4},{6,7},{7,6},{8,9},{9,8},{10,11... | collective-permute-start | bytes 3145736 | tf_op jit(solution)/shard_map/ppermute | solution.py:412
  5.4 19.5 %collective-permute-start.6 = (bf16[256,512]{1,0:T(8,128)(2,1)}, bf16[256,512]{1,0:T(8,128)(2,1)S(1)}, u32[]{:S(2)}, u32[]{:S(2)}) collective-permute-start(bf16[256,512]{1,0:T(8,128)(2,1)} %get-tuple-element.33.kv_here_in), channel_id=1, source_target_pairs={{0,2},{1,3},{2,4},{3,5},{4,6},{5,7},{6,8},{7,9},{8,10},{9,11},{10,... | collective-permute-start | bytes 786440 | tf_op jit(solution)/shard_map/ppermute | solution.py:415
  8.2 17.3 %collective-permute-start.7 = (bf16[256,512]{1,0:T(8,128)(2,1)}, bf16[256,512]{1,0:T(8,128)(2,1)S(1)}, u32[]{:S(2)}, u32[]{:S(2)}) collective-permute-start(bf16[256,512]{1,0:T(8,128)(2,1)} %get-tuple-element.33.kv_here_in), channel_id=1, source_target_pairs={{0,4},{1,5},{2,6},{3,7},{4,8},{5,9},{6,10},{7,11},{8,12},{9,13},{1... | collective-permute-start | bytes 786440 | tf_op jit(solution)/shard_map/ppermute | solution.py:415
  24.3 13.1 %collective-permute-start.4 = (bf16[256,512]{1,0:T(8,128)(2,1)}, bf16[256,512]{1,0:T(8,128)(2,1)S(1)}, u32[]{:S(2)}, u32[]{:S(2)}) collective-permute-start(bf16[256,512]{1,0:T(8,128)(2,1)} %get-tuple-element.37.kv_here_in), channel_id=1, source_target_pairs={{0,2},{1,3},{2,4},{3,5},{4,6},{5,7},{6,8},{7,9},{8,10},{9,11},{10,... | collective-permute-start | bytes 786440 | tf_op jit(solution)/shard_map/ppermute | solution.py:415
  24.8 12.6 %collective-permute-start.5 = (bf16[256,512]{1,0:T(8,128)(2,1)}, bf16[256,512]{1,0:T(8,128)(2,1)S(1)}, u32[]{:S(2)}, u32[]{:S(2)}) collective-permute-start(bf16[256,512]{1,0:T(8,128)(2,1)} %get-tuple-element.37.kv_here_in), channel_id=1, source_target_pairs={{0,4},{1,5},{2,6},{3,7},{4,8},{5,9},{6,10},{7,11},{8,12},{9,13},{1... | collective-permute-start | bytes 786440 | tf_op jit(solution)/shard_map/ppermute | solution.py:415
  31.8 25.7 %collective-permute-start.11 = (bf16[256,512]{1,0:T(8,128)(2,1)S(1)}, bf16[256,512]{1,0:T(8,128)(2,1)S(1)}, u32[]{:S(2)}, u32[]{:S(2)}) collective-permute-start(bf16[256,512]{1,0:T(8,128)(2,1)S(1)} %get-tuple-element.47), channel_id=1, source_target_pairs={{0,14},{1,15},{2,0},{3,1},{4,2},{5,3},{6,4},{7,5},{8,6},{9,7},{10,... | collective-permute-start | bytes 786440 | tf_op jit(solution)/shard_map/ppermute | solution.py:415
  36.0 23.4 %collective-permute-start.12 = (bf16[256,512]{1,0:T(8,128)(2,1)S(1)}, bf16[256,512]{1,0:T(8,128)(2,1)S(1)}, u32[]{:S(2)}, u32[]{:S(2)}) collective-permute-start(bf16[256,512]{1,0:T(8,128)(2,1)S(1)} %get-tuple-element.48), channel_id=1, source_target_pairs={{0,12},{1,13},{2,14},{3,15},{4,0},{5,1},{6,2},{7,3},{8,4},{9,5},{1... | collective-permute-start | bytes 786440 | tf_op jit(solution)/shard_map/ppermute | solution.py:415
  44.4 15.1 %collective-permute-start.9 = (bf16[128,1024]{1,0:T(8,128)(2,1)}, bf16[128,1024]{1,0:T(8,128)(2,1)}, u32[]{:S(2)}, u32[]{:S(2)}) collective-permute-start(bf16[128,1024]{1,0:T(8,128)(2,1)} %get-tuple-element.44), channel_id=1, source_target_pairs={{0,1},{1,0},{2,3},{3,2},{4,5},{5,4},{6,7},{7,6},{8,9},{9,8},{10,11... | collective-permute-start | bytes 786440 | tf_op jit(solution)/shard_map/ppermute | solution.py:412
  44.5 15.0 %collective-permute-start.8 = (bf16[128,1024]{1,0:T(8,128)(2,1)S(1)}, bf16[128,1024]{1,0:T(8,128)(2,1)}, u32[]{:S(2)}, u32[]{:S(2)}) collective-permute-start(bf16[128,1024]{1,0:T(8,128)(2,1)S(1)} %get-tuple-element.43), channel_id=1, source_target_pairs={{0,1},{1,0},{2,3},{3,2},{4,5},{5,4},{6,7},{7,6},{8,9},{9,8},{10,11... | collective-permute-start | bytes 786440 | tf_op jit(solution)/shard_map/ppermute | solution.py:412
  45.0 7.2 %collective-permute-start.10 = (f32[16,128]{1,0:T(8,128)S(1)}, f32[16,128]{1,0:T(8,128)S(1)}, u32[]{:S(2)}, u32[]{:S(2)}) collective-permute-start(f32[16,128]{1,0:T(8,128)S(1)} %get-tuple-element.63), channel_id=1, source_target_pairs={{0,1},{1,0},{2,3},{3,2},{4,5},{5,4},{6,7},{7,6},{8,9},{9,8},{10,11... | collective-permute-start | bytes 24584 | tf_op jit(solution)/shard_map/ppermute | solution.py:412
  45.7 13.6 %all-to-all-start.1 = ((f32[8,2,1024]{2,1,0:T(2,128)}), f32[8,2,1024]{2,1,0:T(2,128)S(1)}, u32[]{:S(2)}, u32[]{:S(2)}) async-start(f32[8,2,1024]{2,1,0:T(2,128)} %reshape.11), calls=%async_computation.1 | async-start | bytes 131072 | tf_op jit(solution)/shard_map/all_to_all | solution.py:419
  52.2 11.7 %collective-permute-start.14 = (bf16[256,512]{1,0:T(8,128)(2,1)}, bf16[256,512]{1,0:T(8,128)(2,1)S(1)}, u32[]{:S(2)}, u32[]{:S(2)}) collective-permute-start(bf16[256,512]{1,0:T(8,128)(2,1)} %get-tuple-element.55), channel_id=1, source_target_pairs={{0,14},{1,15},{2,0},{3,1},{4,2},{5,3},{6,4},{7,5},{8,6},{9,7},{10,... | collective-permute-start | bytes 786440 | tf_op jit(solution)/shard_map/ppermute | solution.py:415
  57.5 11.2 %collective-permute-start.15 = (bf16[256,512]{1,0:T(8,128)(2,1)S(1)}, bf16[256,512]{1,0:T(8,128)(2,1)S(1)}, u32[]{:S(2)}, u32[]{:S(2)}) collective-permute-start(bf16[256,512]{1,0:T(8,128)(2,1)S(1)} %get-tuple-element.56), channel_id=1, source_target_pairs={{0,12},{1,13},{2,14},{3,15},{4,0},{5,1},{6,2},{7,3},{8,4},{9,5},{1... | collective-permute-start | bytes 786440 | tf_op jit(solution)/shard_map/ppermute | solution.py:415
  68.8 1.4 %collective-permute-start.16 = (bf16[128,512]{1,0:T(8,128)(2,1)S(1)}, bf16[128,512]{1,0:T(8,128)(2,1)S(1)}, u32[]{:S(2)}, u32[]{:S(2)}) collective-permute-start(bf16[128,512]{1,0:T(8,128)(2,1)S(1)} %get-tuple-element.58), channel_id=1, source_target_pairs={{0,1},{1,0},{2,3},{3,2},{4,5},{5,4},{6,7},{7,6},{8,9},{9,8},{10,11... | collective-permute-start | bytes 393224 | tf_op jit(solution)/shard_map/ppermute | solution.py:412
  68.9 1.5 %collective-permute-start.13 = (bf16[128,512]{1,0:T(8,128)(2,1)S(1)}, bf16[128,512]{1,0:T(8,128)(2,1)S(1)}, u32[]{:S(2)}, u32[]{:S(2)}) collective-permute-start(bf16[128,512]{1,0:T(8,128)(2,1)S(1)} %get-tuple-element.53), channel_id=1, source_target_pairs={{0,1},{1,0},{2,3},{3,2},{4,5},{5,4},{6,7},{7,6},{8,9},{9,8},{10,11... | collective-permute-start | bytes 393224 | tf_op jit(solution)/shard_map/ppermute | solution.py:412

commit v4 on v3

--- a/solution.py
+++ b/solution.py
@@ -292,18 +292,29 @@
     )
 
 
-def arrange_kernel(keys, values, k_other, v_other, *outs):
+def arrange_kernel(chunk, keys, values, k_other, v_other, payload):
     half = keys.shape[0]
-    payloads = outs
     core, _ = pair_position()
-    count = payloads[0].shape[1] // (2 * HEAD_SIZE)
-    for chunk, payload in enumerate(payloads):
-        for h in range(count):
-            source = head_columns(core * (count * CHUNKS) + chunk * count + h)
-            for side, (mine, theirs) in enumerate(((keys, k_other), (values, v_other))):
-                to = slice((2 * h + side) * HEAD_SIZE, (2 * h + side + 1) * HEAD_SIZE)
-                payload[:half, to] = mine[:, source]
-                payload[half:, to] = theirs[:, source]
+    count = payload.shape[1] // (2 * HEAD_SIZE)
+    for h in range(count):
+        source = head_columns(core * (count * CHUNKS) + chunk * count + h)
+        for side, (mine, theirs) in enumerate(((keys, k_other), (values, v_other))):
+            to = slice((2 * h + side) * HEAD_SIZE, (2 * h + side + 1) * HEAD_SIZE)
+            payload[:half, to] = mine[:, source]
+            payload[half:, to] = theirs[:, source]
+
+
+def arrange(keys, values, k_other, v_other, chunk):
+    half, kv_width = keys.shape
+    whole = pl.BlockSpec(memory_space=pltpu.VMEM)
+    return pl.pallas_call(
+        functools.partial(arrange_kernel, chunk),
+        name=f"arrange_{chunk}",
+        grid=(1,),
+        in_specs=[pl.BlockSpec(keys.shape, lambda i: (0, 0))] * 2 + [whole] * 2,
+        out_specs=whole,
+        out_shape=pltpu.HBM((2 * half, kv_width // CHUNKS), keys.dtype),
+    )(keys, values, *in_vmem(k_other, v_other))
 
 
 def own_rows_kernel(keys, values, out):
@@ -330,20 +341,6 @@
         out_specs=pl.BlockSpec(shape, lambda i: (0, 0, 0)),
         out_shape=jax.ShapeDtypeStruct(shape, keys.dtype),
     )(keys, values)
-
-
-def arrange(keys, values, k_other, v_other):
-    half, kv_width = keys.shape
-    whole = pl.BlockSpec(memory_space=pltpu.VMEM)
-    payload = pltpu.HBM((2 * half, kv_width // CHUNKS), keys.dtype)
-    return pl.pallas_call(
-        arrange_kernel,
-        name="arrange",
-        grid=(1,),
-        in_specs=[pl.BlockSpec(keys.shape, lambda i: (0, 0))] * 2 + [whole] * 2,
-        out_specs=[whole] * CHUNKS,
-        out_shape=[payload] * CHUNKS,
-    )(keys, values, *in_vmem(k_other, v_other))
 
 
 def collect_kernel(chunk, here, near, past, strided, mine, theirs):
@@ -425,8 +422,10 @@
             jnp.concatenate([theirs, mine], axis=1),
         )
 
-    far = lax.all_to_all(own_rows(keys, values, peers), "ctx", 0, 0, tiled=True)
-    here = arrange(keys, values, swap(keys), swap(values))
+    sent = own_rows(keys, values, peers)
+    k_other, v_other, sent = lax.optimization_barrier((swap(keys), swap(values), sent))
+    far = lax.all_to_all(sent, "ctx", 0, 0, tiled=True)
+    here = [arrange(keys, values, k_other, v_other, chunk) for chunk in range(CHUNKS)]
     near, past = [], []
     for chunk in range(CHUNKS):
         payload = here[chunk]
@@ -457,7 +456,8 @@
         far, _ = lax.optimization_barrier((far, out[2]))
         far_terms.append(out[6])
 
-    strided_terms = exchanged(jnp.concatenate(far_terms, axis=1).reshape(pairs, 2, kv_width))
+    terms, *_ = lax.optimization_barrier((jnp.concatenate(far_terms, axis=1), *sums[0][1:]))
+    strided_terms = exchanged(terms.reshape(pairs, 2, kv_width))
     grad_queries = joined(jnp.concatenate(dq_own, axis=1), jnp.concatenate(dq_other, axis=1))
     norm = jnp.concatenate(norms, axis=0)
     log_norm = joined(norm[:, :half].T, swap(norm[:, half:]).T)

time: 71.8 us -> 69 us (0.961)
  blocking collectives: 13.1 us -> 0 us
  waiting for transfers between devices: 10.8 us -> 17.2 us
  starting transfers between devices: 25.3 us -> 27.5 us
  Pallas kernels: 17.8 us -> 19.4 us
    all_to_all x1 -> x0, blocking collectives: 13.1 us -> none  [local(): far = lax.all_to_all(own_rows(keys, values, peers), 'ctx', 0, 0, tiled=True)]
    all_to_all x0 -> x1, waiting for transfers between devices: none -> 8.05 us  [local(): far = lax.all_to_all(sent, 'ctx', 0, 0, tiled=True)]
    ppermute x8, waiting for transfers between devices: 6.84 us -> 0.02 us  [shifted(): return lax.ppermute(x, 'ctx', [(i, (i + by) % peers) for i in range(peers)])]
    all_to_all x1, waiting for transfers between devices: 1.29 us -> 6.5 us  [exchanged(): return lax.all_to_all(x, 'ctx', 0, 0, axis_index_groups=groups)]
    all_to_all x0 -> x1, starting transfers between devices: none -> 4.61 us  [local(): far = lax.all_to_all(sent, 'ctx', 0, 0, tiled=True)]
    pallas_call x1 -> x2, Pallas kernels: 1.95 us -> 3.6 us  [arrange(): pl.pallas_call(functools.partial(arrange_kernel, chunk), name=f'arrange_{...]
    all_to_all x1, starting transfers between devices: 6.44 us -> 5.1 us  [exchanged(): return lax.all_to_all(x, 'ctx', 0, 0, axis_index_groups=groups)]
    ppermute x8, starting transfers between devices: 16.5 us -> 15.5 us  [shifted(): return lax.ppermute(x, 'ctx', [(i, (i + by) % peers) for i in range(peers)])]
  transfers between devices with their start and end apart: 18 -> 19, of which waited for: 7 -> 6; matrix products, arithmetic and copies ran while one was open for 5% -> 5% of each run, Pallas kernels for 21% -> 24%
where the time goes in v4:
time: 69 us; the launch traced here: 68.6 us
  starting transfers between devices  27.5 us (40%)
  Pallas kernels  19.4 us (28%)
  waiting for transfers between devices  17.2 us (25%)
  other arithmetic  3.07 us (4%)
  between operations  0.75 us (1%)
    ppermute x8, starting transfers between devices, shifted(): return lax.ppermute(x, 'ctx', [(i, (i + by) % peers) for i in range(peers)])  15.5 us
    pallas_call x2, Pallas kernels, attention(): pl.pallas_call(functools.partial(attention_kernel, chunk), name=f'attenti...  13.3 us
    all_to_all x1, waiting for transfers between devices, local(): far = lax.all_to_all(sent, 'ctx', 0, 0, tiled=True)  8.05 us
    all_to_all x1, waiting for transfers between devices, exchanged(): return lax.all_to_all(x, 'ctx', 0, 0, axis_index_groups=groups)  6.5 us
    all_to_all x1, starting transfers between devices, exchanged(): return lax.all_to_all(x, 'ctx', 0, 0, axis_index_groups=groups)  5.1 us
    all_to_all x1, starting transfers between devices, local(): far = lax.all_to_all(sent, 'ctx', 0, 0, tiled=True)  4.61 us
    pallas_call x2, Pallas kernels, arrange(): pl.pallas_call(functools.partial(arrange_kernel, chunk), name=f'arrange_{...  3.6 us
    select_n x2, other arithmetic, joined(): jnp.where(core == 0, jnp.concatenate([mine, theirs], axis=1), jnp.concate...  3.06 us
  transfers between devices with their start and end apart: 19, of which 6 were waited for; matrix products, arithmetic and copies ran while one was open for 5% of the time, Pallas kernels for 24%

profile of v4, /device:TPU:0, one launch (start us, length us, event | category | flops | bytes accessed | tf_op | source)
XLA Modules:
  0.0 68.6 jit_solution(5613827060689536106)
XLA Ops:
  0.6 0.5 collective-permute-start
  1.2 1.4 %own_rows.1 = bf16[16,8,128]{2,1,0:T(8,128)(2,1)} custom-call(bf16[128,1024]{1,0:T(8,128)(2,1)} %keys.5, bf16[128,1024]{1,0:T(8,128)(2,1)} %values.5), custom_call_target="tpu_custom_call" | custom-call | tf_op jit(solution)/shard_map/own_rows/pallas_call | solution.py:336
  2.9 1.8 %arrange_0.1.kv_here_in = bf16[256,512]{1,0:T(8,128)(2,1)} custom-call(bf16[128,1024]{1,0:T(8,128)(2,1)} %keys.5, bf16[128,1024]{1,0:T(8,128)(2,1)} %values.5, bf16[128,1024]{1,0:T(8,128)(2,1)S(1)} %collective-permute-done.k_other, bf16[128,1024]{1,0:T(8,128)(2,1)S(1)} %collective-permute-done.1.v_other), custom_call_target="tpu_custom_call" | custom-call | tf_op jit(solution)/shard_map/arrange_0/pallas_call | solution.py:310
  5.2 2.9 %collective-permute-start.6 = (bf16[256,512]{1,0:T(8,128)(2,1)}, bf16[256,512]{1,0:T(8,128)(2,1)S(1)}, u32[]{:S(2)}, u32[]{:S(2)}) collective-permute-start(bf16[256,512]{1,0:T(8,128)(2,1)} %arrange_0.1.kv_here_in), channel_id=1, source_target_pairs={{0,2},{1,3},{2,4},{3,5},{4,6},{5,7},{6,8},{7,9},{8,10},{9,11},{10,... | collective-permute-start | bytes 786440 | tf_op jit(solution)/shard_map/ppermute | solution.py:412
  8.1 1.6 %collective-permute-start.7 = (bf16[256,512]{1,0:T(8,128)(2,1)}, bf16[256,512]{1,0:T(8,128)(2,1)S(1)}, u32[]{:S(2)}, u32[]{:S(2)}) collective-permute-start(bf16[256,512]{1,0:T(8,128)(2,1)} %arrange_0.1.kv_here_in), channel_id=1, source_target_pairs={{0,4},{1,5},{2,6},{3,7},{4,8},{5,9},{6,10},{7,11},{8,12},{9,13},{1... | collective-permute-start | bytes 786440 | tf_op jit(solution)/shard_map/ppermute | solution.py:412
  9.7 4.6 %all-to-all-start = ((bf16[16,8,128]{2,1,0:T(8,128)(2,1)}), bf16[16,8,128]{2,1,0:T(8,128)(2,1)S(1)}, u32[]{:S(2)}, u32[]{:S(2)}) async-start(bf16[16,8,128]{2,1,0:T(8,128)(2,1)} %own_rows.1), calls=%async_computation | async-start | bytes 65536 | tf_op jit(solution)/shard_map/all_to_all | solution.py:427
  14.3 1.8 %arrange_1.1.kv_here_in = bf16[256,512]{1,0:T(8,128)(2,1)} custom-call(bf16[128,1024]{1,0:T(8,128)(2,1)} %keys.5, bf16[128,1024]{1,0:T(8,128)(2,1)} %values.5, bf16[128,1024]{1,0:T(8,128)(2,1)S(1)} %collective-permute-done.k_other, bf16[128,1024]{1,0:T(8,128)(2,1)S(1)} %collective-permute-done.1.v_other), custom_call_target="tpu_custom_call" | custom-call | tf_op jit(solution)/shard_map/arrange_1/pallas_call | solution.py:310
  16.1 8.1 %all-to-all-done.kv_far = bf16[16,8,128]{2,1,0:T(8,128)(2,1)S(1)} async-done(((bf16[16,8,128]{2,1,0:T(8,128)(2,1)}), bf16[16,8,128]{2,1,0:T(8,128)(2,1)S(1)}, u32[]{:S(2)}, u32[]{:S(2)}) %all-to-all-start) | async-done | bytes 32800 | tf_op jit(solution)/shard_map/all_to_all | solution.py:427
  24.1 0.5 collective-permute-start.4
  24.7 0.7 collective-permute-start.5
  25.4 6.3 %attention_0.1 = (bf16[128,1024]{1,0:T(8,128)(2,1)S(1)}, bf16[128,1024]{1,0:T(8,128)(2,1)S(1)}, f32[8,256]{1,0:T(8,128)S(1)}, f32[256,512]{1,0:T(8,128)S(1)}, bf...) custom-call(bf16[128,4096]{1,0:T(8,128)(2,1)} %q_own.3, ...), custom_call_target="tpu_custom_call" | custom-call | flops 4110417920 | bytes 4194304 | tf_op jit(solution)/shard_map/attention_0/pallas_call | solution.py:263
  31.7 4.2 %collective-permute-start.11 = (bf16[256,512]{1,0:T(8,128)(2,1)S(1)}, bf16[256,512]{1,0:T(8,128)(2,1)S(1)}, u32[]{:S(2)}, u32[]{:S(2)}) collective-permute-start(bf16[256,512]{1,0:T(8,128)(2,1)S(1)} %get-tuple-element.50), channel_id=1, source_target_pairs={{0,14},{1,15},{2,0},{3,1},{4,2},{5,3},{6,4},{7,5},{8,6},{9,7},{10,... | collective-permute-start | bytes 786440 | tf_op jit(solution)/shard_map/ppermute | solution.py:412
  35.8 1.4 %collective-permute-start.12 = (bf16[256,512]{1,0:T(8,128)(2,1)S(1)}, bf16[256,512]{1,0:T(8,128)(2,1)S(1)}, u32[]{:S(2)}, u32[]{:S(2)}) collective-permute-start(bf16[256,512]{1,0:T(8,128)(2,1)S(1)} %get-tuple-element.51), channel_id=1, source_target_pairs={{0,12},{1,13},{2,14},{3,15},{4,0},{5,1},{6,2},{7,3},{8,4},{9,5},{1... | collective-permute-start | bytes 786440 | tf_op jit(solution)/shard_map/ppermute | solution.py:412
  37.3 7.0 %attention_1.1 = (bf16[128,1024]{1,0:T(8,128)(2,1)S(1)}, bf16[128,1024]{1,0:T(8,128)(2,1)}, f32[8,256]{1,0:T(8,128)S(1)}, f32[256,512]{1,0:T(8,128)S(1)}, bf16[2...) custom-call(bf16[128,4096]{1,0:T(8,128)(2,1)} %q_own.3, ...), custom_call_target="tpu_custom_call" | custom-call | flops 4110417920 | bytes 4194304 | tf_op jit(solution)/shard_map/attention_1/pallas_call | solution.py:263
  44.9 1.3 %collective-permute-done.10 = f32[16,128]{1,0:T(8,128)S(1)} collective-permute-done((f32[16,128]{1,0:T(8,128)S(1)}, f32[16,128]{1,0:T(8,128)S(1)}, u32[]{:S(2)}, u32[]{:S(2)}) %collective-permute-start.10) | collective-permute-done | bytes 8224 | tf_op jit(solution)/shard_map/ppermute | solution.py:409
  46.2 4.3 %collective-permute-start.14 = (bf16[256,512]{1,0:T(8,128)(2,1)S(1)}, bf16[256,512]{1,0:T(8,128)(2,1)S(1)}, u32[]{:S(2)}, u32[]{:S(2)}) collective-permute-start(bf16[256,512]{1,0:T(8,128)(2,1)S(1)} %get-tuple-element.59), channel_id=1, source_target_pairs={{0,14},{1,15},{2,0},{3,1},{4,2},{5,3},{6,4},{7,5},{8,6},{9,7},{10,... | collective-permute-start | bytes 786440 | tf_op jit(solution)/shard_map/ppermute | solution.py:412
  50.5 0.6 maximum_select_fusion.1
  51.1 0.7 reshape.11
  51.8 5.1 %all-to-all-start.1 = ((f32[8,2,1024]{2,1,0:T(2,128)}), f32[8,2,1024]{2,1,0:T(2,128)S(1)}, u32[]{:S(2)}, u32[]{:S(2)}) async-start(f32[8,2,1024]{2,1,0:T(2,128)} %reshape.11), calls=%async_computation.1 | async-start | bytes 131072 | tf_op jit(solution)/shard_map/all_to_all | solution.py:416
  56.9 2.5 %maximum_select_fusion = bf16[128,4096]{1,0:T(8,128)(2,1)} fusion(bf16[128,1024]{1,0:T(8,128)(2,1)} %collective-permute-done.9, bf16[128,1024]{1,0:T(8,128)(2,1)} %collective-permute-done.8, bf16[128,1024]{1,0:T(8,128)(2,1)S(1)} %get-tuple-element.45, bf16[128,1024]{1,0:T(8,128)(2,1)S(1)} %get-tuple-element.44, pred[]{:T(512)S(6)} %eq.4), kind=kLoop, calls=%fused_computation | loop fusion | flops 8912896 | bytes 2097153 | tf_op jit(solution)/shard_map/jit(_where)/select_n | solution.py:419
  59.3 6.5 %all-to-all-done.1.strided = f32[8,2,1024]{2,1,0:T(2,128)S(1)} async-done(((f32[8,2,1024]{2,1,0:T(2,128)}), f32[8,2,1024]{2,1,0:T(2,128)S(1)}, u32[]{:S(2)}, u32[]{:S(2)}) %all-to-all-start.1) | async-done | bytes 65568 | tf_op jit(solution)/shard_map/all_to_all | solution.py:416
  66.2 0.5 collective-permute-start.13
  66.6 0.8 %collective-permute-done.16.refs_3_ = bf16[128,512]{1,0:T(8,128)(2,1)S(1)} collective-permute-done((bf16[128,512]{1,0:T(8,128)(2,1)S(1)}, bf16[128,512]{1,0:T(8,128)(2,1)S(1)}, u32[]{:S(2)}, u32[]{:S(2)}) %collective-permute-start.16) | collective-permute-done | bytes 131104 | tf_op jit(solution)/shard_map/ppermute | solution.py:409
  67.7 0.9 %place.1 = (bf16[128,1024]{1,0:T(8,128)(2,1)}, bf16[128,1024]{1,0:T(8,128)(2,1)}) custom-call(bf16[128,512]{1,0:T(8,128)(2,1)S(1)} %get-tuple-element.55.refs_0_, bf16[128,512]{1,0:T(8,128)(2,1)S(1)} %collective-permute-done.13.refs_1_, bf16[128,512]{1,0:T(8,128)(2,1)S(1)} %get-tuple-element.61.refs_2_, bf16[128,512]{1,0:T(8,128)(2,1)S(1)} %collective-permute-done.16.refs_3_), custom_call_target="tpu_custom_call" | custom-call | tf_op jit(solution)/shard_map/place/pallas_call | solution.py:390
  (31 shorter events, 2.0 us)
Async XLA Ops:
  0.6 4.1 %copy-start = (bf16[128,4096]{1,0:T(8,128)(2,1)S(1)}, bf16[128,4096]{1,0:T(8,128)(2,1)}, u32[]{:S(2)}) copy-start(bf16[128,4096]{1,0:T(8,128)(2,1)} %q_own.3) | copy-start | bytes 3145732
  0.6 2.0 %collective-permute-start = (bf16[128,1024]{1,0:T(8,128)(2,1)}, bf16[128,1024]{1,0:T(8,128)(2,1)S(1)}, u32[]{:S(2)}, u32[]{:S(2)}) collective-permute-start(bf16[128,1024]{1,0:T(8,128)(2,1)} %keys.5), channel_id=1, source_target_pairs={{0,1},{1,0},{2,3},{3,2},{4,5},{5,4},{6,7},{7,6},{8,9},{9,8},{10,11... | collective-permute-start | bytes 786440 | tf_op jit(solution)/shard_map/ppermute | solution.py:409
  1.2 1.7 %collective-permute-start.1 = (bf16[128,1024]{1,0:T(8,128)(2,1)}, bf16[128,1024]{1,0:T(8,128)(2,1)S(1)}, u32[]{:S(2)}, u32[]{:S(2)}) collective-permute-start(bf16[128,1024]{1,0:T(8,128)(2,1)} %values.5), channel_id=1, source_target_pairs={{0,1},{1,0},{2,3},{3,2},{4,5},{5,4},{6,7},{7,6},{8,9},{9,8},{10,11... | collective-permute-start | bytes 786440 | tf_op jit(solution)/shard_map/ppermute | solution.py:409
  4.7 20.6 %collective-permute-start.2 = (bf16[128,4096]{1,0:T(8,128)(2,1)S(1)}, bf16[128,4096]{1,0:T(8,128)(2,1)}, u32[]{:S(2)}, u32[]{:S(2)}) collective-permute-start(bf16[128,4096]{1,0:T(8,128)(2,1)S(1)} %copy-done), channel_id=1, source_target_pairs={{0,1},{1,0},{2,3},{3,2},{4,5},{5,4},{6,7},{7,6},{8,9},{9,8},{10,11... | collective-permute-start | bytes 3145736 | tf_op jit(solution)/shard_map/ppermute | solution.py:409
  5.1 20.3 %collective-permute-start.3 = (bf16[128,4096]{1,0:T(8,128)(2,1)}, bf16[128,4096]{1,0:T(8,128)(2,1)}, u32[]{:S(2)}, u32[]{:S(2)}) collective-permute-start(bf16[128,4096]{1,0:T(8,128)(2,1)} %o_own.3), channel_id=1, source_target_pairs={{0,1},{1,0},{2,3},{3,2},{4,5},{5,4},{6,7},{7,6},{8,9},{9,8},{10,11... | collective-permute-start | bytes 3145736 | tf_op jit(solution)/shard_map/ppermute | solution.py:409
  5.2 19.5 %collective-permute-start.6 = (bf16[256,512]{1,0:T(8,128)(2,1)}, bf16[256,512]{1,0:T(8,128)(2,1)S(1)}, u32[]{:S(2)}, u32[]{:S(2)}) collective-permute-start(bf16[256,512]{1,0:T(8,128)(2,1)} %arrange_0.1.kv_here_in), channel_id=1, source_target_pairs={{0,2},{1,3},{2,4},{3,5},{4,6},{5,7},{6,8},{7,9},{8,10},{9,11},{10,... | collective-permute-start | bytes 786440 | tf_op jit(solution)/shard_map/ppermute | solution.py:412
  8.1 17.3 %collective-permute-start.7 = (bf16[256,512]{1,0:T(8,128)(2,1)}, bf16[256,512]{1,0:T(8,128)(2,1)S(1)}, u32[]{:S(2)}, u32[]{:S(2)}) collective-permute-start(bf16[256,512]{1,0:T(8,128)(2,1)} %arrange_0.1.kv_here_in), channel_id=1, source_target_pairs={{0,4},{1,5},{2,6},{3,7},{4,8},{5,9},{6,10},{7,11},{8,12},{9,13},{1... | collective-permute-start | bytes 786440 | tf_op jit(solution)/shard_map/ppermute | solution.py:412
  9.7 14.5 %all-to-all-start = ((bf16[16,8,128]{2,1,0:T(8,128)(2,1)}), bf16[16,8,128]{2,1,0:T(8,128)(2,1)S(1)}, u32[]{:S(2)}, u32[]{:S(2)}) async-start(bf16[16,8,128]{2,1,0:T(8,128)(2,1)} %own_rows.1), calls=%async_computation | async-start | bytes 65536 | tf_op jit(solution)/shard_map/all_to_all | solution.py:427
  24.1 13.1 %collective-permute-start.4 = (bf16[256,512]{1,0:T(8,128)(2,1)}, bf16[256,512]{1,0:T(8,128)(2,1)S(1)}, u32[]{:S(2)}, u32[]{:S(2)}) collective-permute-start(bf16[256,512]{1,0:T(8,128)(2,1)} %arrange_1.1.kv_here_in), channel_id=1, source_target_pairs={{0,2},{1,3},{2,4},{3,5},{4,6},{5,7},{6,8},{7,9},{8,10},{9,11},{10,... | collective-permute-start | bytes 786440 | tf_op jit(solution)/shard_map/ppermute | solution.py:412
  24.7 12.6 %collective-permute-start.5 = (bf16[256,512]{1,0:T(8,128)(2,1)}, bf16[256,512]{1,0:T(8,128)(2,1)S(1)}, u32[]{:S(2)}, u32[]{:S(2)}) collective-permute-start(bf16[256,512]{1,0:T(8,128)(2,1)} %arrange_1.1.kv_here_in), channel_id=1, source_target_pairs={{0,4},{1,5},{2,6},{3,7},{4,8},{5,9},{6,10},{7,11},{8,12},{9,13},{1... | collective-permute-start | bytes 786440 | tf_op jit(solution)/shard_map/ppermute | solution.py:412
  31.7 19.4 %collective-permute-start.11 = (bf16[256,512]{1,0:T(8,128)(2,1)S(1)}, bf16[256,512]{1,0:T(8,128)(2,1)S(1)}, u32[]{:S(2)}, u32[]{:S(2)}) collective-permute-start(bf16[256,512]{1,0:T(8,128)(2,1)S(1)} %get-tuple-element.50), channel_id=1, source_target_pairs={{0,14},{1,15},{2,0},{3,1},{4,2},{5,3},{6,4},{7,5},{8,6},{9,7},{10,... | collective-permute-start | bytes 786440 | tf_op jit(solution)/shard_map/ppermute | solution.py:412
  35.8 15.3 %collective-permute-start.12 = (bf16[256,512]{1,0:T(8,128)(2,1)S(1)}, bf16[256,512]{1,0:T(8,128)(2,1)S(1)}, u32[]{:S(2)}, u32[]{:S(2)}) collective-permute-start(bf16[256,512]{1,0:T(8,128)(2,1)S(1)} %get-tuple-element.51), channel_id=1, source_target_pairs={{0,12},{1,13},{2,14},{3,15},{4,0},{5,1},{6,2},{7,3},{8,4},{9,5},{1... | collective-permute-start | bytes 786440 | tf_op jit(solution)/shard_map/ppermute | solution.py:412
  44.2 12.6 %collective-permute-start.9 = (bf16[128,1024]{1,0:T(8,128)(2,1)}, bf16[128,1024]{1,0:T(8,128)(2,1)}, u32[]{:S(2)}, u32[]{:S(2)}) collective-permute-start(bf16[128,1024]{1,0:T(8,128)(2,1)} %get-tuple-element.47), channel_id=1, source_target_pairs={{0,1},{1,0},{2,3},{3,2},{4,5},{5,4},{6,7},{7,6},{8,9},{9,8},{10,11... | collective-permute-start | bytes 786440 | tf_op jit(solution)/shard_map/ppermute | solution.py:409
  44.3 12.6 %collective-permute-start.8 = (bf16[128,1024]{1,0:T(8,128)(2,1)S(1)}, bf16[128,1024]{1,0:T(8,128)(2,1)}, u32[]{:S(2)}, u32[]{:S(2)}) collective-permute-start(bf16[128,1024]{1,0:T(8,128)(2,1)S(1)} %get-tuple-element.46), channel_id=1, source_target_pairs={{0,1},{1,0},{2,3},{3,2},{4,5},{5,4},{6,7},{7,6},{8,9},{9,8},{10,11... | collective-permute-start | bytes 786440 | tf_op jit(solution)/shard_map/ppermute | solution.py:409
  44.8 1.4 %collective-permute-start.10 = (f32[16,128]{1,0:T(8,128)S(1)}, f32[16,128]{1,0:T(8,128)S(1)}, u32[]{:S(2)}, u32[]{:S(2)}) collective-permute-start(f32[16,128]{1,0:T(8,128)S(1)} %get-tuple-element.67), channel_id=1, source_target_pairs={{0,1},{1,0},{2,3},{3,2},{4,5},{5,4},{6,7},{7,6},{8,9},{9,8},{10,11... | collective-permute-start | bytes 24584 | tf_op jit(solution)/shard_map/ppermute | solution.py:409
  46.2 19.7 %collective-permute-start.14 = (bf16[256,512]{1,0:T(8,128)(2,1)S(1)}, bf16[256,512]{1,0:T(8,128)(2,1)S(1)}, u32[]{:S(2)}, u32[]{:S(2)}) collective-permute-start(bf16[256,512]{1,0:T(8,128)(2,1)S(1)} %get-tuple-element.59), channel_id=1, source_target_pairs={{0,14},{1,15},{2,0},{3,1},{4,2},{5,3},{6,4},{7,5},{8,6},{9,7},{10,... | collective-permute-start | bytes 786440 | tf_op jit(solution)/shard_map/ppermute | solution.py:412
  51.1 14.9 %collective-permute-start.15 = (bf16[256,512]{1,0:T(8,128)(2,1)S(1)}, bf16[256,512]{1,0:T(8,128)(2,1)S(1)}, u32[]{:S(2)}, u32[]{:S(2)}) collective-permute-start(bf16[256,512]{1,0:T(8,128)(2,1)S(1)} %get-tuple-element.60), channel_id=1, source_target_pairs={{0,12},{1,13},{2,14},{3,15},{4,0},{5,1},{6,2},{7,3},{8,4},{9,5},{1... | collective-permute-start | bytes 786440 | tf_op jit(solution)/shard_map/ppermute | solution.py:412
  51.8 14.1 %all-to-all-start.1 = ((f32[8,2,1024]{2,1,0:T(2,128)}), f32[8,2,1024]{2,1,0:T(2,128)S(1)}, u32[]{:S(2)}, u32[]{:S(2)}) async-start(f32[8,2,1024]{2,1,0:T(2,128)} %reshape.11), calls=%async_computation.1 | async-start | bytes 131072 | tf_op jit(solution)/shard_map/all_to_all | solution.py:416
  66.1 1.4 %collective-permute-start.16 = (bf16[128,512]{1,0:T(8,128)(2,1)S(1)}, bf16[128,512]{1,0:T(8,128)(2,1)S(1)}, u32[]{:S(2)}, u32[]{:S(2)}) collective-permute-start(bf16[128,512]{1,0:T(8,128)(2,1)S(1)} %get-tuple-element.62), channel_id=1, source_target_pairs={{0,1},{1,0},{2,3},{3,2},{4,5},{5,4},{6,7},{7,6},{8,9},{9,8},{10,11... | collective-permute-start | bytes 393224 | tf_op jit(solution)/shard_map/ppermute | solution.py:409
  66.2 1.5 %collective-permute-start.13 = (bf16[128,512]{1,0:T(8,128)(2,1)S(1)}, bf16[128,512]{1,0:T(8,128)(2,1)S(1)}, u32[]{:S(2)}, u32[]{:S(2)}) collective-permute-start(bf16[128,512]{1,0:T(8,128)(2,1)S(1)} %get-tuple-element.57), channel_id=1, source_target_pairs={{0,1},{1,0},{2,3},{3,2},{4,5},{5,4},{6,7},{7,6},{8,9},{9,8},{10,11... | collective-permute-start | bytes 393224 | tf_op jit(solution)/shard_map/ppermute | solution.py:409

commit v5 on v4

--- a/solution.py
+++ b/solution.py
@@ -408,8 +408,9 @@
     def swap(x):
         return lax.ppermute(x, "ctx", [(i, i ^ 1) for i in range(peers)])
 
-    def shifted(x, by):
-        return lax.ppermute(x, "ctx", [(i, (i + by) % peers) for i in range(peers)])
+    def shifted(x, by, wrap=True):
+        pairs_sent = [(i, (i + by) % peers) for i in range(peers)]
+        return lax.ppermute(x, "ctx", [(i, j) for i, j in pairs_sent if wrap or j == i + by])
 
     def exchanged(x):
         groups = [list(range(parity, peers, 2)) for parity in range(2)]
@@ -449,7 +450,8 @@
             far,
             chunk,
         )
-        sums.append((out[3], shifted(out[4], -2), shifted(out[5], -4)))
+        last = chunk == CHUNKS - 1
+        sums.append((out[3], shifted(out[4], -2, last), shifted(out[5], -4, last)))
         dq_own.append(out[0])
         dq_other.append(swap(out[1]))
         norms.append(out[2])
@@ -460,7 +462,8 @@
     strided_terms = exchanged(terms.reshape(pairs, 2, kv_width))
     grad_queries = joined(jnp.concatenate(dq_own, axis=1), jnp.concatenate(dq_other, axis=1))
     norm = jnp.concatenate(norms, axis=0)
-    log_norm = joined(norm[:, :half].T, swap(norm[:, half:]).T)
+    norm_sent, *_ = lax.optimization_barrier((norm[:, half:], *sums[0][1:]))
+    log_norm = joined(norm[:, :half].T, swap(norm_sent).T)
     parts = []
     for chunk, (own, near_terms, past_terms) in enumerate(sums):
         if chunk > 0:

time: 69 us -> 66.8 us (0.968)
  starting transfers between devices: 27.5 us -> 25.5 us
  waiting for transfers between devices: 17.2 us -> 15.9 us
  local copies, waits for them, and re-layouts: 0.68 us -> 1.65 us
    ppermute x8, starting transfers between devices: 15.5 us -> 14.2 us  [shifted(): lax.ppermute(x, 'ctx', [(i, j) for i, j in pairs_sent if wrap or j == i +...]
    ppermute x9, waiting for transfers between devices: 2.62 us -> 1.3 us  [swap(): return lax.ppermute(x, 'ctx', [(i, i ^ 1) for i in range(peers)])]
    unnamed x3 -> x5, local copies, waits for them, and re-layouts: 0.01 us -> 0.98 us
    ppermute x8, waiting for transfers between devices: 0.02 us -> 0.99 us  [shifted(): lax.ppermute(x, 'ctx', [(i, j) for i, j in pairs_sent if wrap or j == i +...]
    all_to_all x1, waiting for transfers between devices: 6.5 us -> 5.58 us  [exchanged(): return lax.all_to_all(x, 'ctx', 0, 0, axis_index_groups=groups)]
  transfers between devices with their start and end apart: 19 -> 19, of which waited for: 6 -> 6; matrix products, arithmetic and copies ran while one was open for 5% -> 6% of each run, Pallas kernels for 24% -> 25%
where the time goes in v5:
time: 66.8 us; the launch traced here: 66.4 us
  starting transfers between devices  25.5 us (38%)
  Pallas kernels  19.4 us (29%)
  waiting for transfers between devices  15.9 us (24%)
  other arithmetic  3.07 us (5%)
  local copies, waits for them, and re-layouts  1.65 us (2%)
  between operations  0.8 us (1%)
    ppermute x8, starting transfers between devices, shifted(): lax.ppermute(x, 'ctx', [(i, j) for i, j in pairs_sent if wrap or j == i +...  14.2 us
    pallas_call x2, Pallas kernels, attention(): pl.pallas_call(functools.partial(attention_kernel, chunk), name=f'attenti...  13.2 us
    all_to_all x1, waiting for transfers between devices, local(): far = lax.all_to_all(sent, 'ctx', 0, 0, tiled=True)  8.05 us
    all_to_all x1, waiting for transfers between devices, exchanged(): return lax.all_to_all(x, 'ctx', 0, 0, axis_index_groups=groups)  5.58 us
    all_to_all x1, starting transfers between devices, local(): far = lax.all_to_all(sent, 'ctx', 0, 0, tiled=True)  4.61 us
    all_to_all x1, starting transfers between devices, exchanged(): return lax.all_to_all(x, 'ctx', 0, 0, axis_index_groups=groups)  4.53 us
    pallas_call x2, Pallas kernels, arrange(): pl.pallas_call(functools.partial(arrange_kernel, chunk), name=f'arrange_{...  3.6 us
    select_n x2, other arithmetic, joined(): jnp.where(core == 0, jnp.concatenate([mine, theirs], axis=1), jnp.concate...  3.06 us
  transfers between devices with their start and end apart: 19, of which 6 were waited for; matrix products, arithmetic and copies ran while one was open for 6% of the time, Pallas kernels for 25%

profile of v5, /device:TPU:0, one launch (start us, length us, event | category | flops | bytes accessed | tf_op | source)
XLA Modules:
  0.0 66.4 jit_solution(18375744106219055737)
XLA Ops:
  0.6 0.5 collective-permute-start
  1.2 1.4 %own_rows.1 = bf16[16,8,128]{2,1,0:T(8,128)(2,1)} custom-call(bf16[128,1024]{1,0:T(8,128)(2,1)} %keys.5, bf16[128,1024]{1,0:T(8,128)(2,1)} %values.5), custom_call_target="tpu_custom_call" | custom-call | tf_op jit(solution)/shard_map/own_rows/pallas_call | solution.py:336
  2.9 1.8 %arrange_0.1.kv_here_in = bf16[256,512]{1,0:T(8,128)(2,1)} custom-call(bf16[128,1024]{1,0:T(8,128)(2,1)} %keys.5, bf16[128,1024]{1,0:T(8,128)(2,1)} %values.5, bf16[128,1024]{1,0:T(8,128)(2,1)S(1)} %collective-permute-done.k_other, bf16[128,1024]{1,0:T(8,128)(2,1)S(1)} %collective-permute-done.1.v_other), custom_call_target="tpu_custom_call" | custom-call | tf_op jit(solution)/shard_map/arrange_0/pallas_call | solution.py:310
  5.2 2.9 %collective-permute-start.6 = (bf16[256,512]{1,0:T(8,128)(2,1)}, bf16[256,512]{1,0:T(8,128)(2,1)S(1)}, u32[]{:S(2)}, u32[]{:S(2)}) collective-permute-start(bf16[256,512]{1,0:T(8,128)(2,1)} %arrange_0.1.kv_here_in), channel_id=1, source_target_pairs={{0,2},{1,3},{2,4},{3,5},{4,6},{5,7},{6,8},{7,9},{8,10},{9,11},{10,... | collective-permute-start | bytes 786440 | tf_op jit(solution)/shard_map/ppermute | solution.py:413
  8.1 1.6 %collective-permute-start.7 = (bf16[256,512]{1,0:T(8,128)(2,1)}, bf16[256,512]{1,0:T(8,128)(2,1)S(1)}, u32[]{:S(2)}, u32[]{:S(2)}) collective-permute-start(bf16[256,512]{1,0:T(8,128)(2,1)} %arrange_0.1.kv_here_in), channel_id=1, source_target_pairs={{0,4},{1,5},{2,6},{3,7},{4,8},{5,9},{6,10},{7,11},{8,12},{9,13},{1... | collective-permute-start | bytes 786440 | tf_op jit(solution)/shard_map/ppermute | solution.py:413
  9.7 4.6 %all-to-all-start = ((bf16[16,8,128]{2,1,0:T(8,128)(2,1)}), bf16[16,8,128]{2,1,0:T(8,128)(2,1)S(1)}, u32[]{:S(2)}, u32[]{:S(2)}) async-start(bf16[16,8,128]{2,1,0:T(8,128)(2,1)} %own_rows.1), calls=%async_computation | async-start | bytes 65536 | tf_op jit(solution)/shard_map/all_to_all | solution.py:428
  14.3 1.8 %arrange_1.1.kv_here_in = bf16[256,512]{1,0:T(8,128)(2,1)} custom-call(bf16[128,1024]{1,0:T(8,128)(2,1)} %keys.5, bf16[128,1024]{1,0:T(8,128)(2,1)} %values.5, bf16[128,1024]{1,0:T(8,128)(2,1)S(1)} %collective-permute-done.k_other, bf16[128,1024]{1,0:T(8,128)(2,1)S(1)} %collective-permute-done.1.v_other), custom_call_target="tpu_custom_call" | custom-call | tf_op jit(solution)/shard_map/arrange_1/pallas_call | solution.py:310
  16.1 8.1 %all-to-all-done.kv_far = bf16[16,8,128]{2,1,0:T(8,128)(2,1)S(1)} async-done(((bf16[16,8,128]{2,1,0:T(8,128)(2,1)}), bf16[16,8,128]{2,1,0:T(8,128)(2,1)S(1)}, u32[]{:S(2)}, u32[]{:S(2)}) %all-to-all-start) | async-done | bytes 32800 | tf_op jit(solution)/shard_map/all_to_all | solution.py:428
  24.1 0.5 collective-permute-start.4
  24.7 0.7 %collective-permute-start.5 = (bf16[256,512]{1,0:T(8,128)(2,1)}, bf16[256,512]{1,0:T(8,128)(2,1)S(1)}, u32[]{:S(2)}, u32[]{:S(2)}) collective-permute-start(bf16[256,512]{1,0:T(8,128)(2,1)} %arrange_1.1.kv_here_in), channel_id=1, source_target_pairs={{0,4},{1,5},{2,6},{3,7},{4,8},{5,9},{6,10},{7,11},{8,12},{9,13},{1... | collective-permute-start | bytes 786440 | tf_op jit(solution)/shard_map/ppermute | solution.py:413
  25.4 1.0 %copy-done.1 = bf16[128,4096]{1,0:T(8,128)(2,1)} copy-done((bf16[128,4096]{1,0:T(8,128)(2,1)}, bf16[128,4096]{1,0:T(8,128)(2,1)S(1)}, u32[]{:S(2)}) %copy-start.1) | copy-done | bytes 1048600
  26.3 6.3 %attention_0.1 = (bf16[128,1024]{1,0:T(8,128)(2,1)S(1)}, bf16[128,1024]{1,0:T(8,128)(2,1)S(1)}, f32[8,256]{1,0:T(8,128)S(1)}, f32[256,512]{1,0:T(8,128)S(1)}, bf...) custom-call(bf16[128,4096]{1,0:T(8,128)(2,1)} %q_own.3, ...), custom_call_target="tpu_custom_call" | custom-call | flops 4110417920 | bytes 4194304 | tf_op jit(solution)/shard_map/attention_0/pallas_call | solution.py:263
  32.6 1.3 %collective-permute-start.10 = (bf16[256,512]{1,0:T(8,128)(2,1)S(1)}, bf16[256,512]{1,0:T(8,128)(2,1)S(1)}, u32[]{:S(2)}, u32[]{:S(2)}) collective-permute-start(bf16[256,512]{1,0:T(8,128)(2,1)S(1)} %get-tuple-element.50), channel_id=1, source_target_pairs={{2,0},{3,1},{4,2},{5,3},{6,4},{7,5},{8,6},{9,7},{10,8},{11,9},{12,... | collective-permute-start | bytes 786440 | tf_op jit(solution)/shard_map/ppermute | solution.py:413
  33.9 1.3 %collective-permute-start.11 = (bf16[256,512]{1,0:T(8,128)(2,1)S(1)}, bf16[256,512]{1,0:T(8,128)(2,1)S(1)}, u32[]{:S(2)}, u32[]{:S(2)}) collective-permute-start(bf16[256,512]{1,0:T(8,128)(2,1)S(1)} %get-tuple-element.51), channel_id=1, source_target_pairs={{4,0},{5,1},{6,2},{7,3},{8,4},{9,5},{10,6},{11,7},{12,8},{13,9},{1... | collective-permute-start | bytes 786440 | tf_op jit(solution)/shard_map/ppermute | solution.py:413
  35.2 1.0 %collective-permute-done.4.kv_near = bf16[256,512]{1,0:T(8,128)(2,1)S(1)} collective-permute-done((bf16[256,512]{1,0:T(8,128)(2,1)}, bf16[256,512]{1,0:T(8,128)(2,1)S(1)}, u32[]{:S(2)}, u32[]{:S(2)}) %collective-permute-start.4) | collective-permute-done | bytes 262176 | tf_op jit(solution)/shard_map/ppermute | solution.py:413
  36.2 7.0 %attention_1.1 = (bf16[128,1024]{1,0:T(8,128)(2,1)S(1)}, bf16[128,1024]{1,0:T(8,128)(2,1)}, f32[8,256]{1,0:T(8,128)S(1)}, f32[256,512]{1,0:T(8,128)S(1)}, bf16[2...) custom-call(bf16[128,4096]{1,0:T(8,128)(2,1)} %q_own.3, bf16[128,4096]{1,0:T(8,128)(2,1)} %copy-done.1, ...), custom_call_target="tpu_custom_call" | custom-call | flops 4110417920 | bytes 4194304 | tf_op jit(solution)/shard_map/attention_1/pallas_call | solution.py:263
  43.8 5.9 %collective-permute-start.14 = (bf16[256,512]{1,0:T(8,128)(2,1)S(1)}, bf16[256,512]{1,0:T(8,128)(2,1)S(1)}, u32[]{:S(2)}, u32[]{:S(2)}) collective-permute-start(bf16[256,512]{1,0:T(8,128)(2,1)S(1)} %get-tuple-element.61), channel_id=1, source_target_pairs={{0,14},{1,15},{2,0},{3,1},{4,2},{5,3},{6,4},{7,5},{8,6},{9,7},{10,... | collective-permute-start | bytes 786440 | tf_op jit(solution)/shard_map/ppermute | solution.py:413
  49.7 0.7 %reshape.11 = f32[8,2,1024]{2,1,0:T(2,128)} reshape(f32[16,1024]{1,0:T(8,128)S(1)} %pad_maximum_fusion) | data formatting | bytes 131072 | tf_op jit(solution)/shard_map/reshape | solution.py:462
  50.4 4.5 %all-to-all-start.1 = ((f32[8,2,1024]{2,1,0:T(2,128)}), f32[8,2,1024]{2,1,0:T(2,128)S(1)}, u32[]{:S(2)}, u32[]{:S(2)}) async-start(f32[8,2,1024]{2,1,0:T(2,128)} %reshape.11), calls=%async_computation.1 | async-start | bytes 131072 | tf_op jit(solution)/shard_map/all_to_all | solution.py:417
  55.0 2.5 %maximum_select_fusion = bf16[128,4096]{1,0:T(8,128)(2,1)} fusion(bf16[128,1024]{1,0:T(8,128)(2,1)} %collective-permute-done.9, bf16[128,1024]{1,0:T(8,128)(2,1)} %collective-permute-done.8, bf16[128,1024]{1,0:T(8,128)(2,1)S(1)} %get-tuple-element.46, bf16[128,1024]{1,0:T(8,128)(2,1)S(1)} %get-tuple-element.45, pred[]{:T(512)S(6)} %eq.4), kind=kLoop, calls=%fused_computation | loop fusion | flops 8912896 | bytes 2097153 | tf_op jit(solution)/shard_map/jit(_where)/select_n | solution.py:420
  57.4 0.6 maximum_select_fusion.1
  58.0 5.6 %all-to-all-done.1.strided = f32[8,2,1024]{2,1,0:T(2,128)S(1)} async-done(((f32[8,2,1024]{2,1,0:T(2,128)}), f32[8,2,1024]{2,1,0:T(2,128)S(1)}, u32[]{:S(2)}, u32[]{:S(2)}) %all-to-all-start.1) | async-done | bytes 65568 | tf_op jit(solution)/shard_map/all_to_all | solution.py:417
  64.4 0.8 %collective-permute-done.16.refs_3_ = bf16[128,512]{1,0:T(8,128)(2,1)S(1)} collective-permute-done((bf16[128,512]{1,0:T(8,128)(2,1)S(1)}, bf16[128,512]{1,0:T(8,128)(2,1)S(1)}, u32[]{:S(2)}, u32[]{:S(2)}) %collective-permute-start.16) | collective-permute-done | bytes 131104 | tf_op jit(solution)/shard_map/ppermute | solution.py:409
  65.4 0.9 %place.1 = (bf16[128,1024]{1,0:T(8,128)(2,1)}, bf16[128,1024]{1,0:T(8,128)(2,1)}) custom-call(bf16[128,512]{1,0:T(8,128)(2,1)S(1)} %get-tuple-element.57.refs_0_, bf16[128,512]{1,0:T(8,128)(2,1)S(1)} %collective-permute-done.13.refs_1_, bf16[128,512]{1,0:T(8,128)(2,1)S(1)} %get-tuple-element.63.refs_2_, bf16[128,512]{1,0:T(8,128)(2,1)S(1)} %collective-permute-done.16.refs_3_), custom_call_target="tpu_custom_call" | custom-call | tf_op jit(solution)/shard_map/place/pallas_call | solution.py:390
  (33 shorter events, 2.5 us)
Async XLA Ops:
  0.6 4.1 %copy-start = (bf16[128,4096]{1,0:T(8,128)(2,1)S(1)}, bf16[128,4096]{1,0:T(8,128)(2,1)}, u32[]{:S(2)}) copy-start(bf16[128,4096]{1,0:T(8,128)(2,1)} %q_own.3) | copy-start | bytes 3145732
  0.6 2.0 %collective-permute-start = (bf16[128,1024]{1,0:T(8,128)(2,1)}, bf16[128,1024]{1,0:T(8,128)(2,1)S(1)}, u32[]{:S(2)}, u32[]{:S(2)}) collective-permute-start(bf16[128,1024]{1,0:T(8,128)(2,1)} %keys.5), channel_id=1, source_target_pairs={{0,1},{1,0},{2,3},{3,2},{4,5},{5,4},{6,7},{7,6},{8,9},{9,8},{10,11... | collective-permute-start | bytes 786440 | tf_op jit(solution)/shard_map/ppermute | solution.py:409
  1.2 1.7 %collective-permute-start.1 = (bf16[128,1024]{1,0:T(8,128)(2,1)}, bf16[128,1024]{1,0:T(8,128)(2,1)S(1)}, u32[]{:S(2)}, u32[]{:S(2)}) collective-permute-start(bf16[128,1024]{1,0:T(8,128)(2,1)} %values.5), channel_id=1, source_target_pairs={{0,1},{1,0},{2,3},{3,2},{4,5},{5,4},{6,7},{7,6},{8,9},{9,8},{10,11... | collective-permute-start | bytes 786440 | tf_op jit(solution)/shard_map/ppermute | solution.py:409
  4.7 20.6 %collective-permute-start.2 = (bf16[128,4096]{1,0:T(8,128)(2,1)S(1)}, bf16[128,4096]{1,0:T(8,128)(2,1)S(1)}, u32[]{:S(2)}, u32[]{:S(2)}) collective-permute-start(bf16[128,4096]{1,0:T(8,128)(2,1)S(1)} %copy-done), channel_id=1, source_target_pairs={{0,1},{1,0},{2,3},{3,2},{4,5},{5,4},{6,7},{7,6},{8,9},{9,8},{10,11... | collective-permute-start | bytes 3145736 | tf_op jit(solution)/shard_map/ppermute | solution.py:409
  5.1 21.2 %collective-permute-start.3 = (bf16[128,4096]{1,0:T(8,128)(2,1)}, bf16[128,4096]{1,0:T(8,128)(2,1)}, u32[]{:S(2)}, u32[]{:S(2)}) collective-permute-start(bf16[128,4096]{1,0:T(8,128)(2,1)} %o_own.3), channel_id=1, source_target_pairs={{0,1},{1,0},{2,3},{3,2},{4,5},{5,4},{6,7},{7,6},{8,9},{9,8},{10,11... | collective-permute-start | bytes 3145736 | tf_op jit(solution)/shard_map/ppermute | solution.py:409
  5.2 19.5 %collective-permute-start.6 = (bf16[256,512]{1,0:T(8,128)(2,1)}, bf16[256,512]{1,0:T(8,128)(2,1)S(1)}, u32[]{:S(2)}, u32[]{:S(2)}) collective-permute-start(bf16[256,512]{1,0:T(8,128)(2,1)} %arrange_0.1.kv_here_in), channel_id=1, source_target_pairs={{0,2},{1,3},{2,4},{3,5},{4,6},{5,7},{6,8},{7,9},{8,10},{9,11},{10,... | collective-permute-start | bytes 786440 | tf_op jit(solution)/shard_map/ppermute | solution.py:413
  8.1 17.3 %collective-permute-start.7 = (bf16[256,512]{1,0:T(8,128)(2,1)}, bf16[256,512]{1,0:T(8,128)(2,1)S(1)}, u32[]{:S(2)}, u32[]{:S(2)}) collective-permute-start(bf16[256,512]{1,0:T(8,128)(2,1)} %arrange_0.1.kv_here_in), channel_id=1, source_target_pairs={{0,4},{1,5},{2,6},{3,7},{4,8},{5,9},{6,10},{7,11},{8,12},{9,13},{1... | collective-permute-start | bytes 786440 | tf_op jit(solution)/shard_map/ppermute | solution.py:413
  9.7 14.5 %all-to-all-start = ((bf16[16,8,128]{2,1,0:T(8,128)(2,1)}), bf16[16,8,128]{2,1,0:T(8,128)(2,1)S(1)}, u32[]{:S(2)}, u32[]{:S(2)}) async-start(bf16[16,8,128]{2,1,0:T(8,128)(2,1)} %own_rows.1), calls=%async_computation | async-start | bytes 65536 | tf_op jit(solution)/shard_map/all_to_all | solution.py:428
  24.1 12.1 %collective-permute-start.4 = (bf16[256,512]{1,0:T(8,128)(2,1)}, bf16[256,512]{1,0:T(8,128)(2,1)S(1)}, u32[]{:S(2)}, u32[]{:S(2)}) collective-permute-start(bf16[256,512]{1,0:T(8,128)(2,1)} %arrange_1.1.kv_here_in), channel_id=1, source_target_pairs={{0,2},{1,3},{2,4},{3,5},{4,6},{5,7},{6,8},{7,9},{8,10},{9,11},{10,... | collective-permute-start | bytes 786440 | tf_op jit(solution)/shard_map/ppermute | solution.py:413
  24.7 11.5 %collective-permute-start.5 = (bf16[256,512]{1,0:T(8,128)(2,1)}, bf16[256,512]{1,0:T(8,128)(2,1)S(1)}, u32[]{:S(2)}, u32[]{:S(2)}) collective-permute-start(bf16[256,512]{1,0:T(8,128)(2,1)} %arrange_1.1.kv_here_in), channel_id=1, source_target_pairs={{0,4},{1,5},{2,6},{3,7},{4,8},{5,9},{6,10},{7,11},{8,12},{9,13},{1... | collective-permute-start | bytes 786440 | tf_op jit(solution)/shard_map/ppermute | solution.py:413
  25.4 1.0 %copy-start.1 = (bf16[128,4096]{1,0:T(8,128)(2,1)}, bf16[128,4096]{1,0:T(8,128)(2,1)S(1)}, u32[]{:S(2)}) copy-start(bf16[128,4096]{1,0:T(8,128)(2,1)S(1)} %collective-permute-done.2.q_other) | copy-start | bytes 3145732
  32.6 17.0 %collective-permute-start.10 = (bf16[256,512]{1,0:T(8,128)(2,1)S(1)}, bf16[256,512]{1,0:T(8,128)(2,1)S(1)}, u32[]{:S(2)}, u32[]{:S(2)}) collective-permute-start(bf16[256,512]{1,0:T(8,128)(2,1)S(1)} %get-tuple-element.50), channel_id=1, source_target_pairs={{2,0},{3,1},{4,2},{5,3},{6,4},{7,5},{8,6},{9,7},{10,8},{11,9},{12,... | collective-permute-start | bytes 786440 | tf_op jit(solution)/shard_map/ppermute | solution.py:413
  33.9 15.8 %collective-permute-start.11 = (bf16[256,512]{1,0:T(8,128)(2,1)S(1)}, bf16[256,512]{1,0:T(8,128)(2,1)S(1)}, u32[]{:S(2)}, u32[]{:S(2)}) collective-permute-start(bf16[256,512]{1,0:T(8,128)(2,1)S(1)} %get-tuple-element.51), channel_id=1, source_target_pairs={{4,0},{5,1},{6,2},{7,3},{8,4},{9,5},{10,6},{11,7},{12,8},{13,9},{1... | collective-permute-start | bytes 786440 | tf_op jit(solution)/shard_map/ppermute | solution.py:413
  43.2 11.8 %collective-permute-start.9 = (bf16[128,1024]{1,0:T(8,128)(2,1)}, bf16[128,1024]{1,0:T(8,128)(2,1)}, u32[]{:S(2)}, u32[]{:S(2)}) collective-permute-start(bf16[128,1024]{1,0:T(8,128)(2,1)} %get-tuple-element.48), channel_id=1, source_target_pairs={{0,1},{1,0},{2,3},{3,2},{4,5},{5,4},{6,7},{7,6},{8,9},{9,8},{10,11... | collective-permute-start | bytes 786440 | tf_op jit(solution)/shard_map/ppermute | solution.py:409
  43.3 11.7 %collective-permute-start.8 = (bf16[128,1024]{1,0:T(8,128)(2,1)S(1)}, bf16[128,1024]{1,0:T(8,128)(2,1)}, u32[]{:S(2)}, u32[]{:S(2)}) collective-permute-start(bf16[128,1024]{1,0:T(8,128)(2,1)S(1)} %get-tuple-element.47), channel_id=1, source_target_pairs={{0,1},{1,0},{2,3},{3,2},{4,5},{5,4},{6,7},{7,6},{8,9},{9,8},{10,11... | collective-permute-start | bytes 786440 | tf_op jit(solution)/shard_map/ppermute | solution.py:409
  43.8 20.0 %collective-permute-start.14 = (bf16[256,512]{1,0:T(8,128)(2,1)S(1)}, bf16[256,512]{1,0:T(8,128)(2,1)S(1)}, u32[]{:S(2)}, u32[]{:S(2)}) collective-permute-start(bf16[256,512]{1,0:T(8,128)(2,1)S(1)} %get-tuple-element.61), channel_id=1, source_target_pairs={{0,14},{1,15},{2,0},{3,1},{4,2},{5,3},{6,4},{7,5},{8,6},{9,7},{10,... | collective-permute-start | bytes 786440 | tf_op jit(solution)/shard_map/ppermute | solution.py:413
  49.6 14.1 %collective-permute-start.15 = (bf16[256,512]{1,0:T(8,128)(2,1)S(1)}, bf16[256,512]{1,0:T(8,128)(2,1)S(1)}, u32[]{:S(2)}, u32[]{:S(2)}) collective-permute-start(bf16[256,512]{1,0:T(8,128)(2,1)S(1)} %get-tuple-element.62), channel_id=1, source_target_pairs={{0,12},{1,13},{2,14},{3,15},{4,0},{5,1},{6,2},{7,3},{8,4},{9,5},{1... | collective-permute-start | bytes 786440 | tf_op jit(solution)/shard_map/ppermute | solution.py:413
  50.4 13.2 %all-to-all-start.1 = ((f32[8,2,1024]{2,1,0:T(2,128)}), f32[8,2,1024]{2,1,0:T(2,128)S(1)}, u32[]{:S(2)}, u32[]{:S(2)}) async-start(f32[8,2,1024]{2,1,0:T(2,128)} %reshape.11), calls=%async_computation.1 | async-start | bytes 131072 | tf_op jit(solution)/shard_map/all_to_all | solution.py:417
  54.9 2.5 %collective-permute-start.12 = (f32[16,128]{1,0:T(8,128)S(1)}, f32[16,128]{1,0:T(8,128)S(1)}, u32[]{:S(2)}, u32[]{:S(2)}) collective-permute-start(f32[16,128]{1,0:T(8,128)S(1)} %get-tuple-element.52), channel_id=1, source_target_pairs={{0,1},{1,0},{2,3},{3,2},{4,5},{5,4},{6,7},{7,6},{8,9},{9,8},{10,11... | collective-permute-start | bytes 24584 | tf_op jit(solution)/shard_map/ppermute | solution.py:409
  63.8 1.4 %collective-permute-start.16 = (bf16[128,512]{1,0:T(8,128)(2,1)S(1)}, bf16[128,512]{1,0:T(8,128)(2,1)S(1)}, u32[]{:S(2)}, u32[]{:S(2)}) collective-permute-start(bf16[128,512]{1,0:T(8,128)(2,1)S(1)} %get-tuple-element.64), channel_id=1, source_target_pairs={{0,1},{1,0},{2,3},{3,2},{4,5},{5,4},{6,7},{7,6},{8,9},{9,8},{10,11... | collective-permute-start | bytes 393224 | tf_op jit(solution)/shard_map/ppermute | solution.py:409
  63.9 1.5 %collective-permute-start.13 = (bf16[128,512]{1,0:T(8,128)(2,1)S(1)}, bf16[128,512]{1,0:T(8,128)(2,1)S(1)}, u32[]{:S(2)}, u32[]{:S(2)}) collective-permute-start(bf16[128,512]{1,0:T(8,128)(2,1)S(1)} %get-tuple-element.59), channel_id=1, source_target_pairs={{0,1},{1,0},{2,3},{3,2},{4,5},{5,4},{6,7},{7,6},{8,9},{9,8},{10,11... | collective-permute-start | bytes 393224 | tf_op jit(solution)/shard_map/ppermute | solution.py:409

commit v6 on v5

--- a/solution.py
+++ b/solution.py
@@ -56,13 +56,11 @@
     )
 
 
-def attention_kernel(
+def attend(
     chunk,
-    q_own,
-    q_other,
-    o_own,
-    o_other,
-    kv_here_in,
+    staged_q,
+    staged_o,
+    here,
     kv_near,
     kv_past,
     kv_far,
@@ -73,13 +71,8 @@
     g_near,
     g_past,
     g_far,
-    q_held,
-    o_held,
-    here_held,
-    here_done,
-    held_done,
 ):
-    half = q_own.shape[0]
+    half = staged_q.shape[1]
     rows = 2 * half
     far_rows = kv_far.shape[0]
     both = 2 * HEAD_SIZE
@@ -87,31 +80,6 @@
     width = dq_own.shape[1]
     heads = width // (count * HEAD_SIZE)
     core, pair = pair_position()
-    here = here_held
-    loads = []
-    for at in range(count):
-        columns = slice(at * both, (at + 1) * both)
-        first = core * (count * CHUNKS) + chunk * count + at
-        for side in range(2):
-            batch = []
-            if side == 0:
-                batch.append(
-                    pltpu.make_async_copy(
-                        kv_here_in.at[:, columns], here_held.at[:, columns], here_done.at[at]
-                    )
-                )
-            for which in range(2):
-                source = (q_own, q_other, o_own, o_other)[2 * which + side]
-                batch.append(
-                    pltpu.make_async_copy(
-                        source.at[:, head_columns(first, heads * HEAD_SIZE)],
-                        (q_held, o_held)[which].at[at, side],
-                        held_done.at[at, side, which],
-                    )
-                )
-            loads.append(batch)
-    for copy in sum(loads, []):
-        copy.start()
     wide = (half, rows)
     lane = lax.broadcasted_iota(jnp.int32, wide, 1) % half
     lower = lax.broadcasted_iota(jnp.int32, wide, 0) <= lane
@@ -152,12 +120,12 @@
         query, grad = (
             jnp.concatenate(
                 [
-                    held[at, side, :, (first + k) * HEAD_SIZE : (first + k + 1) * HEAD_SIZE]
-                    for k in range(2)
+                    staged[side, :, head * HEAD_SIZE : (head + 1) * HEAD_SIZE]
+                    for head in (at * heads + first, at * heads + first + 1)
                 ],
                 axis=0,
             )
-            for held in (q_held, o_held)
+            for staged in (staged_q, staged_o)
         )
         key_all, value_all = keys_of(at, side, 0), keys_of(at, side, 1)
         return query, grad, key_all, dot_nt(key_all, query), dot_nt(value_all, grad)
@@ -212,8 +180,6 @@
         for side in range(2)
         for first in range(0, heads, 2)
     ]
-    for copy in sum(loads, []):
-        copy.wait()
     following = operands(*steps[0])
     terms = {}
     for number, (at, side, first) in enumerate(steps):
@@ -248,48 +214,83 @@
                 g_far[:, columns] = joint[rows:]
 
 
-def attention(queries, q_other, grad_out, o_other, kv_here, kv_near, kv_past, kv_far, chunk):
-    half = queries.shape[0]
+def stage_copies(chunk, sources, targets, done):
+    q_own, q_other, o_own, o_other = sources[:4]
+    staged_q, staged_o, here = targets
+    core, _ = pair_position()
+    columns = head_columns(core * CHUNKS + chunk, staged_q.shape[2])
+    pieces = [
+        (sources[4 + chunk], here),
+        (q_own.at[:, columns], staged_q.at[0]),
+        (o_own.at[:, columns], staged_o.at[0]),
+        (q_other.at[:, columns], staged_q.at[1]),
+        (o_other.at[:, columns], staged_o.at[1]),
+    ]
+    return [
+        pltpu.make_async_copy(source, target, done.at[chunk, number])
+        for number, (source, target) in enumerate(pieces)
+    ]
+
+
+def first_kernel(*refs):
+    sources, blocks, outs = refs[: 4 + CHUNKS], refs[4 + CHUNKS : 7 + CHUNKS], refs[7 + CHUNKS :]
+    mine, *later = (
+        stage_copies(chunk, sources, targets, outs[-1])
+        for chunk, targets in enumerate(
+            [outs[-4:-1]] + [outs[7 + 3 * k : 10 + 3 * k] for k in range(CHUNKS - 1)]
+        )
+    )
+    for copy in mine + sum(later, []):
+        copy.start()
+    for copy in mine:
+        copy.wait()
+    attend(0, *outs[-4:-1], *blocks, *outs[:7])
+    for copy in sum(later, []):
+        copy.wait()
+
+
+def attention(chunk, operands, kv_near, kv_past, kv_far, width):
+    half = kv_near.shape[0] // 2
     rows = 2 * half
     far_rows = kv_far.shape[0]
     both = 2 * HEAD_SIZE
-    count = kv_here.shape[1] // both
-    per_core = count * CHUNKS
-    group_width = queries.shape[1] // (2 * per_core)
-    heads = group_width // HEAD_SIZE
-
+    count = kv_near.shape[1] // both
+    heads = width // (count * HEAD_SIZE)
     whole = pl.BlockSpec(memory_space=pltpu.VMEM)
     keys_seen = 3 * rows + far_rows
+    staged = [(2, half, width), (2, half, width), (rows, count * both)]
+    outs = [
+        vmem_shape((half, width), jnp.bfloat16),
+        vmem_shape((half, width), jnp.bfloat16),
+        vmem_shape((count * heads, rows), jnp.float32),
+        vmem_shape((rows, count * both), jnp.float32),
+        vmem_shape((rows, count * both), jnp.bfloat16),
+        vmem_shape((rows, count * both), jnp.bfloat16),
+        vmem_shape((far_rows, count * both), jnp.float32),
+    ]
+    if chunk == 0:
+        outs += [vmem_shape(shape, jnp.bfloat16) for shape in staged] * (CHUNKS - 1)
+        operands = in_hbm(*operands)
+        scratch = [pltpu.VMEM(shape, jnp.bfloat16) for shape in staged]
+        scratch.append(pltpu.SemaphoreType.DMA((CHUNKS, 5)))
+    else:
+        operands = in_vmem(*operands)
+        scratch = []
+    space = pl.BlockSpec(memory_space=pl.ANY) if chunk == 0 else whole
     return pl.pallas_call(
-        functools.partial(attention_kernel, chunk),
+        first_kernel if chunk == 0 else functools.partial(attend, chunk),
         name=f"attention_{chunk}",
-        in_specs=[pl.BlockSpec(memory_space=pl.ANY)] * 5 + [whole] * 3,
-        out_specs=[whole] * 7,
-        out_shape=[
-            vmem_shape((half, count * group_width), jnp.bfloat16),
-            vmem_shape((half, count * group_width), jnp.bfloat16),
-            vmem_shape((count * heads, rows), jnp.float32),
-            vmem_shape((rows, count * both), jnp.float32),
-            vmem_shape((rows, count * both), jnp.bfloat16),
-            vmem_shape((rows, count * both), jnp.bfloat16),
-            vmem_shape((far_rows, count * both), jnp.float32),
-        ],
-        scratch_shapes=[
-            pltpu.VMEM((count, 2, half, group_width), jnp.bfloat16),
-            pltpu.VMEM((count, 2, half, group_width), jnp.bfloat16),
-            pltpu.VMEM((rows, count * both), jnp.bfloat16),
-            pltpu.SemaphoreType.DMA((count,)),
-            pltpu.SemaphoreType.DMA((count, 2, 2)),
-        ],
+        in_specs=[space] * len(operands) + [whole] * 3,
+        out_specs=[whole] * len(outs),
+        out_shape=outs,
+        scratch_shapes=scratch,
         compiler_params=pltpu.CompilerParams(vmem_limit_bytes=20 * 1024 * 1024),
         cost_estimate=pl.CostEstimate(
             flops=count * heads * rows * keys_seen * HEAD_SIZE * 20,
             transcendentals=count * heads * rows * keys_seen,
-            bytes_accessed=count * (6 * half * group_width * 2 + 5 * rows * both * 4),
+            bytes_accessed=6 * half * width * 2 + count * 5 * rows * both * 4,
         ),
-    )(
-        *in_hbm(queries, q_other, grad_out, o_other, kv_here), *in_vmem(kv_near, kv_past, kv_far)
-    )
+    )(*operands, *in_vmem(kv_near, kv_past, kv_far))
 
 
 def arrange_kernel(chunk, keys, values, k_other, v_other, payload):
@@ -437,19 +438,14 @@
     q_sent, o_sent, _ = lax.optimization_barrier((queries, grad_out, here[0]))
     q_other, o_other = swap(q_sent), swap(o_sent)
 
+    width = queries.shape[1] // (2 * CHUNKS)
+    operands = (queries, q_other, grad_out, o_other, *here)
     dq_own, dq_other, norms, sums, far_terms = [], [], [], [], []
     for chunk in range(CHUNKS):
-        out = attention(
-            queries,
-            q_other,
-            grad_out,
-            o_other,
-            here[chunk],
-            near[chunk],
-            past[chunk],
-            far,
-            chunk,
-        )
+        out = attention(chunk, operands, near[chunk], past[chunk], far, width)
+        if chunk == 0:
+            staged = out[7:]
+        operands = staged[3 * chunk : 3 * chunk + 3]
         last = chunk == CHUNKS - 1
         sums.append((out[3], shifted(out[4], -2, last), shifted(out[5], -4, last)))
         dq_own.append(out[0])

time: 66.8 us -> 65.6 us (0.982)
  Pallas kernels: 19.4 us -> 17.9 us
  local copies, waits for them, and re-layouts: 1.65 us -> 0.68 us
  waiting for transfers between devices: 15.9 us -> 16.7 us
    all_to_all x1, starting transfers between devices: 4.53 us -> 6.13 us  [exchanged(): return lax.all_to_all(x, 'ctx', 0, 0, axis_index_groups=groups)]
    pallas_call x2, Pallas kernels: 13.2 us -> 11.7 us  [attention(): pl.pallas_call(first_kernel if chunk == 0 else functools.partial(attend,...]
    ppermute x8, waiting for transfers between devices: 0.99 us -> 2.34 us  [shifted(): lax.ppermute(x, 'ctx', [(i, j) for i, j in pairs_sent if wrap or j == i +...]
    ppermute x8, starting transfers between devices: 14.2 us -> 13.2 us  [shifted(): lax.ppermute(x, 'ctx', [(i, j) for i, j in pairs_sent if wrap or j == i +...]
    unnamed x5 -> x3, local copies, waits for them, and re-layouts: 0.98 us -> 0.01 us
  transfers between devices with their start and end apart: 19 -> 19, of which waited for: 6 -> 7; matrix products, arithmetic and copies ran while one was open for 6% -> 6% of each run, Pallas kernels for 25% -> 23%
where the time goes in v6:
time: 65.6 us; the launch traced here: 65.2 us
  starting transfers between devices  26.1 us (40%)
  Pallas kernels  17.9 us (27%)
  waiting for transfers between devices  16.7 us (25%)
  other arithmetic  3.07 us (5%)
  between operations  0.77 us (1%)
  local copies, waits for them, and re-layouts  0.68 us (1%)
    ppermute x8, starting transfers between devices, shifted(): lax.ppermute(x, 'ctx', [(i, j) for i, j in pairs_sent if wrap or j == i +...  13.2 us
    pallas_call x2, Pallas kernels, attention(): pl.pallas_call(first_kernel if chunk == 0 else functools.partial(attend,...  11.7 us
    all_to_all x1, waiting for transfers between devices, local(): far = lax.all_to_all(sent, 'ctx', 0, 0, tiled=True)  8.05 us
    all_to_all x1, starting transfers between devices, exchanged(): return lax.all_to_all(x, 'ctx', 0, 0, axis_index_groups=groups)  6.13 us
    all_to_all x1, waiting for transfers between devices, exchanged(): return lax.all_to_all(x, 'ctx', 0, 0, axis_index_groups=groups)  5.04 us
    all_to_all x1, starting transfers between devices, local(): far = lax.all_to_all(sent, 'ctx', 0, 0, tiled=True)  4.61 us
    pallas_call x2, Pallas kernels, arrange(): pl.pallas_call(functools.partial(arrange_kernel, chunk), name=f'arrange_{...  3.6 us
    select_n x2, other arithmetic, joined(): jnp.where(core == 0, jnp.concatenate([mine, theirs], axis=1), jnp.concate...  3.06 us
  transfers between devices with their start and end apart: 19, of which 7 were waited for; matrix products, arithmetic and copies ran while one was open for 6% of the time, Pallas kernels for 23%

profile of v6, /device:TPU:0, one launch (start us, length us, event | category | flops | bytes accessed | tf_op | source)
XLA Modules:
  0.0 65.2 jit_solution(4029446291793465064)
XLA Ops:
  0.6 0.5 collective-permute-start
  1.2 1.4 %own_rows.1 = bf16[16,8,128]{2,1,0:T(8,128)(2,1)} custom-call(bf16[128,1024]{1,0:T(8,128)(2,1)} %keys.5, bf16[128,1024]{1,0:T(8,128)(2,1)} %values.5), custom_call_target="tpu_custom_call" | custom-call | tf_op jit(solution)/shard_map/own_rows/pallas_call | solution.py:337
  2.9 1.8 %arrange_0.1.refs_4_ = bf16[256,512]{1,0:T(8,128)(2,1)} custom-call(bf16[128,1024]{1,0:T(8,128)(2,1)} %keys.5, bf16[128,1024]{1,0:T(8,128)(2,1)} %values.5, bf16[128,1024]{1,0:T(8,128)(2,1)S(1)} %collective-permute-done.k_other, bf16[128,1024]{1,0:T(8,128)(2,1)S(1)} %collective-permute-done.1.v_other), custom_call_target="tpu_custom_call" | custom-call | tf_op jit(solution)/shard_map/arrange_0/pallas_call | solution.py:311
  5.2 2.9 %collective-permute-start.4 = (bf16[256,512]{1,0:T(8,128)(2,1)}, bf16[256,512]{1,0:T(8,128)(2,1)S(1)}, u32[]{:S(2)}, u32[]{:S(2)}) collective-permute-start(bf16[256,512]{1,0:T(8,128)(2,1)} %arrange_0.1.refs_4_), channel_id=1, source_target_pairs={{0,2},{1,3},{2,4},{3,5},{4,6},{5,7},{6,8},{7,9},{8,10},{9,11},{10,... | collective-permute-start | bytes 786440 | tf_op jit(solution)/shard_map/ppermute | solution.py:414
  8.1 1.6 %collective-permute-start.5 = (bf16[256,512]{1,0:T(8,128)(2,1)}, bf16[256,512]{1,0:T(8,128)(2,1)S(1)}, u32[]{:S(2)}, u32[]{:S(2)}) collective-permute-start(bf16[256,512]{1,0:T(8,128)(2,1)} %arrange_0.1.refs_4_), channel_id=1, source_target_pairs={{0,4},{1,5},{2,6},{3,7},{4,8},{5,9},{6,10},{7,11},{8,12},{9,13},{1... | collective-permute-start | bytes 786440 | tf_op jit(solution)/shard_map/ppermute | solution.py:414
  9.7 4.6 %all-to-all-start = ((bf16[16,8,128]{2,1,0:T(8,128)(2,1)}), bf16[16,8,128]{2,1,0:T(8,128)(2,1)S(1)}, u32[]{:S(2)}, u32[]{:S(2)}) async-start(bf16[16,8,128]{2,1,0:T(8,128)(2,1)} %own_rows.1), calls=%async_computation | async-start | bytes 65536 | tf_op jit(solution)/shard_map/all_to_all | solution.py:429
  14.3 1.8 %arrange_1.1.refs_5_ = bf16[256,512]{1,0:T(8,128)(2,1)} custom-call(bf16[128,1024]{1,0:T(8,128)(2,1)} %keys.5, bf16[128,1024]{1,0:T(8,128)(2,1)} %values.5, bf16[128,1024]{1,0:T(8,128)(2,1)S(1)} %collective-permute-done.k_other, bf16[128,1024]{1,0:T(8,128)(2,1)S(1)} %collective-permute-done.1.v_other), custom_call_target="tpu_custom_call" | custom-call | tf_op jit(solution)/shard_map/arrange_1/pallas_call | solution.py:311
  16.1 8.1 %all-to-all-done.refs_8_.kv_far = bf16[16,8,128]{2,1,0:T(8,128)(2,1)S(1)} async-done(((bf16[16,8,128]{2,1,0:T(8,128)(2,1)}), bf16[16,8,128]{2,1,0:T(8,128)(2,1)S(1)}, u32[]{:S(2)}, u32[]{:S(2)}) %all-to-all-start) | async-done | bytes 32800 | tf_op jit(solution)/shard_map/all_to_all | solution.py:429
  24.1 0.5 collective-permute-start.6
  24.7 0.7 %collective-permute-start.7 = (bf16[256,512]{1,0:T(8,128)(2,1)}, bf16[256,512]{1,0:T(8,128)(2,1)S(1)}, u32[]{:S(2)}, u32[]{:S(2)}) collective-permute-start(bf16[256,512]{1,0:T(8,128)(2,1)} %arrange_1.1.refs_5_), channel_id=1, source_target_pairs={{0,4},{1,5},{2,6},{3,7},{4,8},{5,9},{6,10},{7,11},{8,12},{9,13},{1... | collective-permute-start | bytes 786440 | tf_op jit(solution)/shard_map/ppermute | solution.py:414
  25.4 6.2 %attention_0.1 = (bf16[128,1024]{1,0:T(8,128)(2,1)S(1)}, bf16[128,1024]{1,0:T(8,128)(2,1)S(1)}, f32[8,256]{1,0:T(8,128)S(1)}, f32[256,512]{1,0:T(8,128)S(1)}, bf...) custom-call(bf16[128,4096]{1,0:T(8,128)(2,1)} %refs_0_.1, ...), custom_call_target="tpu_custom_call" | custom-call | flops 4110417920 | bytes 4194304 | tf_op jit(solution)/shard_map/attention_0/pallas_call | solution.py:280
  31.6 1.3 %collective-permute-start.10 = (bf16[256,512]{1,0:T(8,128)(2,1)S(1)}, bf16[256,512]{1,0:T(8,128)(2,1)S(1)}, u32[]{:S(2)}, u32[]{:S(2)}) collective-permute-start(bf16[256,512]{1,0:T(8,128)(2,1)S(1)} %get-tuple-element.56), channel_id=1, source_target_pairs={{2,0},{3,1},{4,2},{5,3},{6,4},{7,5},{8,6},{9,7},{10,8},{11,9},{12,... | collective-permute-start | bytes 786440 | tf_op jit(solution)/shard_map/ppermute | solution.py:414
  32.9 1.3 %collective-permute-start.11 = (bf16[256,512]{1,0:T(8,128)(2,1)S(1)}, bf16[256,512]{1,0:T(8,128)(2,1)S(1)}, u32[]{:S(2)}, u32[]{:S(2)}) collective-permute-start(bf16[256,512]{1,0:T(8,128)(2,1)S(1)} %get-tuple-element.57), channel_id=1, source_target_pairs={{4,0},{5,1},{6,2},{7,3},{8,4},{9,5},{10,6},{11,7},{12,8},{13,9},{1... | collective-permute-start | bytes 786440 | tf_op jit(solution)/shard_map/ppermute | solution.py:414
  34.2 2.0 %collective-permute-done.6.kv_near = bf16[256,512]{1,0:T(8,128)(2,1)S(1)} collective-permute-done((bf16[256,512]{1,0:T(8,128)(2,1)}, bf16[256,512]{1,0:T(8,128)(2,1)S(1)}, u32[]{:S(2)}, u32[]{:S(2)}) %collective-permute-start.6) | collective-permute-done | bytes 262176 | tf_op jit(solution)/shard_map/ppermute | solution.py:414
  36.2 5.6 %attention_1.1 = (bf16[128,1024]{1,0:T(8,128)(2,1)S(1)}, bf16[128,1024]{1,0:T(8,128)(2,1)}, f32[8,256]{1,0:T(8,128)S(1)}, f32[256,512]{1,0:T(8,128)S(1)}, bf16[2...) custom-call(bf16[2,128,1024]{2,1,0:T(8,128)(2,1)S(1)} %get-tuple-element.44.staged_q, ...), custom_call_target="tpu_custom_call" | custom-call | flops 4110417920 | bytes 4194304 | tf_op jit(solution)/shard_map/attention_1/pallas_call | solution.py:280
  41.8 0.5 collective-permute-start.8
  42.3 4.8 %collective-permute-start.14 = (bf16[256,512]{1,0:T(8,128)(2,1)S(1)}, bf16[256,512]{1,0:T(8,128)(2,1)S(1)}, u32[]{:S(2)}, u32[]{:S(2)}) collective-permute-start(bf16[256,512]{1,0:T(8,128)(2,1)S(1)} %get-tuple-element.67), channel_id=1, source_target_pairs={{0,14},{1,15},{2,0},{3,1},{4,2},{5,3},{6,4},{7,5},{8,6},{9,7},{10,... | collective-permute-start | bytes 786440 | tf_op jit(solution)/shard_map/ppermute | solution.py:414
  47.5 0.7 %reshape.11 = f32[8,2,1024]{2,1,0:T(2,128)} reshape(f32[16,1024]{1,0:T(8,128)S(1)} %pad_maximum_fusion) | data formatting | bytes 131072 | tf_op jit(solution)/shard_map/reshape | solution.py:458
  48.2 6.1 %all-to-all-start.1 = ((f32[8,2,1024]{2,1,0:T(2,128)}), f32[8,2,1024]{2,1,0:T(2,128)S(1)}, u32[]{:S(2)}, u32[]{:S(2)}) async-start(f32[8,2,1024]{2,1,0:T(2,128)} %reshape.11), calls=%async_computation.1 | async-start | bytes 131072 | tf_op jit(solution)/shard_map/all_to_all | solution.py:418
  54.4 2.5 %maximum_select_fusion = bf16[128,4096]{1,0:T(8,128)(2,1)} fusion(bf16[128,1024]{1,0:T(8,128)(2,1)} %collective-permute-done.9, bf16[128,1024]{1,0:T(8,128)(2,1)} %collective-permute-done.8, bf16[128,1024]{1,0:T(8,128)(2,1)S(1)} %get-tuple-element.52, bf16[128,1024]{1,0:T(8,128)(2,1)S(1)} %get-tuple-element.51, pred[]{:T(512)S(6)} %eq.4), kind=kLoop, calls=%fused_computation | loop fusion | flops 8912896 | bytes 2097153 | tf_op jit(solution)/shard_map/jit(_where)/select_n | solution.py:421
  56.8 0.6 maximum_select_fusion.1
  57.4 5.0 %all-to-all-done.1.strided = f32[8,2,1024]{2,1,0:T(2,128)S(1)} async-done(((f32[8,2,1024]{2,1,0:T(2,128)}), f32[8,2,1024]{2,1,0:T(2,128)S(1)}, u32[]{:S(2)}, u32[]{:S(2)}) %all-to-all-start.1) | async-done | bytes 65568 | tf_op jit(solution)/shard_map/all_to_all | solution.py:418
  63.3 0.8 %collective-permute-done.16.refs_3_ = bf16[128,512]{1,0:T(8,128)(2,1)S(1)} collective-permute-done((bf16[128,512]{1,0:T(8,128)(2,1)S(1)}, bf16[128,512]{1,0:T(8,128)(2,1)S(1)}, u32[]{:S(2)}, u32[]{:S(2)}) %collective-permute-start.16) | collective-permute-done | bytes 131104 | tf_op jit(solution)/shard_map/ppermute | solution.py:410
  64.3 0.9 %place.1 = (bf16[128,1024]{1,0:T(8,128)(2,1)}, bf16[128,1024]{1,0:T(8,128)(2,1)}) custom-call(bf16[128,512]{1,0:T(8,128)(2,1)S(1)} %get-tuple-element.63.refs_0_, bf16[128,512]{1,0:T(8,128)(2,1)S(1)} %collective-permute-done.13.refs_1_, bf16[128,512]{1,0:T(8,128)(2,1)S(1)} %get-tuple-element.69.refs_2_, bf16[128,512]{1,0:T(8,128)(2,1)S(1)} %collective-permute-done.16.refs_3_), custom_call_target="tpu_custom_call" | custom-call | tf_op jit(solution)/shard_map/place/pallas_call | solution.py:391
  (31 shorter events, 2.3 us)
Async XLA Ops:
  0.6 4.1 %copy-start = (bf16[128,4096]{1,0:T(8,128)(2,1)S(1)}, bf16[128,4096]{1,0:T(8,128)(2,1)}, u32[]{:S(2)}) copy-start(bf16[128,4096]{1,0:T(8,128)(2,1)} %refs_0_.1) | copy-start | bytes 3145732
  0.6 2.0 %collective-permute-start = (bf16[128,1024]{1,0:T(8,128)(2,1)}, bf16[128,1024]{1,0:T(8,128)(2,1)S(1)}, u32[]{:S(2)}, u32[]{:S(2)}) collective-permute-start(bf16[128,1024]{1,0:T(8,128)(2,1)} %keys.5), channel_id=1, source_target_pairs={{0,1},{1,0},{2,3},{3,2},{4,5},{5,4},{6,7},{7,6},{8,9},{9,8},{10,11... | collective-permute-start | bytes 786440 | tf_op jit(solution)/shard_map/ppermute | solution.py:410
  1.2 1.7 %collective-permute-start.1 = (bf16[128,1024]{1,0:T(8,128)(2,1)}, bf16[128,1024]{1,0:T(8,128)(2,1)S(1)}, u32[]{:S(2)}, u32[]{:S(2)}) collective-permute-start(bf16[128,1024]{1,0:T(8,128)(2,1)} %values.5), channel_id=1, source_target_pairs={{0,1},{1,0},{2,3},{3,2},{4,5},{5,4},{6,7},{7,6},{8,9},{9,8},{10,11... | collective-permute-start | bytes 786440 | tf_op jit(solution)/shard_map/ppermute | solution.py:410
  4.7 20.6 %collective-permute-start.2 = (bf16[128,4096]{1,0:T(8,128)(2,1)S(1)}, bf16[128,4096]{1,0:T(8,128)(2,1)}, u32[]{:S(2)}, u32[]{:S(2)}) collective-permute-start(bf16[128,4096]{1,0:T(8,128)(2,1)S(1)} %copy-done), channel_id=1, source_target_pairs={{0,1},{1,0},{2,3},{3,2},{4,5},{5,4},{6,7},{7,6},{8,9},{9,8},{10,11... | collective-permute-start | bytes 3145736 | tf_op jit(solution)/shard_map/ppermute | solution.py:410
  5.1 20.3 %collective-permute-start.3 = (bf16[128,4096]{1,0:T(8,128)(2,1)}, bf16[128,4096]{1,0:T(8,128)(2,1)}, u32[]{:S(2)}, u32[]{:S(2)}) collective-permute-start(bf16[128,4096]{1,0:T(8,128)(2,1)} %refs_2_.1), channel_id=1, source_target_pairs={{0,1},{1,0},{2,3},{3,2},{4,5},{5,4},{6,7},{7,6},{8,9},{9,8},{10,11... | collective-permute-start | bytes 3145736 | tf_op jit(solution)/shard_map/ppermute | solution.py:410
  5.2 19.5 %collective-permute-start.4 = (bf16[256,512]{1,0:T(8,128)(2,1)}, bf16[256,512]{1,0:T(8,128)(2,1)S(1)}, u32[]{:S(2)}, u32[]{:S(2)}) collective-permute-start(bf16[256,512]{1,0:T(8,128)(2,1)} %arrange_0.1.refs_4_), channel_id=1, source_target_pairs={{0,2},{1,3},{2,4},{3,5},{4,6},{5,7},{6,8},{7,9},{8,10},{9,11},{10,... | collective-permute-start | bytes 786440 | tf_op jit(solution)/shard_map/ppermute | solution.py:414
  8.1 17.3 %collective-permute-start.5 = (bf16[256,512]{1,0:T(8,128)(2,1)}, bf16[256,512]{1,0:T(8,128)(2,1)S(1)}, u32[]{:S(2)}, u32[]{:S(2)}) collective-permute-start(bf16[256,512]{1,0:T(8,128)(2,1)} %arrange_0.1.refs_4_), channel_id=1, source_target_pairs={{0,4},{1,5},{2,6},{3,7},{4,8},{5,9},{6,10},{7,11},{8,12},{9,13},{1... | collective-permute-start | bytes 786440 | tf_op jit(solution)/shard_map/ppermute | solution.py:414
  9.7 14.5 %all-to-all-start = ((bf16[16,8,128]{2,1,0:T(8,128)(2,1)}), bf16[16,8,128]{2,1,0:T(8,128)(2,1)S(1)}, u32[]{:S(2)}, u32[]{:S(2)}) async-start(bf16[16,8,128]{2,1,0:T(8,128)(2,1)} %own_rows.1), calls=%async_computation | async-start | bytes 65536 | tf_op jit(solution)/shard_map/all_to_all | solution.py:429
  24.1 12.1 %collective-permute-start.6 = (bf16[256,512]{1,0:T(8,128)(2,1)}, bf16[256,512]{1,0:T(8,128)(2,1)S(1)}, u32[]{:S(2)}, u32[]{:S(2)}) collective-permute-start(bf16[256,512]{1,0:T(8,128)(2,1)} %arrange_1.1.refs_5_), channel_id=1, source_target_pairs={{0,2},{1,3},{2,4},{3,5},{4,6},{5,7},{6,8},{7,9},{8,10},{9,11},{10,... | collective-permute-start | bytes 786440 | tf_op jit(solution)/shard_map/ppermute | solution.py:414
  24.7 11.5 %collective-permute-start.7 = (bf16[256,512]{1,0:T(8,128)(2,1)}, bf16[256,512]{1,0:T(8,128)(2,1)S(1)}, u32[]{:S(2)}, u32[]{:S(2)}) collective-permute-start(bf16[256,512]{1,0:T(8,128)(2,1)} %arrange_1.1.refs_5_), channel_id=1, source_target_pairs={{0,4},{1,5},{2,6},{3,7},{4,8},{5,9},{6,10},{7,11},{8,12},{9,13},{1... | collective-permute-start | bytes 786440 | tf_op jit(solution)/shard_map/ppermute | solution.py:414
  31.6 15.5 %collective-permute-start.10 = (bf16[256,512]{1,0:T(8,128)(2,1)S(1)}, bf16[256,512]{1,0:T(8,128)(2,1)S(1)}, u32[]{:S(2)}, u32[]{:S(2)}) collective-permute-start(bf16[256,512]{1,0:T(8,128)(2,1)S(1)} %get-tuple-element.56), channel_id=1, source_target_pairs={{2,0},{3,1},{4,2},{5,3},{6,4},{7,5},{8,6},{9,7},{10,8},{11,9},{12,... | collective-permute-start | bytes 786440 | tf_op jit(solution)/shard_map/ppermute | solution.py:414
  32.9 14.7 %collective-permute-start.11 = (bf16[256,512]{1,0:T(8,128)(2,1)S(1)}, bf16[256,512]{1,0:T(8,128)(2,1)S(1)}, u32[]{:S(2)}, u32[]{:S(2)}) collective-permute-start(bf16[256,512]{1,0:T(8,128)(2,1)S(1)} %get-tuple-element.57), channel_id=1, source_target_pairs={{4,0},{5,1},{6,2},{7,3},{8,4},{9,5},{10,6},{11,7},{12,8},{13,9},{1... | collective-permute-start | bytes 786440 | tf_op jit(solution)/shard_map/ppermute | solution.py:414
  41.8 12.6 %collective-permute-start.9 = (bf16[128,1024]{1,0:T(8,128)(2,1)}, bf16[128,1024]{1,0:T(8,128)(2,1)}, u32[]{:S(2)}, u32[]{:S(2)}) collective-permute-start(bf16[128,1024]{1,0:T(8,128)(2,1)} %get-tuple-element.54), channel_id=1, source_target_pairs={{0,1},{1,0},{2,3},{3,2},{4,5},{5,4},{6,7},{7,6},{8,9},{9,8},{10,11... | collective-permute-start | bytes 786440 | tf_op jit(solution)/shard_map/ppermute | solution.py:410
  41.8 12.6 %collective-permute-start.8 = (bf16[128,1024]{1,0:T(8,128)(2,1)S(1)}, bf16[128,1024]{1,0:T(8,128)(2,1)}, u32[]{:S(2)}, u32[]{:S(2)}) collective-permute-start(bf16[128,1024]{1,0:T(8,128)(2,1)S(1)} %get-tuple-element.53), channel_id=1, source_target_pairs={{0,1},{1,0},{2,3},{3,2},{4,5},{5,4},{6,7},{7,6},{8,9},{9,8},{10,11... | collective-permute-start | bytes 786440 | tf_op jit(solution)/shard_map/ppermute | solution.py:410
  42.3 20.3 %collective-permute-start.14 = (bf16[256,512]{1,0:T(8,128)(2,1)S(1)}, bf16[256,512]{1,0:T(8,128)(2,1)S(1)}, u32[]{:S(2)}, u32[]{:S(2)}) collective-permute-start(bf16[256,512]{1,0:T(8,128)(2,1)S(1)} %get-tuple-element.67), channel_id=1, source_target_pairs={{0,14},{1,15},{2,0},{3,1},{4,2},{5,3},{6,4},{7,5},{8,6},{9,7},{10,... | collective-permute-start | bytes 786440 | tf_op jit(solution)/shard_map/ppermute | solution.py:414
  47.1 15.5 %collective-permute-start.15 = (bf16[256,512]{1,0:T(8,128)(2,1)S(1)}, bf16[256,512]{1,0:T(8,128)(2,1)S(1)}, u32[]{:S(2)}, u32[]{:S(2)}) collective-permute-start(bf16[256,512]{1,0:T(8,128)(2,1)S(1)} %get-tuple-element.68), channel_id=1, source_target_pairs={{0,12},{1,13},{2,14},{3,15},{4,0},{5,1},{6,2},{7,3},{8,4},{9,5},{1... | collective-permute-start | bytes 786440 | tf_op jit(solution)/shard_map/ppermute | solution.py:414
  48.2 14.3 %all-to-all-start.1 = ((f32[8,2,1024]{2,1,0:T(2,128)}), f32[8,2,1024]{2,1,0:T(2,128)S(1)}, u32[]{:S(2)}, u32[]{:S(2)}) async-start(f32[8,2,1024]{2,1,0:T(2,128)} %reshape.11), calls=%async_computation.1 | async-start | bytes 131072 | tf_op jit(solution)/shard_map/all_to_all | solution.py:418
  54.3 2.5 %collective-permute-start.12 = (f32[16,128]{1,0:T(8,128)S(1)}, f32[16,128]{1,0:T(8,128)S(1)}, u32[]{:S(2)}, u32[]{:S(2)}) collective-permute-start(f32[16,128]{1,0:T(8,128)S(1)} %get-tuple-element.58), channel_id=1, source_target_pairs={{0,1},{1,0},{2,3},{3,2},{4,5},{5,4},{6,7},{7,6},{8,9},{9,8},{10,11... | collective-permute-start | bytes 24584 | tf_op jit(solution)/shard_map/ppermute | solution.py:410
  62.7 1.4 %collective-permute-start.16 = (bf16[128,512]{1,0:T(8,128)(2,1)S(1)}, bf16[128,512]{1,0:T(8,128)(2,1)S(1)}, u32[]{:S(2)}, u32[]{:S(2)}) collective-permute-start(bf16[128,512]{1,0:T(8,128)(2,1)S(1)} %get-tuple-element.70), channel_id=1, source_target_pairs={{0,1},{1,0},{2,3},{3,2},{4,5},{5,4},{6,7},{7,6},{8,9},{9,8},{10,11... | collective-permute-start | bytes 393224 | tf_op jit(solution)/shard_map/ppermute | solution.py:410
  62.8 1.5 %collective-permute-start.13 = (bf16[128,512]{1,0:T(8,128)(2,1)S(1)}, bf16[128,512]{1,0:T(8,128)(2,1)S(1)}, u32[]{:S(2)}, u32[]{:S(2)}) collective-permute-start(bf16[128,512]{1,0:T(8,128)(2,1)S(1)} %get-tuple-element.65), channel_id=1, source_target_pairs={{0,1},{1,0},{2,3},{3,2},{4,5},{5,4},{6,7},{7,6},{8,9},{9,8},{10,11... | collective-permute-start | bytes 393224 | tf_op jit(solution)/shard_map/ppermute | solution.py:410

commit v7 on v6

--- a/solution.py
+++ b/solution.py
@@ -211,7 +211,7 @@
                     ).astype(jnp.bfloat16)
                 joint = own[rows + half :] + other[rows + half :]
                 g_near[:, columns] = joint[:rows].astype(jnp.bfloat16)
-                g_far[:, columns] = joint[rows:]
+                g_far[:, 2 * (chunk * count + at) + which, :] = joint[rows:]
 
 
 def stage_copies(chunk, sources, targets, done):
@@ -249,7 +249,13 @@
         copy.wait()
 
 
-def attention(chunk, operands, kv_near, kv_past, kv_far, width):
+def later_kernel(chunk, *refs):
+    before, g_far = refs[6], refs[-1]
+    g_far[:, : before.shape[1], :] = before[...]
+    attend(chunk, *refs[:6], *refs[7:])
+
+
+def attention(chunk, operands, kv_near, kv_past, kv_far, far_terms, width):
     half = kv_near.shape[0] // 2
     rows = 2 * half
     far_rows = kv_far.shape[0]
@@ -266,8 +272,9 @@
         vmem_shape((rows, count * both), jnp.float32),
         vmem_shape((rows, count * both), jnp.bfloat16),
         vmem_shape((rows, count * both), jnp.bfloat16),
-        vmem_shape((far_rows, count * both), jnp.float32),
+        vmem_shape((far_rows, 2 * count * (chunk + 1), HEAD_SIZE), jnp.float32),
     ]
+    blocks = [kv_near, kv_past, kv_far]
     if chunk == 0:
         outs += [vmem_shape(shape, jnp.bfloat16) for shape in staged] * (CHUNKS - 1)
         operands = in_hbm(*operands)
@@ -275,12 +282,13 @@
         scratch.append(pltpu.SemaphoreType.DMA((CHUNKS, 5)))
     else:
         operands = in_vmem(*operands)
+        blocks.append(far_terms)
         scratch = []
     space = pl.BlockSpec(memory_space=pl.ANY) if chunk == 0 else whole
     return pl.pallas_call(
-        first_kernel if chunk == 0 else functools.partial(attend, chunk),
+        first_kernel if chunk == 0 else functools.partial(later_kernel, chunk),
         name=f"attention_{chunk}",
-        in_specs=[space] * len(operands) + [whole] * 3,
+        in_specs=[space] * len(operands) + [whole] * len(blocks),
         out_specs=[whole] * len(outs),
         out_shape=outs,
         scratch_shapes=scratch,
@@ -290,7 +298,7 @@
             transcendentals=count * heads * rows * keys_seen,
             bytes_accessed=6 * half * width * 2 + count * 5 * rows * both * 4,
         ),
-    )(*operands, *in_vmem(kv_near, kv_past, kv_far))
+    )(*operands, *in_vmem(*blocks))
 
 
 def arrange_kernel(chunk, keys, values, k_other, v_other, payload):
@@ -344,57 +352,72 @@
     )(keys, values)
 
 
-def collect_kernel(chunk, here, near, past, strided, mine, theirs):
-    half, width = mine.shape
+def collect_kernel(*refs):
+    *terms, strided, mine, theirs = refs
+    half = mine.shape[0]
+    width = terms[0].shape[1]
     core, _ = pair_position()
-    extra = jnp.sum(strided[:, :, chunk * width : (chunk + 1) * width], axis=0)
-    extra = jnp.where(core == 0, extra, jnp.concatenate([extra[1:2], extra[0:1]], axis=0))
-    total = here[...] + near[...].astype(jnp.float32) + past[...].astype(jnp.float32)
+    own, other = (
+        jnp.concatenate(
+            [
+                jnp.sum(strided[:, k, column, :], axis=0, keepdims=True)
+                for column in range(strided.shape[2])
+            ],
+            axis=1,
+        )
+        for k in range(2)
+    )
+    extra = jnp.where(
+        core == 0, jnp.concatenate([own, other], axis=0), jnp.concatenate([other, own], axis=0)
+    )
     row = lax.broadcasted_iota(jnp.int32, (half, 1), 0)
-    mine[...] = (total[:half] + jnp.where(row == 0, extra[0:1], 0.0)).astype(mine.dtype)
-    theirs[...] = (total[half:] + jnp.where(row == 0, extra[1:2], 0.0)).astype(theirs.dtype)
-
-
-def collect(here, near, past, strided, chunk):
-    rows, width = here.shape
-    half = vmem_shape((rows // 2, width), jnp.bfloat16)
+    for chunk in range(CHUNKS):
+        here, near, past = terms[3 * chunk : 3 * chunk + 3]
+        columns = slice(chunk * width, (chunk + 1) * width)
+        total = here[...] + near[...].astype(jnp.float32) + past[...].astype(jnp.float32)
+        for k, out in enumerate((mine, theirs)):
+            added = jnp.where(row == 0, extra[k : k + 1, columns], 0.0)
+            out[:, columns] = (total[k * half : (k + 1) * half] + added).astype(out.dtype)
+
+
+def collect(terms, strided):
+    rows, width = terms[0].shape
+    half = vmem_shape((rows // 2, CHUNKS * width), jnp.bfloat16)
     whole = pl.BlockSpec(memory_space=pltpu.VMEM)
     return pl.pallas_call(
-        functools.partial(collect_kernel, chunk),
-        name=f"collect_{chunk}",
-        in_specs=[whole] * 4,
+        collect_kernel,
+        name="collect",
+        in_specs=[whole] * (len(terms) + 1),
         out_specs=[whole, whole],
         out_shape=[half, half],
         cost_estimate=pl.CostEstimate(
-            flops=rows * width * 4, transcendentals=0, bytes_accessed=rows * width * 10
+            flops=CHUNKS * rows * width * 4,
+            transcendentals=0,
+            bytes_accessed=CHUNKS * rows * width * 10,
         ),
-    )(*in_vmem(here, near, past, strided))
-
-
-def place_kernel(*refs):
+    )(*in_vmem(*terms, strided))
+
+
+def place_kernel(mine, theirs, grad_keys, grad_values):
     here, _ = pair_position()
-    *parts, grad_keys, grad_values = refs
-    count = parts[0].shape[1] // (2 * HEAD_SIZE)
-    for chunk in range(CHUNKS):
-        mine, theirs = parts[2 * chunk : 2 * chunk + 2]
-        for h in range(count):
-            at = chunk * count + h
-            for core, block in ((here, mine), (1 - here, theirs)):
-                to = head_columns(core * (count * CHUNKS) + at)
-                grad_keys[:, to] = block[:, 2 * h * HEAD_SIZE : (2 * h + 1) * HEAD_SIZE]
-                grad_values[:, to] = block[:, (2 * h + 1) * HEAD_SIZE : (2 * h + 2) * HEAD_SIZE]
-
-
-def placed_grads(parts, half, kv_width):
+    count = mine.shape[1] // (2 * HEAD_SIZE)
+    for h in range(count):
+        for core, block in ((here, mine), (1 - here, theirs)):
+            to = head_columns(core * count + h)
+            grad_keys[:, to] = block[:, 2 * h * HEAD_SIZE : (2 * h + 1) * HEAD_SIZE]
+            grad_values[:, to] = block[:, (2 * h + 1) * HEAD_SIZE : (2 * h + 2) * HEAD_SIZE]
+
+
+def placed_grads(mine, theirs):
     whole = pl.BlockSpec(memory_space=pltpu.VMEM)
-    out = jax.ShapeDtypeStruct((half, kv_width), jnp.bfloat16)
+    out = jax.ShapeDtypeStruct(mine.shape, jnp.bfloat16)
     return pl.pallas_call(
         place_kernel,
         name="place",
-        in_specs=[whole] * len(parts),
+        in_specs=[whole, whole],
         out_specs=[whole, whole],
         out_shape=[out, out],
-    )(*in_vmem(*parts))
+    )(*in_vmem(mine, theirs))
 
 
 def local(queries, keys, values, grad_out):
@@ -440,9 +463,10 @@
 
     width = queries.shape[1] // (2 * CHUNKS)
     operands = (queries, q_other, grad_out, o_other, *here)
-    dq_own, dq_other, norms, sums, far_terms = [], [], [], [], []
+    dq_own, dq_other, norms, sums = [], [], [], []
+    far_terms = None
     for chunk in range(CHUNKS):
-        out = attention(chunk, operands, near[chunk], past[chunk], far, width)
+        out = attention(chunk, operands, near[chunk], past[chunk], far, far_terms, width)
         if chunk == 0:
             staged = out[7:]
         operands = staged[3 * chunk : 3 * chunk + 3]
@@ -452,23 +476,18 @@
         dq_other.append(swap(out[1]))
         norms.append(out[2])
         far, _ = lax.optimization_barrier((far, out[2]))
-        far_terms.append(out[6])
-
-    terms, *_ = lax.optimization_barrier((jnp.concatenate(far_terms, axis=1), *sums[0][1:]))
-    strided_terms = exchanged(terms.reshape(pairs, 2, kv_width))
+        far_terms = out[6]
+
+    terms, *_ = lax.optimization_barrier((far_terms, *sums[0][1:]))
+    strided_terms = exchanged(terms.reshape(pairs, 2, kv_heads, HEAD_SIZE))
     grad_queries = joined(jnp.concatenate(dq_own, axis=1), jnp.concatenate(dq_other, axis=1))
     norm = jnp.concatenate(norms, axis=0)
     norm_sent, *_ = lax.optimization_barrier((norm[:, half:], *sums[0][1:]))
     log_norm = joined(norm[:, :half].T, swap(norm_sent).T)
-    parts = []
-    for chunk, (own, near_terms, past_terms) in enumerate(sums):
-        if chunk > 0:
-            own, grad_queries, log_norm, _ = lax.optimization_barrier(
-                (own, grad_queries, log_norm, parts[-2])
-            )
-        mine, theirs = collect(own, near_terms, past_terms, strided_terms, chunk)
-        parts += [mine, swap(theirs)]
-    grad_keys, grad_values = placed_grads(parts, half, kv_width)
+    own, grad_queries, log_norm = lax.optimization_barrier((sums[-1][0], grad_queries, log_norm))
+    terms = [x for chunk in sums[:-1] for x in chunk] + [own, *sums[-1][1:]]
+    mine, theirs = collect(terms, strided_terms)
+    grad_keys, grad_values = placed_grads(mine, swap(theirs))
     return (grad_queries, grad_keys, grad_values, log_norm)
 
 

time: 65.6 us -> 65.6 us (level)
  waiting for transfers between devices: 16.7 us -> 17.9 us
  local copies, waits for them, and re-layouts: 0.68 us -> 0.02 us
    ppermute x8, waiting for transfers between devices: 2.34 us -> 7.34 us  [shifted(): lax.ppermute(x, 'ctx', [(i, j) for i, j in pairs_sent if wrap or j == i +...]
    all_to_all x1, waiting for transfers between devices: 5.04 us -> 0.72 us  [exchanged(): return lax.all_to_all(x, 'ctx', 0, 0, axis_index_groups=groups)]
    reshape x1 -> x0, local copies, waits for them, and re-layouts: 0.67 us -> none  [local(): strided_terms = exchanged(terms.reshape(pairs, 2, kv_width))]
    ppermute x9 -> x8, waiting for transfers between devices: 1.3 us -> 1.8 us  [swap(): return lax.ppermute(x, 'ctx', [(i, i ^ 1) for i in range(peers)])]
    ppermute x9 -> x8, starting transfers between devices: 2.19 us -> 1.69 us  [swap(): return lax.ppermute(x, 'ctx', [(i, i ^ 1) for i in range(peers)])]
    pallas_call x5 -> x4, Pallas kernels: 12.9 us -> 12.9 us  [the longest x2 11.7 us: attention(): pl.pallas_call(first_kernel if chunk == 0 else functools.partial(later_ke...]
  transfers between devices with their start and end apart: 19 -> 18, of which waited for: 7 -> 7; matrix products, arithmetic and copies ran while one was open for 6% -> 5% of each run, Pallas kernels for 23% -> 23%
where the time goes in v7:
time: 65.6 us; the launch traced here: 65.2 us
  starting transfers between devices  25.6 us (39%)
  Pallas kernels  17.9 us (27%)
  waiting for transfers between devices  17.9 us (27%)
  other arithmetic  3.07 us (5%)
  between operations  0.74 us (1%)
    ppermute x8, starting transfers between devices, shifted(): lax.ppermute(x, 'ctx', [(i, j) for i, j in pairs_sent if wrap or j == i +...  13.2 us
    pallas_call x2, Pallas kernels, attention(): pl.pallas_call(first_kernel if chunk == 0 else functools.partial(later_ke...  11.7 us
    all_to_all x1, waiting for transfers between devices, local(): far = lax.all_to_all(sent, 'ctx', 0, 0, tiled=True)  8.05 us
    ppermute x8, waiting for transfers between devices, shifted(): lax.ppermute(x, 'ctx', [(i, j) for i, j in pairs_sent if wrap or j == i +...  7.34 us
    all_to_all x1, starting transfers between devices, exchanged(): return lax.all_to_all(x, 'ctx', 0, 0, axis_index_groups=groups)  6.13 us
    all_to_all x1, starting transfers between devices, local(): far = lax.all_to_all(sent, 'ctx', 0, 0, tiled=True)  4.61 us
    pallas_call x2, Pallas kernels, arrange(): pl.pallas_call(functools.partial(arrange_kernel, chunk), name=f'arrange_{...  3.6 us
    select_n x2, other arithmetic, joined(): jnp.where(core == 0, jnp.concatenate([mine, theirs], axis=1), jnp.concate...  3.07 us
  transfers between devices with their start and end apart: 18, of which 7 were waited for; matrix products, arithmetic and copies ran while one was open for 5% of the time, Pallas kernels for 23%

profile of v7, /device:TPU:0, one launch (start us, length us, event | category | flops | bytes accessed | tf_op | source)
XLA Modules:
  0.0 65.2 jit_solution(7627663366025225055)
XLA Ops:
  0.6 0.5 collective-permute-start
  1.2 1.4 %own_rows.1 = bf16[16,8,128]{2,1,0:T(8,128)(2,1)} custom-call(bf16[128,1024]{1,0:T(8,128)(2,1)} %keys.5, bf16[128,1024]{1,0:T(8,128)(2,1)} %values.5), custom_call_target="tpu_custom_call" | custom-call | tf_op jit(solution)/shard_map/own_rows/pallas_call | solution.py:345
  2.9 1.8 %arrange_0.1.refs_4_ = bf16[256,512]{1,0:T(8,128)(2,1)} custom-call(bf16[128,1024]{1,0:T(8,128)(2,1)} %keys.5, bf16[128,1024]{1,0:T(8,128)(2,1)} %values.5, bf16[128,1024]{1,0:T(8,128)(2,1)S(1)} %collective-permute-done.k_other, bf16[128,1024]{1,0:T(8,128)(2,1)S(1)} %collective-permute-done.1.v_other), custom_call_target="tpu_custom_call" | custom-call | tf_op jit(solution)/shard_map/arrange_0/pallas_call | solution.py:319
  5.2 2.9 %collective-permute-start.4 = (bf16[256,512]{1,0:T(8,128)(2,1)}, bf16[256,512]{1,0:T(8,128)(2,1)S(1)}, u32[]{:S(2)}, u32[]{:S(2)}) collective-permute-start(bf16[256,512]{1,0:T(8,128)(2,1)} %arrange_0.1.refs_4_), channel_id=1, source_target_pairs={{0,2},{1,3},{2,4},{3,5},{4,6},{5,7},{6,8},{7,9},{8,10},{9,11},{10,... | collective-permute-start | bytes 786440 | tf_op jit(solution)/shard_map/ppermute | solution.py:437
  8.1 1.6 %collective-permute-start.5 = (bf16[256,512]{1,0:T(8,128)(2,1)}, bf16[256,512]{1,0:T(8,128)(2,1)S(1)}, u32[]{:S(2)}, u32[]{:S(2)}) collective-permute-start(bf16[256,512]{1,0:T(8,128)(2,1)} %arrange_0.1.refs_4_), channel_id=1, source_target_pairs={{0,4},{1,5},{2,6},{3,7},{4,8},{5,9},{6,10},{7,11},{8,12},{9,13},{1... | collective-permute-start | bytes 786440 | tf_op jit(solution)/shard_map/ppermute | solution.py:437
  9.7 4.6 %all-to-all-start = ((bf16[16,8,128]{2,1,0:T(8,128)(2,1)}), bf16[16,8,128]{2,1,0:T(8,128)(2,1)S(1)}, u32[]{:S(2)}, u32[]{:S(2)}) async-start(bf16[16,8,128]{2,1,0:T(8,128)(2,1)} %own_rows.1), calls=%async_computation | async-start | bytes 65536 | tf_op jit(solution)/shard_map/all_to_all | solution.py:452
  14.3 1.8 %arrange_1.1.refs_5_ = bf16[256,512]{1,0:T(8,128)(2,1)} custom-call(bf16[128,1024]{1,0:T(8,128)(2,1)} %keys.5, bf16[128,1024]{1,0:T(8,128)(2,1)} %values.5, bf16[128,1024]{1,0:T(8,128)(2,1)S(1)} %collective-permute-done.k_other, bf16[128,1024]{1,0:T(8,128)(2,1)S(1)} %collective-permute-done.1.v_other), custom_call_target="tpu_custom_call" | custom-call | tf_op jit(solution)/shard_map/arrange_1/pallas_call | solution.py:319
  16.1 8.1 %all-to-all-done.refs_8_.refs_5_ = bf16[16,8,128]{2,1,0:T(8,128)(2,1)S(1)} async-done(((bf16[16,8,128]{2,1,0:T(8,128)(2,1)}), bf16[16,8,128]{2,1,0:T(8,128)(2,1)S(1)}, u32[]{:S(2)}, u32[]{:S(2)}) %all-to-all-start) | async-done | bytes 32800 | tf_op jit(solution)/shard_map/all_to_all | solution.py:452
  24.1 0.5 collective-permute-start.6
  24.7 0.7 %collective-permute-start.7 = (bf16[256,512]{1,0:T(8,128)(2,1)}, bf16[256,512]{1,0:T(8,128)(2,1)S(1)}, u32[]{:S(2)}, u32[]{:S(2)}) collective-permute-start(bf16[256,512]{1,0:T(8,128)(2,1)} %arrange_1.1.refs_5_), channel_id=1, source_target_pairs={{0,4},{1,5},{2,6},{3,7},{4,8},{5,9},{6,10},{7,11},{8,12},{9,13},{1... | collective-permute-start | bytes 786440 | tf_op jit(solution)/shard_map/ppermute | solution.py:437
  25.4 6.2 %attention_0.1 = (bf16[128,1024]{1,0:T(8,128)(2,1)S(1)}, bf16[128,1024]{1,0:T(8,128)(2,1)S(1)}, f32[8,256]{1,0:T(8,128)S(1)}, f32[256,512]{1,0:T(8,128)S(1)}, bf...) custom-call(bf16[128,4096]{1,0:T(8,128)(2,1)} %refs_0_.1, ...), custom_call_target="tpu_custom_call" | custom-call | flops 4110417920 | bytes 4194304 | tf_op jit(solution)/shard_map/attention_0/pallas_call | solution.py:288
  31.6 1.3 %collective-permute-start.10 = (bf16[256,512]{1,0:T(8,128)(2,1)S(1)}, bf16[256,512]{1,0:T(8,128)(2,1)S(1)}, u32[]{:S(2)}, u32[]{:S(2)}) collective-permute-start(bf16[256,512]{1,0:T(8,128)(2,1)S(1)} %get-tuple-element.55), channel_id=1, source_target_pairs={{2,0},{3,1},{4,2},{5,3},{6,4},{7,5},{8,6},{9,7},{10,8},{11,9},{12,... | collective-permute-start | bytes 786440 | tf_op jit(solution)/shard_map/ppermute | solution.py:437
  32.9 1.3 %collective-permute-start.11 = (bf16[256,512]{1,0:T(8,128)(2,1)S(1)}, bf16[256,512]{1,0:T(8,128)(2,1)S(1)}, u32[]{:S(2)}, u32[]{:S(2)}) collective-permute-start(bf16[256,512]{1,0:T(8,128)(2,1)S(1)} %get-tuple-element.56), channel_id=1, source_target_pairs={{4,0},{5,1},{6,2},{7,3},{8,4},{9,5},{10,6},{11,7},{12,8},{13,9},{1... | collective-permute-start | bytes 786440 | tf_op jit(solution)/shard_map/ppermute | solution.py:437
  34.2 2.0 %collective-permute-done.6.refs_3_ = bf16[256,512]{1,0:T(8,128)(2,1)S(1)} collective-permute-done((bf16[256,512]{1,0:T(8,128)(2,1)}, bf16[256,512]{1,0:T(8,128)(2,1)S(1)}, u32[]{:S(2)}, u32[]{:S(2)}) %collective-permute-start.6) | collective-permute-done | bytes 262176 | tf_op jit(solution)/shard_map/ppermute | solution.py:437
  36.2 5.5 %attention_1.1 = (bf16[128,1024]{1,0:T(8,128)(2,1)S(1)}, bf16[128,1024]{1,0:T(8,128)(2,1)}, f32[8,256]{1,0:T(8,128)S(1)}, f32[256,512]{1,0:T(8,128)S(1)}, bf16[2...) custom-call(bf16[2,128,1024]{2,1,0:T(8,128)(2,1)S(1)} %get-tuple-element.42.refs_0_, ...), custom_call_target="tpu_custom_call" | custom-call | flops 4110417920 | bytes 4194304 | tf_op jit(solution)/shard_map/attention_1/pallas_call | solution.py:288
  41.8 0.5 collective-permute-start.8
  42.3 4.8 %collective-permute-start.13 = (bf16[256,512]{1,0:T(8,128)(2,1)S(1)}, bf16[256,512]{1,0:T(8,128)(2,1)S(1)}, u32[]{:S(2)}, u32[]{:S(2)}) collective-permute-start(bf16[256,512]{1,0:T(8,128)(2,1)S(1)} %get-tuple-element.61), channel_id=1, source_target_pairs={{0,14},{1,15},{2,0},{3,1},{4,2},{5,3},{6,4},{7,5},{8,6},{9,7},{10,... | collective-permute-start | bytes 786440 | tf_op jit(solution)/shard_map/ppermute | solution.py:437
  47.5 6.1 %all-to-all-start.1 = ((f32[8,2,8,128]{3,2,1,0:T(8,128)}), f32[8,2,8,128]{3,2,1,0:T(8,128)S(1)}, u32[]{:S(2)}, u32[]{:S(2)}) async-start(f32[8,2,8,128]{3,2,1,0:T(8,128)} %bitcast.2), calls=%async_computation.1 | async-start | bytes 131072 | tf_op jit(solution)/shard_map/all_to_all | solution.py:441
  53.7 2.5 %maximum_select_fusion = bf16[128,4096]{1,0:T(8,128)(2,1)} fusion(bf16[128,1024]{1,0:T(8,128)(2,1)} %collective-permute-done.9, bf16[128,1024]{1,0:T(8,128)(2,1)} %collective-permute-done.8, bf16[128,1024]{1,0:T(8,128)(2,1)S(1)} %get-tuple-element.51, bf16[128,1024]{1,0:T(8,128)(2,1)S(1)} %get-tuple-element.50, pred[]{:T(512)S(6)} %eq.4), kind=kLoop, calls=%fused_computation | loop fusion | flops 8912896 | bytes 2097153 | tf_op jit(solution)/shard_map/jit(_where)/select_n | solution.py:444
  56.2 0.6 maximum_select_fusion.1
  56.8 5.0 %collective-permute-done.14.refs_5_ = bf16[256,512]{1,0:T(8,128)(2,1)S(1)} collective-permute-done((bf16[256,512]{1,0:T(8,128)(2,1)S(1)}, bf16[256,512]{1,0:T(8,128)(2,1)S(1)}, u32[]{:S(2)}, u32[]{:S(2)}) %collective-permute-start.14) | collective-permute-done | bytes 262176 | tf_op jit(solution)/shard_map/ppermute | solution.py:437
  61.7 0.7 %all-to-all-done.1.refs_6_ = f32[8,2,8,128]{3,2,1,0:T(8,128)S(1)} async-done(((f32[8,2,8,128]{3,2,1,0:T(8,128)}), f32[8,2,8,128]{3,2,1,0:T(8,128)S(1)}, u32[]{:S(2)}, u32[]{:S(2)}) %all-to-all-start.1) | async-done | bytes 65568 | tf_op jit(solution)/shard_map/all_to_all | solution.py:441
  62.8 1.5 %collective-permute-done.15.theirs = bf16[128,1024]{1,0:T(8,128)(2,1)S(1)} collective-permute-done((bf16[128,1024]{1,0:T(8,128)(2,1)S(1)}, bf16[128,1024]{1,0:T(8,128)(2,1)S(1)}, u32[]{:S(2)}, u32[]{:S(2)}) %collective-permute-start.15) | collective-permute-done | bytes 262176 | tf_op jit(solution)/shard_map/ppermute | solution.py:433
  64.3 0.9 %place.1 = (bf16[128,1024]{1,0:T(8,128)(2,1)}, bf16[128,1024]{1,0:T(8,128)(2,1)}) custom-call(bf16[128,1024]{1,0:T(8,128)(2,1)S(1)} %get-tuple-element.65.mine, bf16[128,1024]{1,0:T(8,128)(2,1)S(1)} %collective-permute-done.15.theirs), custom_call_target="tpu_custom_call" | custom-call | tf_op jit(solution)/shard_map/place/pallas_call | solution.py:414
  (26 shorter events, 1.7 us)
Async XLA Ops:
  0.6 4.1 %copy-start = (bf16[128,4096]{1,0:T(8,128)(2,1)S(1)}, bf16[128,4096]{1,0:T(8,128)(2,1)}, u32[]{:S(2)}) copy-start(bf16[128,4096]{1,0:T(8,128)(2,1)} %refs_0_.1) | copy-start | bytes 3145732
  0.6 2.0 %collective-permute-start = (bf16[128,1024]{1,0:T(8,128)(2,1)}, bf16[128,1024]{1,0:T(8,128)(2,1)S(1)}, u32[]{:S(2)}, u32[]{:S(2)}) collective-permute-start(bf16[128,1024]{1,0:T(8,128)(2,1)} %keys.5), channel_id=1, source_target_pairs={{0,1},{1,0},{2,3},{3,2},{4,5},{5,4},{6,7},{7,6},{8,9},{9,8},{10,11... | collective-permute-start | bytes 786440 | tf_op jit(solution)/shard_map/ppermute | solution.py:433
  1.2 1.7 %collective-permute-start.1 = (bf16[128,1024]{1,0:T(8,128)(2,1)}, bf16[128,1024]{1,0:T(8,128)(2,1)S(1)}, u32[]{:S(2)}, u32[]{:S(2)}) collective-permute-start(bf16[128,1024]{1,0:T(8,128)(2,1)} %values.5), channel_id=1, source_target_pairs={{0,1},{1,0},{2,3},{3,2},{4,5},{5,4},{6,7},{7,6},{8,9},{9,8},{10,11... | collective-permute-start | bytes 786440 | tf_op jit(solution)/shard_map/ppermute | solution.py:433
  4.7 20.6 %collective-permute-start.2 = (bf16[128,4096]{1,0:T(8,128)(2,1)S(1)}, bf16[128,4096]{1,0:T(8,128)(2,1)}, u32[]{:S(2)}, u32[]{:S(2)}) collective-permute-start(bf16[128,4096]{1,0:T(8,128)(2,1)S(1)} %copy-done), channel_id=1, source_target_pairs={{0,1},{1,0},{2,3},{3,2},{4,5},{5,4},{6,7},{7,6},{8,9},{9,8},{10,11... | collective-permute-start | bytes 3145736 | tf_op jit(solution)/shard_map/ppermute | solution.py:433
  5.1 20.3 %collective-permute-start.3 = (bf16[128,4096]{1,0:T(8,128)(2,1)}, bf16[128,4096]{1,0:T(8,128)(2,1)}, u32[]{:S(2)}, u32[]{:S(2)}) collective-permute-start(bf16[128,4096]{1,0:T(8,128)(2,1)} %refs_2_.1), channel_id=1, source_target_pairs={{0,1},{1,0},{2,3},{3,2},{4,5},{5,4},{6,7},{7,6},{8,9},{9,8},{10,11... | collective-permute-start | bytes 3145736 | tf_op jit(solution)/shard_map/ppermute | solution.py:433
  5.2 19.5 %collective-permute-start.4 = (bf16[256,512]{1,0:T(8,128)(2,1)}, bf16[256,512]{1,0:T(8,128)(2,1)S(1)}, u32[]{:S(2)}, u32[]{:S(2)}) collective-permute-start(bf16[256,512]{1,0:T(8,128)(2,1)} %arrange_0.1.refs_4_), channel_id=1, source_target_pairs={{0,2},{1,3},{2,4},{3,5},{4,6},{5,7},{6,8},{7,9},{8,10},{9,11},{10,... | collective-permute-start | bytes 786440 | tf_op jit(solution)/shard_map/ppermute | solution.py:437
  8.1 17.3 %collective-permute-start.5 = (bf16[256,512]{1,0:T(8,128)(2,1)}, bf16[256,512]{1,0:T(8,128)(2,1)S(1)}, u32[]{:S(2)}, u32[]{:S(2)}) collective-permute-start(bf16[256,512]{1,0:T(8,128)(2,1)} %arrange_0.1.refs_4_), channel_id=1, source_target_pairs={{0,4},{1,5},{2,6},{3,7},{4,8},{5,9},{6,10},{7,11},{8,12},{9,13},{1... | collective-permute-start | bytes 786440 | tf_op jit(solution)/shard_map/ppermute | solution.py:437
  9.7 14.5 %all-to-all-start = ((bf16[16,8,128]{2,1,0:T(8,128)(2,1)}), bf16[16,8,128]{2,1,0:T(8,128)(2,1)S(1)}, u32[]{:S(2)}, u32[]{:S(2)}) async-start(bf16[16,8,128]{2,1,0:T(8,128)(2,1)} %own_rows.1), calls=%async_computation | async-start | bytes 65536 | tf_op jit(solution)/shard_map/all_to_all | solution.py:452
  24.1 12.1 %collective-permute-start.6 = (bf16[256,512]{1,0:T(8,128)(2,1)}, bf16[256,512]{1,0:T(8,128)(2,1)S(1)}, u32[]{:S(2)}, u32[]{:S(2)}) collective-permute-start(bf16[256,512]{1,0:T(8,128)(2,1)} %arrange_1.1.refs_5_), channel_id=1, source_target_pairs={{0,2},{1,3},{2,4},{3,5},{4,6},{5,7},{6,8},{7,9},{8,10},{9,11},{10,... | collective-permute-start | bytes 786440 | tf_op jit(solution)/shard_map/ppermute | solution.py:437
  24.7 11.5 %collective-permute-start.7 = (bf16[256,512]{1,0:T(8,128)(2,1)}, bf16[256,512]{1,0:T(8,128)(2,1)S(1)}, u32[]{:S(2)}, u32[]{:S(2)}) collective-permute-start(bf16[256,512]{1,0:T(8,128)(2,1)} %arrange_1.1.refs_5_), channel_id=1, source_target_pairs={{0,4},{1,5},{2,6},{3,7},{4,8},{5,9},{6,10},{7,11},{8,12},{9,13},{1... | collective-permute-start | bytes 786440 | tf_op jit(solution)/shard_map/ppermute | solution.py:437
  31.6 15.5 %collective-permute-start.10 = (bf16[256,512]{1,0:T(8,128)(2,1)S(1)}, bf16[256,512]{1,0:T(8,128)(2,1)S(1)}, u32[]{:S(2)}, u32[]{:S(2)}) collective-permute-start(bf16[256,512]{1,0:T(8,128)(2,1)S(1)} %get-tuple-element.55), channel_id=1, source_target_pairs={{2,0},{3,1},{4,2},{5,3},{6,4},{7,5},{8,6},{9,7},{10,8},{11,9},{12,... | collective-permute-start | bytes 786440 | tf_op jit(solution)/shard_map/ppermute | solution.py:437
  32.9 14.7 %collective-permute-start.11 = (bf16[256,512]{1,0:T(8,128)(2,1)S(1)}, bf16[256,512]{1,0:T(8,128)(2,1)S(1)}, u32[]{:S(2)}, u32[]{:S(2)}) collective-permute-start(bf16[256,512]{1,0:T(8,128)(2,1)S(1)} %get-tuple-element.56), channel_id=1, source_target_pairs={{4,0},{5,1},{6,2},{7,3},{8,4},{9,5},{10,6},{11,7},{12,8},{13,9},{1... | collective-permute-start | bytes 786440 | tf_op jit(solution)/shard_map/ppermute | solution.py:437
  41.7 11.9 %collective-permute-start.9 = (bf16[128,1024]{1,0:T(8,128)(2,1)}, bf16[128,1024]{1,0:T(8,128)(2,1)}, u32[]{:S(2)}, u32[]{:S(2)}) collective-permute-start(bf16[128,1024]{1,0:T(8,128)(2,1)} %get-tuple-element.53), channel_id=1, source_target_pairs={{0,1},{1,0},{2,3},{3,2},{4,5},{5,4},{6,7},{7,6},{8,9},{9,8},{10,11... | collective-permute-start | bytes 786440 | tf_op jit(solution)/shard_map/ppermute | solution.py:433
  41.8 11.9 %collective-permute-start.8 = (bf16[128,1024]{1,0:T(8,128)(2,1)S(1)}, bf16[128,1024]{1,0:T(8,128)(2,1)}, u32[]{:S(2)}, u32[]{:S(2)}) collective-permute-start(bf16[128,1024]{1,0:T(8,128)(2,1)S(1)} %get-tuple-element.52), channel_id=1, source_target_pairs={{0,1},{1,0},{2,3},{3,2},{4,5},{5,4},{6,7},{7,6},{8,9},{9,8},{10,11... | collective-permute-start | bytes 786440 | tf_op jit(solution)/shard_map/ppermute | solution.py:433
  42.3 14.5 %collective-permute-start.13 = (bf16[256,512]{1,0:T(8,128)(2,1)S(1)}, bf16[256,512]{1,0:T(8,128)(2,1)S(1)}, u32[]{:S(2)}, u32[]{:S(2)}) collective-permute-start(bf16[256,512]{1,0:T(8,128)(2,1)S(1)} %get-tuple-element.61), channel_id=1, source_target_pairs={{0,14},{1,15},{2,0},{3,1},{4,2},{5,3},{6,4},{7,5},{8,6},{9,7},{10,... | collective-permute-start | bytes 786440 | tf_op jit(solution)/shard_map/ppermute | solution.py:437
  47.1 14.7 %collective-permute-start.14 = (bf16[256,512]{1,0:T(8,128)(2,1)S(1)}, bf16[256,512]{1,0:T(8,128)(2,1)S(1)}, u32[]{:S(2)}, u32[]{:S(2)}) collective-permute-start(bf16[256,512]{1,0:T(8,128)(2,1)S(1)} %get-tuple-element.62), channel_id=1, source_target_pairs={{0,12},{1,13},{2,14},{3,15},{4,0},{5,1},{6,2},{7,3},{8,4},{9,5},{1... | collective-permute-start | bytes 786440 | tf_op jit(solution)/shard_map/ppermute | solution.py:437
  47.5 14.9 %all-to-all-start.1 = ((f32[8,2,8,128]{3,2,1,0:T(8,128)}), f32[8,2,8,128]{3,2,1,0:T(8,128)S(1)}, u32[]{:S(2)}, u32[]{:S(2)}) async-start(f32[8,2,8,128]{3,2,1,0:T(8,128)} %bitcast.2), calls=%async_computation.1 | async-start | bytes 131072 | tf_op jit(solution)/shard_map/all_to_all | solution.py:441
  53.7 2.5 %collective-permute-start.12 = (f32[16,128]{1,0:T(8,128)S(1)}, f32[16,128]{1,0:T(8,128)S(1)}, u32[]{:S(2)}, u32[]{:S(2)}) collective-permute-start(f32[16,128]{1,0:T(8,128)S(1)} %get-tuple-element.57), channel_id=1, source_target_pairs={{0,1},{1,0},{2,3},{3,2},{4,5},{5,4},{6,7},{7,6},{8,9},{9,8},{10,11... | collective-permute-start | bytes 24584 | tf_op jit(solution)/shard_map/ppermute | solution.py:433
  62.7 1.6 %collective-permute-start.15 = (bf16[128,1024]{1,0:T(8,128)(2,1)S(1)}, bf16[128,1024]{1,0:T(8,128)(2,1)S(1)}, u32[]{:S(2)}, u32[]{:S(2)}) collective-permute-start(bf16[128,1024]{1,0:T(8,128)(2,1)S(1)} %get-tuple-element.66), channel_id=1, source_target_pairs={{0,1},{1,0},{2,3},{3,2},{4,5},{5,4},{6,7},{7,6},{8,9},{9,8},{10,11... | collective-permute-start | bytes 786440 | tf_op jit(solution)/shard_map/ppermute | solution.py:433

commit v8 on v7

--- a/solution.py
+++ b/solution.py
@@ -292,7 +292,7 @@
         out_specs=[whole] * len(outs),
         out_shape=outs,
         scratch_shapes=scratch,
-        compiler_params=pltpu.CompilerParams(vmem_limit_bytes=20 * 1024 * 1024),
+        compiler_params=pltpu.CompilerParams(vmem_limit_bytes=12 * 1024 * 1024),
         cost_estimate=pl.CostEstimate(
             flops=count * heads * rows * keys_seen * HEAD_SIZE * 20,
             transcendentals=count * heads * rows * keys_seen,

time: 65.6 us -> 65.6 us (level)
  no operation moved by 1% of the time
where the time goes in v8:
time: 65.6 us; the launch traced here: 65.2 us
  starting transfers between devices  25.6 us (39%)
  Pallas kernels  17.9 us (27%)
  waiting for transfers between devices  17.9 us (27%)
  other arithmetic  3.07 us (5%)
  between operations  0.74 us (1%)
    ppermute x8, starting transfers between devices, shifted(): lax.ppermute(x, 'ctx', [(i, j) for i, j in pairs_sent if wrap or j == i +...  13.2 us
    pallas_call x2, Pallas kernels, attention(): pl.pallas_call(first_kernel if chunk == 0 else functools.partial(later_ke...  11.7 us
    all_to_all x1, waiting for transfers between devices, local(): far = lax.all_to_all(sent, 'ctx', 0, 0, tiled=True)  8.05 us
    ppermute x8, waiting for transfers between devices, shifted(): lax.ppermute(x, 'ctx', [(i, j) for i, j in pairs_sent if wrap or j == i +...  7.34 us
    all_to_all x1, starting transfers between devices, exchanged(): return lax.all_to_all(x, 'ctx', 0, 0, axis_index_groups=groups)  6.13 us
    all_to_all x1, starting transfers between devices, local(): far = lax.all_to_all(sent, 'ctx', 0, 0, tiled=True)  4.61 us
    pallas_call x2, Pallas kernels, arrange(): pl.pallas_call(functools.partial(arrange_kernel, chunk), name=f'arrange_{...  3.6 us
    select_n x2, other arithmetic, joined(): jnp.where(core == 0, jnp.concatenate([mine, theirs], axis=1), jnp.concate...  3.07 us
  transfers between devices with their start and end apart: 18, of which 7 were waited for; matrix products, arithmetic and copies ran while one was open for 5% of the time, Pallas kernels for 23%

profile of v8, /device:TPU:0, one launch (start us, length us, event | category | flops | bytes accessed | tf_op | source)
XLA Modules:
  0.0 65.2 jit_solution(17563360771582312917)
XLA Ops:
  0.6 0.5 collective-permute-start
  1.2 1.4 %own_rows.1 = bf16[16,8,128]{2,1,0:T(8,128)(2,1)} custom-call(bf16[128,1024]{1,0:T(8,128)(2,1)} %keys.5, bf16[128,1024]{1,0:T(8,128)(2,1)} %values.5), custom_call_target="tpu_custom_call" | custom-call | tf_op jit(solution)/shard_map/own_rows/pallas_call | solution.py:345
  2.9 1.8 %arrange_0.1.refs_4_ = bf16[256,512]{1,0:T(8,128)(2,1)} custom-call(bf16[128,1024]{1,0:T(8,128)(2,1)} %keys.5, bf16[128,1024]{1,0:T(8,128)(2,1)} %values.5, bf16[128,1024]{1,0:T(8,128)(2,1)S(1)} %collective-permute-done.k_other, bf16[128,1024]{1,0:T(8,128)(2,1)S(1)} %collective-permute-done.1.v_other), custom_call_target="tpu_custom_call" | custom-call | tf_op jit(solution)/shard_map/arrange_0/pallas_call | solution.py:319
  5.2 2.9 %collective-permute-start.4 = (bf16[256,512]{1,0:T(8,128)(2,1)}, bf16[256,512]{1,0:T(8,128)(2,1)S(1)}, u32[]{:S(2)}, u32[]{:S(2)}) collective-permute-start(bf16[256,512]{1,0:T(8,128)(2,1)} %arrange_0.1.refs_4_), channel_id=1, source_target_pairs={{0,2},{1,3},{2,4},{3,5},{4,6},{5,7},{6,8},{7,9},{8,10},{9,11},{10,... | collective-permute-start | bytes 786440 | tf_op jit(solution)/shard_map/ppermute | solution.py:437
  8.1 1.6 %collective-permute-start.5 = (bf16[256,512]{1,0:T(8,128)(2,1)}, bf16[256,512]{1,0:T(8,128)(2,1)S(1)}, u32[]{:S(2)}, u32[]{:S(2)}) collective-permute-start(bf16[256,512]{1,0:T(8,128)(2,1)} %arrange_0.1.refs_4_), channel_id=1, source_target_pairs={{0,4},{1,5},{2,6},{3,7},{4,8},{5,9},{6,10},{7,11},{8,12},{9,13},{1... | collective-permute-start | bytes 786440 | tf_op jit(solution)/shard_map/ppermute | solution.py:437
  9.7 4.6 %all-to-all-start = ((bf16[16,8,128]{2,1,0:T(8,128)(2,1)}), bf16[16,8,128]{2,1,0:T(8,128)(2,1)S(1)}, u32[]{:S(2)}, u32[]{:S(2)}) async-start(bf16[16,8,128]{2,1,0:T(8,128)(2,1)} %own_rows.1), calls=%async_computation | async-start | bytes 65536 | tf_op jit(solution)/shard_map/all_to_all | solution.py:452
  14.3 1.8 %arrange_1.1.refs_5_ = bf16[256,512]{1,0:T(8,128)(2,1)} custom-call(bf16[128,1024]{1,0:T(8,128)(2,1)} %keys.5, bf16[128,1024]{1,0:T(8,128)(2,1)} %values.5, bf16[128,1024]{1,0:T(8,128)(2,1)S(1)} %collective-permute-done.k_other, bf16[128,1024]{1,0:T(8,128)(2,1)S(1)} %collective-permute-done.1.v_other), custom_call_target="tpu_custom_call" | custom-call | tf_op jit(solution)/shard_map/arrange_1/pallas_call | solution.py:319
  16.1 8.1 %all-to-all-done.refs_8_.refs_5_ = bf16[16,8,128]{2,1,0:T(8,128)(2,1)S(1)} async-done(((bf16[16,8,128]{2,1,0:T(8,128)(2,1)}), bf16[16,8,128]{2,1,0:T(8,128)(2,1)S(1)}, u32[]{:S(2)}, u32[]{:S(2)}) %all-to-all-start) | async-done | bytes 32800 | tf_op jit(solution)/shard_map/all_to_all | solution.py:452
  24.1 0.5 collective-permute-start.6
  24.7 0.7 %collective-permute-start.7 = (bf16[256,512]{1,0:T(8,128)(2,1)}, bf16[256,512]{1,0:T(8,128)(2,1)S(1)}, u32[]{:S(2)}, u32[]{:S(2)}) collective-permute-start(bf16[256,512]{1,0:T(8,128)(2,1)} %arrange_1.1.refs_5_), channel_id=1, source_target_pairs={{0,4},{1,5},{2,6},{3,7},{4,8},{5,9},{6,10},{7,11},{8,12},{9,13},{1... | collective-permute-start | bytes 786440 | tf_op jit(solution)/shard_map/ppermute | solution.py:437
  25.4 6.2 %attention_0.1 = (bf16[128,1024]{1,0:T(8,128)(2,1)S(1)}, bf16[128,1024]{1,0:T(8,128)(2,1)S(1)}, f32[8,256]{1,0:T(8,128)S(1)}, f32[256,512]{1,0:T(8,128)S(1)}, bf...) custom-call(bf16[128,4096]{1,0:T(8,128)(2,1)} %refs_0_.1, ...), custom_call_target="tpu_custom_call" | custom-call | flops 4110417920 | bytes 4194304 | tf_op jit(solution)/shard_map/attention_0/pallas_call | solution.py:288
  31.6 1.3 %collective-permute-start.10 = (bf16[256,512]{1,0:T(8,128)(2,1)S(1)}, bf16[256,512]{1,0:T(8,128)(2,1)S(1)}, u32[]{:S(2)}, u32[]{:S(2)}) collective-permute-start(bf16[256,512]{1,0:T(8,128)(2,1)S(1)} %get-tuple-element.55), channel_id=1, source_target_pairs={{2,0},{3,1},{4,2},{5,3},{6,4},{7,5},{8,6},{9,7},{10,8},{11,9},{12,... | collective-permute-start | bytes 786440 | tf_op jit(solution)/shard_map/ppermute | solution.py:437
  32.9 1.3 %collective-permute-start.11 = (bf16[256,512]{1,0:T(8,128)(2,1)S(1)}, bf16[256,512]{1,0:T(8,128)(2,1)S(1)}, u32[]{:S(2)}, u32[]{:S(2)}) collective-permute-start(bf16[256,512]{1,0:T(8,128)(2,1)S(1)} %get-tuple-element.56), channel_id=1, source_target_pairs={{4,0},{5,1},{6,2},{7,3},{8,4},{9,5},{10,6},{11,7},{12,8},{13,9},{1... | collective-permute-start | bytes 786440 | tf_op jit(solution)/shard_map/ppermute | solution.py:437
  34.2 2.0 %collective-permute-done.6.refs_3_ = bf16[256,512]{1,0:T(8,128)(2,1)S(1)} collective-permute-done((bf16[256,512]{1,0:T(8,128)(2,1)}, bf16[256,512]{1,0:T(8,128)(2,1)S(1)}, u32[]{:S(2)}, u32[]{:S(2)}) %collective-permute-start.6) | collective-permute-done | bytes 262176 | tf_op jit(solution)/shard_map/ppermute | solution.py:437
  36.2 5.5 %attention_1.1 = (bf16[128,1024]{1,0:T(8,128)(2,1)S(1)}, bf16[128,1024]{1,0:T(8,128)(2,1)}, f32[8,256]{1,0:T(8,128)S(1)}, f32[256,512]{1,0:T(8,128)S(1)}, bf16[2...) custom-call(bf16[2,128,1024]{2,1,0:T(8,128)(2,1)S(1)} %get-tuple-element.42.refs_0_, ...), custom_call_target="tpu_custom_call" | custom-call | flops 4110417920 | bytes 4194304 | tf_op jit(solution)/shard_map/attention_1/pallas_call | solution.py:288
  41.8 0.5 collective-permute-start.8
  42.3 4.8 %collective-permute-start.13 = (bf16[256,512]{1,0:T(8,128)(2,1)S(1)}, bf16[256,512]{1,0:T(8,128)(2,1)S(1)}, u32[]{:S(2)}, u32[]{:S(2)}) collective-permute-start(bf16[256,512]{1,0:T(8,128)(2,1)S(1)} %get-tuple-element.61), channel_id=1, source_target_pairs={{0,14},{1,15},{2,0},{3,1},{4,2},{5,3},{6,4},{7,5},{8,6},{9,7},{10,... | collective-permute-start | bytes 786440 | tf_op jit(solution)/shard_map/ppermute | solution.py:437
  47.5 6.1 %all-to-all-start.1 = ((f32[8,2,8,128]{3,2,1,0:T(8,128)}), f32[8,2,8,128]{3,2,1,0:T(8,128)S(1)}, u32[]{:S(2)}, u32[]{:S(2)}) async-start(f32[8,2,8,128]{3,2,1,0:T(8,128)} %bitcast.2), calls=%async_computation.1 | async-start | bytes 131072 | tf_op jit(solution)/shard_map/all_to_all | solution.py:441
  53.7 2.5 %maximum_select_fusion = bf16[128,4096]{1,0:T(8,128)(2,1)} fusion(bf16[128,1024]{1,0:T(8,128)(2,1)} %collective-permute-done.9, bf16[128,1024]{1,0:T(8,128)(2,1)} %collective-permute-done.8, bf16[128,1024]{1,0:T(8,128)(2,1)S(1)} %get-tuple-element.51, bf16[128,1024]{1,0:T(8,128)(2,1)S(1)} %get-tuple-element.50, pred[]{:T(512)S(6)} %eq.4), kind=kLoop, calls=%fused_computation | loop fusion | flops 8912896 | bytes 2097153 | tf_op jit(solution)/shard_map/jit(_where)/select_n | solution.py:444
  56.2 0.6 maximum_select_fusion.1
  56.8 5.0 %collective-permute-done.14.refs_5_ = bf16[256,512]{1,0:T(8,128)(2,1)S(1)} collective-permute-done((bf16[256,512]{1,0:T(8,128)(2,1)S(1)}, bf16[256,512]{1,0:T(8,128)(2,1)S(1)}, u32[]{:S(2)}, u32[]{:S(2)}) %collective-permute-start.14) | collective-permute-done | bytes 262176 | tf_op jit(solution)/shard_map/ppermute | solution.py:437
  61.7 0.7 %all-to-all-done.1.refs_6_ = f32[8,2,8,128]{3,2,1,0:T(8,128)S(1)} async-done(((f32[8,2,8,128]{3,2,1,0:T(8,128)}), f32[8,2,8,128]{3,2,1,0:T(8,128)S(1)}, u32[]{:S(2)}, u32[]{:S(2)}) %all-to-all-start.1) | async-done | bytes 65568 | tf_op jit(solution)/shard_map/all_to_all | solution.py:441
  62.8 1.5 %collective-permute-done.15.theirs = bf16[128,1024]{1,0:T(8,128)(2,1)S(1)} collective-permute-done((bf16[128,1024]{1,0:T(8,128)(2,1)S(1)}, bf16[128,1024]{1,0:T(8,128)(2,1)S(1)}, u32[]{:S(2)}, u32[]{:S(2)}) %collective-permute-start.15) | collective-permute-done | bytes 262176 | tf_op jit(solution)/shard_map/ppermute | solution.py:433
  64.3 0.9 %place.1 = (bf16[128,1024]{1,0:T(8,128)(2,1)}, bf16[128,1024]{1,0:T(8,128)(2,1)}) custom-call(bf16[128,1024]{1,0:T(8,128)(2,1)S(1)} %get-tuple-element.65.mine, bf16[128,1024]{1,0:T(8,128)(2,1)S(1)} %collective-permute-done.15.theirs), custom_call_target="tpu_custom_call" | custom-call | tf_op jit(solution)/shard_map/place/pallas_call | solution.py:414
  (26 shorter events, 1.7 us)
Async XLA Ops:
  0.6 4.1 %copy-start = (bf16[128,4096]{1,0:T(8,128)(2,1)S(1)}, bf16[128,4096]{1,0:T(8,128)(2,1)}, u32[]{:S(2)}) copy-start(bf16[128,4096]{1,0:T(8,128)(2,1)} %refs_0_.1) | copy-start | bytes 3145732
  0.6 2.0 %collective-permute-start = (bf16[128,1024]{1,0:T(8,128)(2,1)}, bf16[128,1024]{1,0:T(8,128)(2,1)S(1)}, u32[]{:S(2)}, u32[]{:S(2)}) collective-permute-start(bf16[128,1024]{1,0:T(8,128)(2,1)} %keys.5), channel_id=1, source_target_pairs={{0,1},{1,0},{2,3},{3,2},{4,5},{5,4},{6,7},{7,6},{8,9},{9,8},{10,11... | collective-permute-start | bytes 786440 | tf_op jit(solution)/shard_map/ppermute | solution.py:433
  1.2 1.7 %collective-permute-start.1 = (bf16[128,1024]{1,0:T(8,128)(2,1)}, bf16[128,1024]{1,0:T(8,128)(2,1)S(1)}, u32[]{:S(2)}, u32[]{:S(2)}) collective-permute-start(bf16[128,1024]{1,0:T(8,128)(2,1)} %values.5), channel_id=1, source_target_pairs={{0,1},{1,0},{2,3},{3,2},{4,5},{5,4},{6,7},{7,6},{8,9},{9,8},{10,11... | collective-permute-start | bytes 786440 | tf_op jit(solution)/shard_map/ppermute | solution.py:433
  4.7 20.6 %collective-permute-start.2 = (bf16[128,4096]{1,0:T(8,128)(2,1)S(1)}, bf16[128,4096]{1,0:T(8,128)(2,1)}, u32[]{:S(2)}, u32[]{:S(2)}) collective-permute-start(bf16[128,4096]{1,0:T(8,128)(2,1)S(1)} %copy-done), channel_id=1, source_target_pairs={{0,1},{1,0},{2,3},{3,2},{4,5},{5,4},{6,7},{7,6},{8,9},{9,8},{10,11... | collective-permute-start | bytes 3145736 | tf_op jit(solution)/shard_map/ppermute | solution.py:433
  5.1 20.3 %collective-permute-start.3 = (bf16[128,4096]{1,0:T(8,128)(2,1)}, bf16[128,4096]{1,0:T(8,128)(2,1)}, u32[]{:S(2)}, u32[]{:S(2)}) collective-permute-start(bf16[128,4096]{1,0:T(8,128)(2,1)} %refs_2_.1), channel_id=1, source_target_pairs={{0,1},{1,0},{2,3},{3,2},{4,5},{5,4},{6,7},{7,6},{8,9},{9,8},{10,11... | collective-permute-start | bytes 3145736 | tf_op jit(solution)/shard_map/ppermute | solution.py:433
  5.2 19.5 %collective-permute-start.4 = (bf16[256,512]{1,0:T(8,128)(2,1)}, bf16[256,512]{1,0:T(8,128)(2,1)S(1)}, u32[]{:S(2)}, u32[]{:S(2)}) collective-permute-start(bf16[256,512]{1,0:T(8,128)(2,1)} %arrange_0.1.refs_4_), channel_id=1, source_target_pairs={{0,2},{1,3},{2,4},{3,5},{4,6},{5,7},{6,8},{7,9},{8,10},{9,11},{10,... | collective-permute-start | bytes 786440 | tf_op jit(solution)/shard_map/ppermute | solution.py:437
  8.1 17.3 %collective-permute-start.5 = (bf16[256,512]{1,0:T(8,128)(2,1)}, bf16[256,512]{1,0:T(8,128)(2,1)S(1)}, u32[]{:S(2)}, u32[]{:S(2)}) collective-permute-start(bf16[256,512]{1,0:T(8,128)(2,1)} %arrange_0.1.refs_4_), channel_id=1, source_target_pairs={{0,4},{1,5},{2,6},{3,7},{4,8},{5,9},{6,10},{7,11},{8,12},{9,13},{1... | collective-permute-start | bytes 786440 | tf_op jit(solution)/shard_map/ppermute | solution.py:437
  9.7 14.5 %all-to-all-start = ((bf16[16,8,128]{2,1,0:T(8,128)(2,1)}), bf16[16,8,128]{2,1,0:T(8,128)(2,1)S(1)}, u32[]{:S(2)}, u32[]{:S(2)}) async-start(bf16[16,8,128]{2,1,0:T(8,128)(2,1)} %own_rows.1), calls=%async_computation | async-start | bytes 65536 | tf_op jit(solution)/shard_map/all_to_all | solution.py:452
  24.1 12.1 %collective-permute-start.6 = (bf16[256,512]{1,0:T(8,128)(2,1)}, bf16[256,512]{1,0:T(8,128)(2,1)S(1)}, u32[]{:S(2)}, u32[]{:S(2)}) collective-permute-start(bf16[256,512]{1,0:T(8,128)(2,1)} %arrange_1.1.refs_5_), channel_id=1, source_target_pairs={{0,2},{1,3},{2,4},{3,5},{4,6},{5,7},{6,8},{7,9},{8,10},{9,11},{10,... | collective-permute-start | bytes 786440 | tf_op jit(solution)/shard_map/ppermute | solution.py:437
  24.7 11.5 %collective-permute-start.7 = (bf16[256,512]{1,0:T(8,128)(2,1)}, bf16[256,512]{1,0:T(8,128)(2,1)S(1)}, u32[]{:S(2)}, u32[]{:S(2)}) collective-permute-start(bf16[256,512]{1,0:T(8,128)(2,1)} %arrange_1.1.refs_5_), channel_id=1, source_target_pairs={{0,4},{1,5},{2,6},{3,7},{4,8},{5,9},{6,10},{7,11},{8,12},{9,13},{1... | collective-permute-start | bytes 786440 | tf_op jit(solution)/shard_map/ppermute | solution.py:437
  31.6 15.5 %collective-permute-start.10 = (bf16[256,512]{1,0:T(8,128)(2,1)S(1)}, bf16[256,512]{1,0:T(8,128)(2,1)S(1)}, u32[]{:S(2)}, u32[]{:S(2)}) collective-permute-start(bf16[256,512]{1,0:T(8,128)(2,1)S(1)} %get-tuple-element.55), channel_id=1, source_target_pairs={{2,0},{3,1},{4,2},{5,3},{6,4},{7,5},{8,6},{9,7},{10,8},{11,9},{12,... | collective-permute-start | bytes 786440 | tf_op jit(solution)/shard_map/ppermute | solution.py:437
  32.9 14.7 %collective-permute-start.11 = (bf16[256,512]{1,0:T(8,128)(2,1)S(1)}, bf16[256,512]{1,0:T(8,128)(2,1)S(1)}, u32[]{:S(2)}, u32[]{:S(2)}) collective-permute-start(bf16[256,512]{1,0:T(8,128)(2,1)S(1)} %get-tuple-element.56), channel_id=1, source_target_pairs={{4,0},{5,1},{6,2},{7,3},{8,4},{9,5},{10,6},{11,7},{12,8},{13,9},{1... | collective-permute-start | bytes 786440 | tf_op jit(solution)/shard_map/ppermute | solution.py:437
  41.7 11.9 %collective-permute-start.9 = (bf16[128,1024]{1,0:T(8,128)(2,1)}, bf16[128,1024]{1,0:T(8,128)(2,1)}, u32[]{:S(2)}, u32[]{:S(2)}) collective-permute-start(bf16[128,1024]{1,0:T(8,128)(2,1)} %get-tuple-element.53), channel_id=1, source_target_pairs={{0,1},{1,0},{2,3},{3,2},{4,5},{5,4},{6,7},{7,6},{8,9},{9,8},{10,11... | collective-permute-start | bytes 786440 | tf_op jit(solution)/shard_map/ppermute | solution.py:433
  41.8 11.9 %collective-permute-start.8 = (bf16[128,1024]{1,0:T(8,128)(2,1)S(1)}, bf16[128,1024]{1,0:T(8,128)(2,1)}, u32[]{:S(2)}, u32[]{:S(2)}) collective-permute-start(bf16[128,1024]{1,0:T(8,128)(2,1)S(1)} %get-tuple-element.52), channel_id=1, source_target_pairs={{0,1},{1,0},{2,3},{3,2},{4,5},{5,4},{6,7},{7,6},{8,9},{9,8},{10,11... | collective-permute-start | bytes 786440 | tf_op jit(solution)/shard_map/ppermute | solution.py:433
  42.3 14.5 %collective-permute-start.13 = (bf16[256,512]{1,0:T(8,128)(2,1)S(1)}, bf16[256,512]{1,0:T(8,128)(2,1)S(1)}, u32[]{:S(2)}, u32[]{:S(2)}) collective-permute-start(bf16[256,512]{1,0:T(8,128)(2,1)S(1)} %get-tuple-element.61), channel_id=1, source_target_pairs={{0,14},{1,15},{2,0},{3,1},{4,2},{5,3},{6,4},{7,5},{8,6},{9,7},{10,... | collective-permute-start | bytes 786440 | tf_op jit(solution)/shard_map/ppermute | solution.py:437
  47.1 14.7 %collective-permute-start.14 = (bf16[256,512]{1,0:T(8,128)(2,1)S(1)}, bf16[256,512]{1,0:T(8,128)(2,1)S(1)}, u32[]{:S(2)}, u32[]{:S(2)}) collective-permute-start(bf16[256,512]{1,0:T(8,128)(2,1)S(1)} %get-tuple-element.62), channel_id=1, source_target_pairs={{0,12},{1,13},{2,14},{3,15},{4,0},{5,1},{6,2},{7,3},{8,4},{9,5},{1... | collective-permute-start | bytes 786440 | tf_op jit(solution)/shard_map/ppermute | solution.py:437
  47.5 14.9 %all-to-all-start.1 = ((f32[8,2,8,128]{3,2,1,0:T(8,128)}), f32[8,2,8,128]{3,2,1,0:T(8,128)S(1)}, u32[]{:S(2)}, u32[]{:S(2)}) async-start(f32[8,2,8,128]{3,2,1,0:T(8,128)} %bitcast.2), calls=%async_computation.1 | async-start | bytes 131072 | tf_op jit(solution)/shard_map/all_to_all | solution.py:441
  53.7 2.5 %collective-permute-start.12 = (f32[16,128]{1,0:T(8,128)S(1)}, f32[16,128]{1,0:T(8,128)S(1)}, u32[]{:S(2)}, u32[]{:S(2)}) collective-permute-start(f32[16,128]{1,0:T(8,128)S(1)} %get-tuple-element.57), channel_id=1, source_target_pairs={{0,1},{1,0},{2,3},{3,2},{4,5},{5,4},{6,7},{7,6},{8,9},{9,8},{10,11... | collective-permute-start | bytes 24584 | tf_op jit(solution)/shard_map/ppermute | solution.py:433
  62.7 1.6 %collective-permute-start.15 = (bf16[128,1024]{1,0:T(8,128)(2,1)S(1)}, bf16[128,1024]{1,0:T(8,128)(2,1)S(1)}, u32[]{:S(2)}, u32[]{:S(2)}) collective-permute-start(bf16[128,1024]{1,0:T(8,128)(2,1)S(1)} %get-tuple-element.66), channel_id=1, source_target_pairs={{0,1},{1,0},{2,3},{3,2},{4,5},{5,4},{6,7},{7,6},{8,9},{9,8},{10,11... | collective-permute-start | bytes 786440 | tf_op jit(solution)/shard_map/ppermute | solution.py:433
